TPU v7x, 128 devices: a whole 4x4x4 slice. The times are simulated.
128 devices in a mesh: rad: 8 (over z, x_hi), azi: 16 (over x_lo, y, core).
Axes of the slice: x: 4 (x_hi: 2, x_lo: 2; x = x_hi * 2 + x_lo), y: 4, z: 4, core: 2. Of those that a mesh axis runs over, the one named last changes fastest.
Arguments:
- fields: float32 [8, 2, 512, 8192], P(None, None, 'rad', 'azi'), may hold values from -6 to 6
- offsets: int32 [2, 512], P(None, 'rad'), may hold values from 0 to 8191
- fractions: float32 [2, 512], P(None, 'rad'), may hold values from 0 to 1
- coefs: float32 [512], P('rad'), may hold values from 0.02 to 0.3
Outputs:
- advanced: float32 [8, 2, 512, 8192], P(None, None, 'rad', 'azi')
All inputs are finite; a program needn't handle non-finite values.
Results may differ from a plain program's by a relative error of at most 0.00002.
Values sent between devices are 32-bit elements; how exact they have to be, the bound alone decides.
No kernel may reach another device: no remote copies, remote signals or barrier semaphores. Data moves between devices by JAX's collectives and lax.ppermute only.
A program may use at most 128 MiB of HBM per device.

v0:
```python
import jax
import jax.numpy as jnp
from jax import lax
from jax.sharding import PartitionSpec as P

STEPS = 2


def with_halo(shard, sides, width):
    for axis, dim in sides:
        peers, length = (lax.axis_size(axis), shard.shape[dim])
        up = [(i, (i + 1) % peers) for i in range(peers - 1)]
        down = [(j, i) for i, j in up]
        last = lax.slice_in_dim(shard, length - width, length, axis=dim)
        leading = lax.slice_in_dim(shard, 0, width, axis=dim)
        before = lax.ppermute(last, axis, up)
        after = lax.ppermute(leading, axis, down)
        shard = jnp.concatenate([before, shard, after], axis=dim)
    return shard


def passed_along(block, axis, distance):
    devices = range(lax.axis_size(axis))
    route = [((i - distance) % len(devices), i) for i in devices]
    return lax.ppermute(block, axis, route)


def diffuse(state, coefs):
    padded = with_halo(state, (("rad", 2),), 2)
    second = (
        16.0 * (padded[:, :, 1:-3] + padded[:, :, 3:-1])
        - (padded[:, :, :-4] + padded[:, :, 4:])
        - 30.0 * state
    ) / 12.0
    return state + coefs[:, None] * second


def slide_rows(values, amounts, limit):
    length = values.shape[3]
    for bit_number in range(max(limit - 1, 1).bit_length()):
        step_size = 1 << bit_number
        moved = jnp.concatenate(
            [
                jnp.zeros(values.shape[:3] + (step_size,), values.dtype),
                values[:, :, :, : length - step_size],
            ],
            axis=3,
        )
        picked = amounts >> bit_number & 1 == 1
        values = jnp.where(picked[None, None, :, None], moved, values)
    return values


def shards(fields, offsets, fractions, coefs):
    state = fields
    width = state.shape[3]
    devices = lax.axis_size("azi")
    for section in range(STEPS):
        state = diffuse(state, coefs)
        shifts = offsets[section]
        weights = fractions[section]
        blocks = shifts // width
        remain = shifts % width
        for bit_number in range((devices - 1).bit_length()):
            moved = passed_along(state, "azi", 1 << bit_number)
            picked = blocks >> bit_number & 1 == 1
            state = jnp.where(picked[None, None, :, None], moved, state)
        before = passed_along(state, "azi", 1)
        joined = jnp.concatenate([before, state], axis=3)
        slid = slide_rows(joined, remain, width)
        first = slid[:, :, :, width:]
        edge = passed_along(first[:, :, :, width - 1 :], "azi", 1)
        behind = jnp.concatenate([edge, first[:, :, :, : width - 1]], axis=3)
        weight = weights[:, None]
        state = (1.0 - weight) * first + weight * behind
    return state


def solution(mesh):
    placed = (P(None, None, "rad", "azi"), P(None, "rad"), P(None, "rad"), P("rad"))
    return jax.shard_map(
        shards, mesh=mesh, in_specs=placed, out_specs=P(None, None, "rad", "azi"), check_vma=False
    )
```

profile of v0, /device:TPU:1, one launch (start us, length us, event | category | flops | bytes accessed | tf_op | source)
XLA Modules:
  0.0 463.5 jit_solution(3188122759695139580)
XLA Ops:
  0.0 1.2 fusion.23
  1.2 1.3 collective-permute-start.1
  2.5 6.1 %collective-permute-start = (f32[8,2,2,512]{3,2,1,0:T(2,128)S(1)}, f32[8,2,2,512]{3,2,1,0:T(2,128)S(1)}, u32[]{:S(2)}, u32[]{:S(2)}) collective-permute-start(f32[8,2,2,512]{3,2,1,0:T(2,128)S(1)} %get-tuple-element.18), channel_id=1, source_target_pairs={{0,16},{16,32},{32,48},{48,64},{64,80},{80,96},{96,112},{1,17},{17... | collective-permute-start | bytes 196616 | tf_op jit(solution)/shard_map/ppermute | solution.py:16
  8.7 0.7 broadcast_multiply_fusion
  9.3 1.8 constant_dynamic-update-slice_fusion.1
  11.2 1.1 fusion.18
  12.3 2.7 collective-permute-start.2
  15.1 22.9 %collective-permute-done.2 = f32[8,2,64,512]{3,2,1,0:T(8,128)S(1)} collective-permute-done((f32[8,2,64,512]{3,2,1,0:T(8,128)S(1)}, f32[8,2,64,512]{3,2,1,0:T(8,128)S(1)}, u32[]{:S(2)}, u32[]{:S(2)}) %collective-permute-start.2) | collective-permute-done | bytes 2097184 | tf_op jit(solution)/shard_map/ppermute | solution.py:25
  38.0 0.5 broadcast_select_fusion
  38.5 1.4 collective-permute-start.3
  39.9 44.6 %collective-permute-done.3 = f32[8,2,64,512]{3,2,1,0:T(8,128)S(1)} collective-permute-done((f32[8,2,64,512]{3,2,1,0:T(8,128)S(1)}, f32[8,2,64,512]{3,2,1,0:T(8,128)S(1)}, u32[]{:S(2)}, u32[]{:S(2)}) %collective-permute-start.3) | collective-permute-done | bytes 2097184 | tf_op jit(solution)/shard_map/ppermute | solution.py:25
  84.5 0.6 broadcast_select_fusion.1
  85.1 2.3 collective-permute-start.4
  87.4 43.0 %collective-permute-done.4 = f32[8,2,64,512]{3,2,1,0:T(8,128)S(1)} collective-permute-done((f32[8,2,64,512]{3,2,1,0:T(8,128)S(1)}, f32[8,2,64,512]{3,2,1,0:T(8,128)S(1)}, u32[]{:S(2)}, u32[]{:S(2)}) %collective-permute-start.4) | collective-permute-done | bytes 2097184 | tf_op jit(solution)/shard_map/ppermute | solution.py:25
  130.4 0.6 broadcast_select_fusion.2
  131.0 1.1 collective-permute-start.5
  132.1 40.9 %collective-permute-done.5 = f32[8,2,64,512]{3,2,1,0:T(8,128)S(1)} collective-permute-done((f32[8,2,64,512]{3,2,1,0:T(8,128)S(1)}, f32[8,2,64,512]{3,2,1,0:T(8,128)S(1)}, u32[]{:S(2)}, u32[]{:S(2)}) %collective-permute-start.5) | collective-permute-done | bytes 2097184 | tf_op jit(solution)/shard_map/ppermute | solution.py:25
  173.0 0.5 broadcast_select_fusion.3
  173.6 8.5 %collective-permute-start.6 = (f32[8,2,64,512]{3,2,1,0:T(8,128)S(1)}, f32[8,2,64,512]{3,2,1,0:T(8,128)S(1)}, u32[]{:S(2)}, u32[]{:S(2)}) collective-permute-start(f32[8,2,64,512]{3,2,1,0:T(8,128)S(1)} %broadcast_select_fusion.3), channel_id=1, source_target_pairs={{15,0},{0,1},{1,2},{2,3},{3,4},{4,5},{5,6},{6,7},{7,8},{8,9},{9,10... | collective-permute-start | bytes 6291464 | tf_op jit(solution)/shard_map/ppermute | solution.py:25
  182.1 23.0 %collective-permute-done.6 = f32[8,2,64,512]{3,2,1,0:T(8,128)S(1)} collective-permute-done((f32[8,2,64,512]{3,2,1,0:T(8,128)S(1)}, f32[8,2,64,512]{3,2,1,0:T(8,128)S(1)}, u32[]{:S(2)}, u32[]{:S(2)}) %collective-permute-start.6) | collective-permute-done | bytes 2097184 | tf_op jit(solution)/shard_map/ppermute | solution.py:25
  205.1 0.4 fusion.2
  205.5 1.3 fusion.3
  206.9 1.2 pad_select_fusion.15
  208.0 1.6 pad_select_fusion.14
  209.6 1.6 pad_select_fusion.13
  211.2 1.6 pad_select_fusion.12
  212.8 1.6 pad_select_fusion.11
  214.3 1.6 pad_select_fusion.10
  216.3 0.8 pad_select_fusion.9
  217.3 1.0 pad_select_fusion.8
  218.6 2.8 collective-permute-start.7
  221.6 5.9 %collective-permute-done.7 = f32[8,2,64,1]{3,2,1,0:T(8,128)S(1)} collective-permute-done((f32[8,2,64,1]{3,2,1,0:T(8,128)S(1)}, f32[8,2,64,1]{3,2,1,0:T(8,128)S(1)}, u32[]{:S(2)}, u32[]{:S(2)}) %collective-permute-start.7) | collective-permute-done | bytes 4128 | tf_op jit(solution)/shard_map/ppermute | solution.py:25
  227.5 0.7 fusion.21
  228.3 5.4 %collective-permute-start.8 = (f32[8,2,2,512]{3,2,1,0:T(2,128)S(1)}, f32[8,2,2,512]{3,2,1,0:T(2,128)S(1)}, u32[]{:S(2)}, u32[]{:S(2)}) collective-permute-start(f32[8,2,2,512]{3,2,1,0:T(2,128)S(1)} %get-tuple-element.15), channel_id=1, source_target_pairs={{0,16},{16,32},{32,48},{48,64},{64,80},{80,96},{96,112},{1,17},{17... | collective-permute-start | bytes 196616 | tf_op jit(solution)/shard_map/ppermute | solution.py:16
  233.7 1.3 collective-permute-start.9
  235.0 6.1 %collective-permute-done.9 = f32[8,2,2,512]{3,2,1,0:T(2,128)S(1)} collective-permute-done((f32[8,2,2,512]{3,2,1,0:T(2,128)S(1)}, f32[8,2,2,512]{3,2,1,0:T(2,128)S(1)}, u32[]{:S(2)}, u32[]{:S(2)}) %collective-permute-start.9) | collective-permute-done | bytes 65568 | tf_op jit(solution)/shard_map/ppermute | solution.py:17
  241.1 1.3 fusion.10
  242.5 3.7 collective-permute-start.10
  246.2 23.0 %collective-permute-done.10 = f32[8,2,64,512]{3,2,1,0:T(8,128)S(1)} collective-permute-done((f32[8,2,64,512]{3,2,1,0:T(8,128)S(1)}, f32[8,2,64,512]{3,2,1,0:T(8,128)S(1)}, u32[]{:S(2)}, u32[]{:S(2)}) %collective-permute-start.10) | collective-permute-done | bytes 2097184 | tf_op jit(solution)/shard_map/ppermute | solution.py:25
  269.1 0.5 broadcast_select_fusion.4
  269.7 0.7 collective-permute-start.11
  270.3 45.8 %collective-permute-done.11 = f32[8,2,64,512]{3,2,1,0:T(8,128)S(1)} collective-permute-done((f32[8,2,64,512]{3,2,1,0:T(8,128)S(1)}, f32[8,2,64,512]{3,2,1,0:T(8,128)S(1)}, u32[]{:S(2)}, u32[]{:S(2)}) %collective-permute-start.11) | collective-permute-done | bytes 2097184 | tf_op jit(solution)/shard_map/ppermute | solution.py:25
  316.2 0.6 broadcast_select_fusion.5
  316.7 3.5 collective-permute-start.12
  320.2 43.0 %collective-permute-done.12 = f32[8,2,64,512]{3,2,1,0:T(8,128)S(1)} collective-permute-done((f32[8,2,64,512]{3,2,1,0:T(8,128)S(1)}, f32[8,2,64,512]{3,2,1,0:T(8,128)S(1)}, u32[]{:S(2)}, u32[]{:S(2)}) %collective-permute-start.12) | collective-permute-done | bytes 2097184 | tf_op jit(solution)/shard_map/ppermute | solution.py:25
  363.2 0.6 broadcast_select_fusion.6
  363.8 1.7 collective-permute-start.13
  365.4 41.7 %collective-permute-done.13 = f32[8,2,64,512]{3,2,1,0:T(8,128)S(1)} collective-permute-done((f32[8,2,64,512]{3,2,1,0:T(8,128)S(1)}, f32[8,2,64,512]{3,2,1,0:T(8,128)S(1)}, u32[]{:S(2)}, u32[]{:S(2)}) %collective-permute-start.13) | collective-permute-done | bytes 2097184 | tf_op jit(solution)/shard_map/ppermute | solution.py:25
  407.1 0.5 broadcast_select_fusion.7
  407.6 8.7 %collective-permute-start.14 = (f32[8,2,64,512]{3,2,1,0:T(8,128)S(1)}, f32[8,2,64,512]{3,2,1,0:T(8,128)S(1)}, u32[]{:S(2)}, u32[]{:S(2)}) collective-permute-start(f32[8,2,64,512]{3,2,1,0:T(8,128)S(1)} %broadcast_select_fusion.7), channel_id=1, source_target_pairs={{15,0},{0,1},{1,2},{2,3},{3,4},{4,5},{5,6},{6,7},{7,8},{8,9},{9,10... | collective-permute-start | bytes 6291464 | tf_op jit(solution)/shard_map/ppermute | solution.py:25
  416.4 23.0 %collective-permute-done.14 = f32[8,2,64,512]{3,2,1,0:T(8,128)S(1)} collective-permute-done((f32[8,2,64,512]{3,2,1,0:T(8,128)S(1)}, f32[8,2,64,512]{3,2,1,0:T(8,128)S(1)}, u32[]{:S(2)}, u32[]{:S(2)}) %collective-permute-start.14) | collective-permute-done | bytes 2097184 | tf_op jit(solution)/shard_map/ppermute | solution.py:25
  439.3 0.4 fusion
  439.8 1.3 fusion.1
  441.1 1.2 pad_select_fusion.7
  442.3 1.6 pad_select_fusion.6
  443.8 1.6 pad_select_fusion.5
  445.4 1.6 pad_select_fusion.4
  447.0 1.6 pad_select_fusion.3
  448.6 1.6 pad_select_fusion.2
  450.5 0.8 pad_select_fusion.1
  451.6 1.0 pad_select_fusion
  452.8 2.5 collective-permute-start.15
  455.6 5.9 %collective-permute-done.15 = f32[8,2,64,1]{3,2,1,0:T(8,128)S(1)} collective-permute-done((f32[8,2,64,1]{3,2,1,0:T(8,128)S(1)}, f32[8,2,64,1]{3,2,1,0:T(8,128)S(1)}, u32[]{:S(2)}, u32[]{:S(2)}) %collective-permute-start.15) | collective-permute-done | bytes 4128 | tf_op jit(solution)/shard_map/ppermute | solution.py:25
  461.5 2.0 fusion.19
  (27 shorter events, 2.4 us)
Async XLA Ops:
  0.0 11.1 %copy-start = (f32[8,2,64,512]{3,2,1,0:T(8,128)S(1)}, f32[8,2,64,512]{3,2,1,0:T(8,128)}, u32[]{:S(2)}) copy-start(f32[8,2,64,512]{3,2,1,0:T(8,128)} %param.4) | copy-start | bytes 6291460
  1.2 9.8 %collective-permute-start.1 = (f32[8,2,2,512]{3,2,1,0:T(2,128)S(1)}, f32[8,2,2,512]{3,2,1,0:T(2,128)S(1)}, u32[]{:S(2)}, u32[]{:S(2)}) collective-permute-start(f32[8,2,2,512]{3,2,1,0:T(2,128)S(1)} %get-tuple-element.17), channel_id=1, source_target_pairs={{16,0},{32,16},{48,32},{64,48},{80,64},{96,80},{112,96},{17,1},{33... | collective-permute-start | bytes 196616 | tf_op jit(solution)/shard_map/ppermute | solution.py:17
  2.5 8.6 %collective-permute-start = (f32[8,2,2,512]{3,2,1,0:T(2,128)S(1)}, f32[8,2,2,512]{3,2,1,0:T(2,128)S(1)}, u32[]{:S(2)}, u32[]{:S(2)}) collective-permute-start(f32[8,2,2,512]{3,2,1,0:T(2,128)S(1)} %get-tuple-element.18), channel_id=1, source_target_pairs={{0,16},{16,32},{32,48},{48,64},{64,80},{80,96},{96,112},{1,17},{17... | collective-permute-start | bytes 196616 | tf_op jit(solution)/shard_map/ppermute | solution.py:16
  11.1 3.9 copy-start.2
  12.3 25.7 %collective-permute-start.2 = (f32[8,2,64,512]{3,2,1,0:T(8,128)S(1)}, f32[8,2,64,512]{3,2,1,0:T(8,128)S(1)}, u32[]{:S(2)}, u32[]{:S(2)}) collective-permute-start(f32[8,2,64,512]{3,2,1,0:T(8,128)S(1)} %fusion.18), channel_id=1, source_target_pairs={{15,0},{0,1},{1,2},{2,3},{3,4},{4,5},{5,6},{6,7},{7,8},{8,9},{9,10... | collective-permute-start | bytes 6291464 | tf_op jit(solution)/shard_map/ppermute | solution.py:25
  38.5 46.0 %collective-permute-start.3 = (f32[8,2,64,512]{3,2,1,0:T(8,128)S(1)}, f32[8,2,64,512]{3,2,1,0:T(8,128)S(1)}, u32[]{:S(2)}, u32[]{:S(2)}) collective-permute-start(f32[8,2,64,512]{3,2,1,0:T(8,128)S(1)} %broadcast_select_fusion), channel_id=1, source_target_pairs={{14,0},{15,1},{0,2},{1,3},{2,4},{3,5},{4,6},{5,7},{6,8},{7,9},{8,1... | collective-permute-start | bytes 6291464 | tf_op jit(solution)/shard_map/ppermute | solution.py:25
  85.1 45.4 %collective-permute-start.4 = (f32[8,2,64,512]{3,2,1,0:T(8,128)S(1)}, f32[8,2,64,512]{3,2,1,0:T(8,128)S(1)}, u32[]{:S(2)}, u32[]{:S(2)}) collective-permute-start(f32[8,2,64,512]{3,2,1,0:T(8,128)S(1)} %broadcast_select_fusion.1), channel_id=1, source_target_pairs={{12,0},{13,1},{14,2},{15,3},{0,4},{1,5},{2,6},{3,7},{4,8},{5,9},{6... | collective-permute-start | bytes 6291464 | tf_op jit(solution)/shard_map/ppermute | solution.py:25
  131.0 42.0 %collective-permute-start.5 = (f32[8,2,64,512]{3,2,1,0:T(8,128)S(1)}, f32[8,2,64,512]{3,2,1,0:T(8,128)S(1)}, u32[]{:S(2)}, u32[]{:S(2)}) collective-permute-start(f32[8,2,64,512]{3,2,1,0:T(8,128)S(1)} %broadcast_select_fusion.2), channel_id=1, source_target_pairs={{8,0},{9,1},{10,2},{11,3},{12,4},{13,5},{14,6},{15,7},{0,8},{1,9},... | collective-permute-start | bytes 6291464 | tf_op jit(solution)/shard_map/ppermute | solution.py:25
  173.0 9.1 %copy-start.1 = (f32[2,64]{1,0:T(2,128)S(1)}, f32[2,64]{1,0:T(2,128)}, u32[]{:S(2)}) copy-start(f32[2,64]{1,0:T(2,128)} %param.6) | copy-start | bytes 1540
  173.6 31.5 %collective-permute-start.6 = (f32[8,2,64,512]{3,2,1,0:T(8,128)S(1)}, f32[8,2,64,512]{3,2,1,0:T(8,128)S(1)}, u32[]{:S(2)}, u32[]{:S(2)}) collective-permute-start(f32[8,2,64,512]{3,2,1,0:T(8,128)S(1)} %broadcast_select_fusion.3), channel_id=1, source_target_pairs={{15,0},{0,1},{1,2},{2,3},{3,4},{4,5},{5,6},{6,7},{7,8},{8,9},{9,10... | collective-permute-start | bytes 6291464 | tf_op jit(solution)/shard_map/ppermute | solution.py:25
  218.6 8.9 %collective-permute-start.7 = (f32[8,2,64,1]{3,2,1,0:T(8,128)S(1)}, f32[8,2,64,1]{3,2,1,0:T(8,128)S(1)}, u32[]{:S(2)}, u32[]{:S(2)}) collective-permute-start(f32[8,2,64,1]{3,2,1,0:T(8,128)S(1)} %slice.187), channel_id=1, source_target_pairs={{15,0},{0,1},{1,2},{2,3},{3,4},{4,5},{5,6},{6,7},{7,8},{8,9},{9,10... | collective-permute-start | bytes 12296 | tf_op jit(solution)/shard_map/ppermute | solution.py:25
  228.3 6.7 %collective-permute-start.8 = (f32[8,2,2,512]{3,2,1,0:T(2,128)S(1)}, f32[8,2,2,512]{3,2,1,0:T(2,128)S(1)}, u32[]{:S(2)}, u32[]{:S(2)}) collective-permute-start(f32[8,2,2,512]{3,2,1,0:T(2,128)S(1)} %get-tuple-element.15), channel_id=1, source_target_pairs={{0,16},{16,32},{32,48},{48,64},{64,80},{80,96},{96,112},{1,17},{17... | collective-permute-start | bytes 196616 | tf_op jit(solution)/shard_map/ppermute | solution.py:16
  233.7 7.4 %collective-permute-start.9 = (f32[8,2,2,512]{3,2,1,0:T(2,128)S(1)}, f32[8,2,2,512]{3,2,1,0:T(2,128)S(1)}, u32[]{:S(2)}, u32[]{:S(2)}) collective-permute-start(f32[8,2,2,512]{3,2,1,0:T(2,128)S(1)} %get-tuple-element.16), channel_id=1, source_target_pairs={{16,0},{32,16},{48,32},{64,48},{80,64},{96,80},{112,96},{17,1},{33... | collective-permute-start | bytes 196616 | tf_op jit(solution)/shard_map/ppermute | solution.py:17
  242.5 26.7 %collective-permute-start.10 = (f32[8,2,64,512]{3,2,1,0:T(8,128)S(1)}, f32[8,2,64,512]{3,2,1,0:T(8,128)S(1)}, u32[]{:S(2)}, u32[]{:S(2)}) collective-permute-start(f32[8,2,64,512]{3,2,1,0:T(8,128)S(1)} %fusion.10), channel_id=1, source_target_pairs={{15,0},{0,1},{1,2},{2,3},{3,4},{4,5},{5,6},{6,7},{7,8},{8,9},{9,10... | collective-permute-start | bytes 6291464 | tf_op jit(solution)/shard_map/ppermute | solution.py:25
  269.7 46.5 %collective-permute-start.11 = (f32[8,2,64,512]{3,2,1,0:T(8,128)S(1)}, f32[8,2,64,512]{3,2,1,0:T(8,128)S(1)}, u32[]{:S(2)}, u32[]{:S(2)}) collective-permute-start(f32[8,2,64,512]{3,2,1,0:T(8,128)S(1)} %broadcast_select_fusion.4), channel_id=1, source_target_pairs={{14,0},{15,1},{0,2},{1,3},{2,4},{3,5},{4,6},{5,7},{6,8},{7,9},{8,1... | collective-permute-start | bytes 6291464 | tf_op jit(solution)/shard_map/ppermute | solution.py:25
  316.7 46.4 %collective-permute-start.12 = (f32[8,2,64,512]{3,2,1,0:T(8,128)S(1)}, f32[8,2,64,512]{3,2,1,0:T(8,128)S(1)}, u32[]{:S(2)}, u32[]{:S(2)}) collective-permute-start(f32[8,2,64,512]{3,2,1,0:T(8,128)S(1)} %broadcast_select_fusion.5), channel_id=1, source_target_pairs={{12,0},{13,1},{14,2},{15,3},{0,4},{1,5},{2,6},{3,7},{4,8},{5,9},{6... | collective-permute-start | bytes 6291464 | tf_op jit(solution)/shard_map/ppermute | solution.py:25
  363.8 43.4 %collective-permute-start.13 = (f32[8,2,64,512]{3,2,1,0:T(8,128)S(1)}, f32[8,2,64,512]{3,2,1,0:T(8,128)S(1)}, u32[]{:S(2)}, u32[]{:S(2)}) collective-permute-start(f32[8,2,64,512]{3,2,1,0:T(8,128)S(1)} %broadcast_select_fusion.6), channel_id=1, source_target_pairs={{8,0},{9,1},{10,2},{11,3},{12,4},{13,5},{14,6},{15,7},{0,8},{1,9},... | collective-permute-start | bytes 6291464 | tf_op jit(solution)/shard_map/ppermute | solution.py:25
  407.6 31.7 %collective-permute-start.14 = (f32[8,2,64,512]{3,2,1,0:T(8,128)S(1)}, f32[8,2,64,512]{3,2,1,0:T(8,128)S(1)}, u32[]{:S(2)}, u32[]{:S(2)}) collective-permute-start(f32[8,2,64,512]{3,2,1,0:T(8,128)S(1)} %broadcast_select_fusion.7), channel_id=1, source_target_pairs={{15,0},{0,1},{1,2},{2,3},{3,4},{4,5},{5,6},{6,7},{7,8},{8,9},{9,10... | collective-permute-start | bytes 6291464 | tf_op jit(solution)/shard_map/ppermute | solution.py:25
  452.8 8.7 %collective-permute-start.15 = (f32[8,2,64,1]{3,2,1,0:T(8,128)S(1)}, f32[8,2,64,1]{3,2,1,0:T(8,128)S(1)}, u32[]{:S(2)}, u32[]{:S(2)}) collective-permute-start(f32[8,2,64,1]{3,2,1,0:T(8,128)S(1)} %slice.206), channel_id=1, source_target_pairs={{15,0},{0,1},{1,2},{2,3},{3,4},{4,5},{5,6},{6,7},{7,8},{8,9},{9,10... | collective-permute-start | bytes 12296 | tf_op jit(solution)/shard_map/ppermute | solution.py:25
where the time goes:
time: 470 us; the launch traced here: 464 us
  waiting for transfers between devices  369 us (79%)
  starting transfers between devices  53.6 us (11%)
  other arithmetic  35.4 us (8%)
  local copies, waits for them, and re-layouts  5.29 us (1%)
    ppermute x12, waiting for transfers between devices, passed_along(): return lax.ppermute(block, axis, route)  363 us
    ppermute x12, starting transfers between devices, passed_along(): return lax.ppermute(block, axis, route)  39.5 us
    select_n x18, other arithmetic, slide_rows(): values = jnp.where(picked[None, None, :, None], moved, values)  24.2 us
    ppermute x2, starting transfers between devices, with_halo(): before = lax.ppermute(last, axis, up)  11.5 us
  transfers between devices with their start and end apart: 16, of which 13 were waited for; matrix products, arithmetic and copies ran while one was open for 1% of the time, Pallas kernels for 0%

commit v1 on v0

v1 whole, which is shorter than its diff:
```python
import functools

import jax
import jax.numpy as jnp
from jax import lax
from jax.experimental import pallas as pl
from jax.experimental.pallas import tpu as pltpu
from jax.sharding import PartitionSpec as P

LANES = 128
HALO = 4


def diffused(far_up, up, here, down, far_down, factor):
    return here + factor * (16.0 * (up + down) - (far_up + far_down) - 30.0 * here)


def partly_shifted(row, shift, weight, carry_ref):
    lines = row.shape[0]
    part = shift & (LANES - 1)
    lane = lax.broadcasted_iota(jnp.int32, row.shape, 1)
    first = (1.0 - weight) * pltpu.roll(row, part, 1)
    behind = weight * pltpu.roll(row, (part + 1) & (LANES - 1), 1)
    stays_first = lane >= part
    stays_behind = lane > part
    stays = jnp.where(stays_first, first, 0.0) + jnp.where(stays_behind, behind, 0.0)
    moves = jnp.where(stays_first, 0.0, first) + jnp.where(stays_behind, 0.0, behind)
    carry_ref[pl.ds(8, lines)] = moves
    carry_ref[pl.ds(7, 1)] = moves[lines - 1 :]
    return stays + carry_ref[pl.ds(7, lines)]


def advance_kernel(offsets, fractions, factors, up, main, down, out, grid, once, final, carry, twice, sems):
    rows, lines = final.shape[0], final.shape[1]
    blocks = main.shape[0]
    per = lines // blocks
    ext = rows + 4

    copies = [
        pltpu.make_async_copy(up, grid.at[pl.ds(0, HALO)], sems.at[0]),
        pltpu.make_async_copy(down, grid.at[pl.ds(HALO + rows, HALO)], sems.at[1]),
    ]
    for block in range(blocks):
        for c in range(per):
            copies.append(
                pltpu.make_async_copy(
                    main.at[block, :, pl.ds(c * LANES, LANES)],
                    grid.at[pl.ds(HALO, rows), block * per + c],
                    sems.at[2 + block * per + c],
                )
            )
    for copy in copies:
        copy.start()
    for copy in copies:
        copy.wait()

    def first_step(i, _):
        row = diffused(grid[i], grid[i + 1], grid[i + 2], grid[i + 3], grid[i + 4], factors[i])
        row = partly_shifted(row, offsets[0, i], fractions[0, i], carry.at[0])
        once[i, pl.ds(0, lines)] = row
        once[i, pl.ds(lines, lines)] = row
        return _

    lax.fori_loop(0, ext, first_step, 0)

    def moved(i):
        return once[i, pl.ds(lines - (offsets[0, i] >> 7), lines)]

    def second_step(i, _):
        row = diffused(moved(i), moved(i + 1), moved(i + 2), moved(i + 3), moved(i + 4), factors[i + 2])
        row = partly_shifted(row, offsets[1, i + 2], fractions[1, i + 2], carry.at[0])
        twice[0, pl.ds(0, lines)] = row
        twice[0, pl.ds(lines, lines)] = row
        final[i] = twice[0, pl.ds(lines - (offsets[1, i + 2] >> 7), lines)]
        return _

    lax.fori_loop(0, rows, second_step, 0)

    copies = []
    for block in range(blocks):
        for c in range(per):
            copies.append(
                pltpu.make_async_copy(
                    final.at[:, block * per + c],
                    out.at[block, :, pl.ds(c * LANES, LANES)],
                    sems.at[2 + block * per + c],
                )
            )
    for copy in copies:
        copy.start()
    for copy in copies:
        copy.wait()


def advance(offsets, fractions, factors, up, main, down):
    blocks, rows, width = main.shape
    lines = blocks * width // LANES
    smem = pl.BlockSpec(memory_space=pltpu.SMEM)
    anywhere = pl.BlockSpec(memory_space=pl.ANY)
    return pl.pallas_call(
        advance_kernel,
        out_shape=jax.ShapeDtypeStruct(main.shape, main.dtype),
        in_specs=[smem] * 3 + [anywhere] * 3,
        out_specs=anywhere,
        scratch_shapes=[
            pltpu.VMEM((rows + 2 * HALO, lines, LANES), jnp.float32),
            pltpu.VMEM((rows + 4, 2 * lines, LANES), jnp.float32),
            pltpu.VMEM((rows, lines, LANES), jnp.float32),
            pltpu.VMEM((1, lines + 8, LANES), jnp.float32),
            pltpu.VMEM((1, 2 * lines, LANES), jnp.float32),
            pltpu.SemaphoreType.DMA((2 + lines,)),
        ],
        compiler_params=pltpu.CompilerParams(vmem_limit_bytes=32 << 20),
    )(offsets, fractions, factors, up, main, down)


def from_neighbours(first, last, axis):
    peers = lax.axis_size(axis)
    forth = [(i, i + 1) for i in range(peers - 1)]
    back = [(j, i) for i, j in forth]
    return lax.ppermute(last, axis, forth), lax.ppermute(first, axis, back)


def as_rows(part):
    blocks, rows, width = part.shape
    cut = part.reshape(blocks, rows, width // LANES, LANES)
    return jnp.transpose(cut, (1, 0, 2, 3)).reshape(rows, blocks * width // LANES, LANES)


def shards(fields, offsets, fractions, coefs):
    shape = fields.shape
    rows, width = shape[2], shape[3]
    packed = jnp.concatenate([offsets.astype(jnp.float32), fractions, coefs[None] / 12.0])
    before, after = from_neighbours(packed[:, :2], packed[:, rows - 2 :], "rad")
    packed = jnp.concatenate([before, packed, after], axis=1)
    steps = offsets.shape[0]

    main = lax.all_to_all(fields.reshape(-1, rows, width), "azi", 0, 0, tiled=True)
    up, down = from_neighbours(as_rows(main[:, :HALO]), as_rows(main[:, rows - HALO :]), "rad")
    done = advance(
        packed[:steps].astype(jnp.int32), packed[steps : 2 * steps], packed[2 * steps], up, main, down
    )
    return lax.all_to_all(done, "azi", 0, 0, tiled=True).reshape(shape)


def solution(mesh):
    placed = (P(None, None, "rad", "azi"), P(None, "rad"), P(None, "rad"), P("rad"))
    return jax.shard_map(
        shards, mesh=mesh, in_specs=placed, out_specs=P(None, None, "rad", "azi"), check_vma=False
    )
```

time: 470 us -> 104 us (0.22); the launches traced: 464 us -> 104 us
  waiting for transfers between devices: 369 us -> 28 us
  other arithmetic: 35.4 us -> 0.1 us
  starting transfers between devices: 53.6 us -> 18.4 us
  blocking collectives: 0 us -> 34.5 us
  Pallas kernels: 0 us -> 20.9 us
    ppermute x16 -> x4, waiting for transfers between devices: 369 us -> 27.7 us  [from_neighbours(): return (lax.ppermute(last, axis, forth), lax.ppermute(first, axis, back))]
    ppermute x16 -> x4, starting transfers between devices: 53.6 us -> 11.3 us  [from_neighbours(): return (lax.ppermute(last, axis, forth), lax.ppermute(first, axis, back))]
    all_to_all x0 -> x1, blocking collectives: none -> 34.5 us  [shards(): return lax.all_to_all(done, 'azi', 0, 0, tiled=True).reshape(shape)]
    select_n x26 -> x0, other arithmetic: 28.5 us -> none  [the longest x18 24.2 us: slide_rows(): values = jnp.where(picked[None, None, :, None], moved, values)]
    pallas_call x0 -> x1, Pallas kernels: none -> 20.9 us  [advance(): pl.pallas_call(advance_kernel, out_shape=jax.ShapeDtypeStruct(main.shape,...]
    all_to_all x0 -> x1, starting transfers between devices: none -> 7.06 us  [shards(): lax.all_to_all(fields.reshape(-1, rows, width), 'azi', 0, 0, tiled=True)]
    add x4 -> x0, other arithmetic: 5.24 us -> none  [the longest x2 2.76 us: shards(): state = (1.0 - weight) * first + weight * behind]
  transfers between devices with their start and end apart: 16 -> 5, of which waited for: 13 -> 5; matrix products, arithmetic and copies ran while one was open for 1% -> 0% of each run, Pallas kernels for 0% -> 0%
where the time goes in v1:
time: 104 us
  blocking collectives  34.5 us (33%)
  waiting for transfers between devices  28 us (27%)
  Pallas kernels  20.9 us (20%)
  starting transfers between devices  18.4 us (18%)
  local copies, waits for them, and re-layouts  1.66 us (2%)
    all_to_all x1, blocking collectives, shards(): return lax.all_to_all(done, 'azi', 0, 0, tiled=True).reshape(shape)  34.5 us
    ppermute x4, waiting for transfers between devices, from_neighbours(): return (lax.ppermute(last, axis, forth), lax.ppermute(first, axis, back))  27.7 us
    pallas_call x1, Pallas kernels, advance(): pl.pallas_call(advance_kernel, out_shape=jax.ShapeDtypeStruct(main.shape,...  20.9 us
    ppermute x4, starting transfers between devices, from_neighbours(): return (lax.ppermute(last, axis, forth), lax.ppermute(first, axis, back))  11.3 us
    all_to_all x1, starting transfers between devices, shards(): lax.all_to_all(fields.reshape(-1, rows, width), 'azi', 0, 0, tiled=True)  7.06 us
  transfers between devices with their start and end apart: 5, of which 5 were waited for; matrix products, arithmetic and copies ran while one was open for 0% of the time, Pallas kernels for 0%

profile of v1, /device:TPU:1, one launch (start us, length us, event | category | flops | bytes accessed | tf_op | source)
XLA Modules:
  0.0 103.7 jit_solution(13113621780475861408)
XLA Ops:
  0.0 0.0 copy-start.1
  0.0 0.0 copy-start.2
  0.0 0.0 copy-start
  0.0 7.1 %all-to-all-start = ((f32[16,64,512]{2,1,0:T(8,128)}), f32[16,64,512]{2,1,0:T(8,128)S(1)}, u32[]{:S(2)}, u32[]{:S(2)}) async-start(f32[16,64,512]{2,1,0:T(8,128)} %bitcast.12), calls=%async_computation | async-start | bytes 4194304 | tf_op jit(solution)/shard_map/all_to_all | solution.py:138
  7.1 0.0 copy-done.1
  7.1 0.0 copy-done.2
  7.1 0.0 copy-done
  7.1 0.1 fusion.2
  7.2 4.4 %collective-permute-start = (f32[5,2]{1,0:T(8,128)S(1)}, f32[5,2]{1,0:T(8,128)S(1)}, u32[]{:S(2)}, u32[]{:S(2)}) collective-permute-start(f32[5,2]{1,0:T(8,128)S(1)} %get-tuple-element.9), channel_id=1, source_target_pairs={{0,16},{16,32},{32,48},{48,64},{64,80},{80,96},{96,112},{1,17},{17... | collective-permute-start | bytes 128 | tf_op jit(solution)/shard_map/ppermute | solution.py:121
  11.6 1.3 %collective-permute-start.1 = (f32[5,2]{1,0:T(8,128)S(1)}, f32[5,2]{1,0:T(8,128)S(1)}, u32[]{:S(2)}, u32[]{:S(2)}) collective-permute-start(f32[5,2]{1,0:T(8,128)S(1)} %get-tuple-element.10), channel_id=1, source_target_pairs={{16,0},{32,16},{48,32},{64,48},{80,64},{96,80},{112,96},{17,1},{33... | collective-permute-start | bytes 128 | tf_op jit(solution)/shard_map/ppermute | solution.py:121
  12.9 18.5 %collective-permute-done = f32[5,2]{1,0:T(8,128)S(1)} collective-permute-done((f32[5,2]{1,0:T(8,128)S(1)}, f32[5,2]{1,0:T(8,128)S(1)}, u32[]{:S(2)}, u32[]{:S(2)}) %collective-permute-start) | collective-permute-done | bytes 72 | tf_op jit(solution)/shard_map/ppermute | solution.py:121
  31.4 3.3 %collective-permute-done.1 = f32[5,2]{1,0:T(8,128)S(1)} collective-permute-done((f32[5,2]{1,0:T(8,128)S(1)}, f32[5,2]{1,0:T(8,128)S(1)}, u32[]{:S(2)}, u32[]{:S(2)}) %collective-permute-start.1) | collective-permute-done | bytes 72 | tf_op jit(solution)/shard_map/ppermute | solution.py:121
  34.7 0.1 pad_maximum_fusion.1
  34.7 0.3 all-to-all-done.main
  35.1 0.1 fusion
  35.1 0.1 reshape.22
  35.2 0.1 reshape.20
  35.3 4.4 %collective-permute-start.2 = (f32[4,64,128]{2,1,0:T(8,128)S(1)}, f32[4,64,128]{2,1,0:T(8,128)S(1)}, u32[]{:S(2)}, u32[]{:S(2)}) collective-permute-start(f32[4,64,128]{2,1,0:T(8,128)S(1)} %bitcast.15), channel_id=1, source_target_pairs={{0,16},{16,32},{32,48},{48,64},{64,80},{80,96},{96,112},{1,17},{17... | collective-permute-start | bytes 393224 | tf_op jit(solution)/shard_map/ppermute | solution.py:121
  39.7 1.3 %collective-permute-start.3 = (f32[4,64,128]{2,1,0:T(8,128)S(1)}, f32[4,64,128]{2,1,0:T(8,128)S(1)}, u32[]{:S(2)}, u32[]{:S(2)}) collective-permute-start(f32[4,64,128]{2,1,0:T(8,128)S(1)} %bitcast.14), channel_id=1, source_target_pairs={{16,0},{32,16},{48,32},{64,48},{80,64},{96,80},{112,96},{17,1},{33... | collective-permute-start | bytes 393224 | tf_op jit(solution)/shard_map/ppermute | solution.py:121
  41.0 0.6 collective-permute-done.2.up
  41.6 5.3 %collective-permute-done.3.down = f32[4,64,128]{2,1,0:T(8,128)S(1)} collective-permute-done((f32[4,64,128]{2,1,0:T(8,128)S(1)}, f32[4,64,128]{2,1,0:T(8,128)S(1)}, u32[]{:S(2)}, u32[]{:S(2)}) %collective-permute-start.3) | collective-permute-done | bytes 131104 | tf_op jit(solution)/shard_map/ppermute | solution.py:121
  46.9 20.9 %shard_map.46 = f32[16,64,512]{2,1,0:T(8,128)S(1)} custom-call(s32[2,68]{1,0:T(2,128)S(1)} %get-tuple-element.8.offsets, f32[2,68]{1,0:T(2,128)S(1)} %get-tuple-element.7.fractions, f32[68]{0:T(128)S(1)} %slice_bitcast_fusion.factors, f32[4,64,128]{2,1,0:T(8,128)S(1)} %collective-permute-done.2.up, f32[16,64,512]{2,1,0:T(8,128)S(1)} %all-to-all-done.main, ...), custom_call_target="tpu_custom_call" | custom-call | tf_op jit(solution)/shard_map/pallas_call | solution.py:100
  67.8 34.5 %all_to_all.10 = f32[16,64,512]{2,1,0:T(8,128)S(1)} all-to-all(f32[16,64,512]{2,1,0:T(8,128)S(1)} %shard_map.46), channel_id=1, replica_groups=mesh['rad'=8,'azi'=16] {'azi'}, dimensions={0} | all-to-all | bytes 4194304 | tf_op jit(solution)/shard_map/all_to_all | solution.py:143
  102.3 1.3 %copy.8 = f32[8,2,64,512]{3,2,1,0:T(8,128)} copy(f32[8,2,64,512]{3,2,1,0:T(8,128)S(1)} %bitcast.11) | data formatting | bytes 4194304
  (7 shorter events, 0.1 us)
Async XLA Ops:
  0.0 7.1 %copy-start.1 = (s32[2,64]{1,0:T(2,128)S(1)}, s32[2,64]{1,0:T(2,128)}, u32[]{:S(2)}) copy-start(s32[2,64]{1,0:T(2,128)} %param.5) | copy-start | bytes 1540
  0.0 7.1 %copy-start.2 = (f32[64]{0:T(128)S(1)}, f32[64]{0:T(128)}, u32[]{:S(2)}) copy-start(f32[64]{0:T(128)} %param.7) | copy-start | bytes 772
  0.0 7.1 %copy-start = (f32[2,64]{1,0:T(2,128)S(1)}, f32[2,64]{1,0:T(2,128)}, u32[]{:S(2)}) copy-start(f32[2,64]{1,0:T(2,128)} %param.6) | copy-start | bytes 1540
  0.0 35.0 %all-to-all-start = ((f32[16,64,512]{2,1,0:T(8,128)}), f32[16,64,512]{2,1,0:T(8,128)S(1)}, u32[]{:S(2)}, u32[]{:S(2)}) async-start(f32[16,64,512]{2,1,0:T(8,128)} %bitcast.12), calls=%async_computation | async-start | bytes 4194304 | tf_op jit(solution)/shard_map/all_to_all | solution.py:138
  7.2 24.2 %collective-permute-start = (f32[5,2]{1,0:T(8,128)S(1)}, f32[5,2]{1,0:T(8,128)S(1)}, u32[]{:S(2)}, u32[]{:S(2)}) collective-permute-start(f32[5,2]{1,0:T(8,128)S(1)} %get-tuple-element.9), channel_id=1, source_target_pairs={{0,16},{16,32},{32,48},{48,64},{64,80},{80,96},{96,112},{1,17},{17... | collective-permute-start | bytes 128 | tf_op jit(solution)/shard_map/ppermute | solution.py:121
  11.6 23.1 %collective-permute-start.1 = (f32[5,2]{1,0:T(8,128)S(1)}, f32[5,2]{1,0:T(8,128)S(1)}, u32[]{:S(2)}, u32[]{:S(2)}) collective-permute-start(f32[5,2]{1,0:T(8,128)S(1)} %get-tuple-element.10), channel_id=1, source_target_pairs={{16,0},{32,16},{48,32},{64,48},{80,64},{96,80},{112,96},{17,1},{33... | collective-permute-start | bytes 128 | tf_op jit(solution)/shard_map/ppermute | solution.py:121
  35.3 6.3 %collective-permute-start.2 = (f32[4,64,128]{2,1,0:T(8,128)S(1)}, f32[4,64,128]{2,1,0:T(8,128)S(1)}, u32[]{:S(2)}, u32[]{:S(2)}) collective-permute-start(f32[4,64,128]{2,1,0:T(8,128)S(1)} %bitcast.15), channel_id=1, source_target_pairs={{0,16},{16,32},{32,48},{48,64},{64,80},{80,96},{96,112},{1,17},{17... | collective-permute-start | bytes 393224 | tf_op jit(solution)/shard_map/ppermute | solution.py:121
  39.7 7.2 %collective-permute-start.3 = (f32[4,64,128]{2,1,0:T(8,128)S(1)}, f32[4,64,128]{2,1,0:T(8,128)S(1)}, u32[]{:S(2)}, u32[]{:S(2)}) collective-permute-start(f32[4,64,128]{2,1,0:T(8,128)S(1)} %bitcast.14), channel_id=1, source_target_pairs={{16,0},{32,16},{48,32},{64,48},{80,64},{96,80},{112,96},{17,1},{33... | collective-permute-start | bytes 393224 | tf_op jit(solution)/shard_map/ppermute | solution.py:121

commit v2 on v0

v2 whole, which is shorter than its diff:
```python
import jax
import jax.numpy as jnp
from jax import lax
from jax.experimental import pallas as pl
from jax.experimental.pallas import tpu as pltpu
from jax.sharding import PartitionSpec as P

LANES = 128
REACH = 2
HALO = 2 * REACH
TILE = 8


def diffused(far_up, up, here, down, far_down, factor):
    return here + factor * (16.0 * (up + down) - (far_up + far_down) - 30.0 * here)


def partly_shifted(row, shift, weight):
    part = shift & (LANES - 1)
    lane = lax.broadcasted_iota(jnp.int32, row[0].shape, 1)
    own_first, own_behind = lane >= part, lane > part
    first = [pltpu.roll(line, part, 1) for line in row]
    behind = [pltpu.roll(line, (part + 1) & (LANES - 1), 1) for line in row]
    first = [pltpu.roll(first[-1], 1, 0)] + first
    behind = [pltpu.roll(behind[-1], 1, 0)] + behind
    return [
        (1.0 - weight) * jnp.where(own_first, first[c + 1], first[c])
        + weight * jnp.where(own_behind, behind[c + 1], behind[c])
        for c in range(len(row))
    ]


def keep(ref, i, row):
    blocks = row[0].shape[0]
    for c, line in enumerate(row):
        ref[i, c, pl.ds(0, blocks)] = line
        ref[i, c, pl.ds(blocks, blocks)] = line


def moved(ref, i, shift):
    per, blocks = ref.shape[1], ref.shape[2] // 2
    lines = shift // LANES
    some, whole = lines % per, lines // per
    row = []
    for c in range(per):
        wraps = (c < some).astype(jnp.int32)
        row.append(ref[i, c - some + wraps * per, pl.ds(blocks - whole - wraps, blocks)])
    return row


def in_groups(count, size, body):
    size = next(s for s in range(size, 0, -1) if count % s == 0)

    def group(t, carry):
        body(t * size, size)
        return carry

    lax.fori_loop(0, count // size, group, 0)


def two_steps(offsets, fractions, factors, base, grid, once, twice, to):
    per = grid.shape[1]
    rows = grid.shape[0] - 2 * HALO

    def first_step(start, size):
        for u in range(size):
            i = start + u
            at = base + REACH + i
            row = [diffused(*[grid[i + j, c] for j in range(2 * REACH + 1)], factors[at]) for c in range(per)]
            keep(once, i, partly_shifted(row, offsets[0, at], fractions[0, at]))

    def second_step(start, size):
        lines = [moved(once, start + j, offsets[0, base + REACH + start + j]) for j in range(size + 2 * REACH)]
        for u in range(size):
            i = start + u
            at = base + HALO + i
            row = [diffused(*[lines[u + j][c] for j in range(2 * REACH + 1)], factors[at]) for c in range(per)]
            keep(twice, to + i, partly_shifted(row, offsets[1, at], fractions[1, at]))

    in_groups(rows + 2 * REACH, 4, first_step)
    in_groups(rows, 4, second_step)


def write(offsets, base, twice, start, count, out, to):
    def some(first, size):
        for u in range(size):
            i = first + u
            out[:, to + i, :] = jnp.concatenate(moved(twice, start + i, offsets[1, base + i]), axis=1)

    in_groups(count, 4, some)


def load(grid, at, source, row):
    line = source[:, row, :]
    for c in range(grid.shape[1]):
        grid[at, c] = line[:, c * LANES : (c + 1) * LANES]


def inner_kernel(offsets, fractions, factors, main, out, grid, once, twice, laid, sem):
    rows = main.shape[1]

    def relay(start, size):
        for u in range(size):
            load(grid, start + u, main, start + u)

    in_groups(rows, 4, relay)
    two_steps(offsets, fractions, factors, 0, grid, once, twice, 0)
    write(offsets, HALO, twice, 0, rows - 2 * HALO, laid, HALO)
    copy = pltpu.make_async_copy(laid, out, sem)
    copy.start()
    copy.wait()


def edge_kernel(offsets, fractions, factors, halo, main, given, out, grid, once, twice, laid, sems):
    rows = main.shape[1]
    inside = rows - 2 * HALO
    near = [pl.ds(0, TILE), pl.ds(rows - TILE, TILE)]
    fetches = [pltpu.make_async_copy(given.at[:, near[s]], laid.at[s], sems.at[s]) for s in range(2)]
    for fetch in fetches:
        fetch.start()
    stores = []
    for side in range(2):
        base = side * (inside + HALO)
        for r in range(HALO):
            load(grid, r + side * 2 * HALO, halo, side * HALO + r)
        for r in range(2 * HALO):
            load(grid, r + (1 - side) * HALO, main, r + side * inside)
        two_steps(offsets, fractions, factors, base, grid, once, twice, side * HALO)
        fetches[side].wait()
        write(offsets, base + HALO, twice, side * HALO, HALO, laid.at[side], side * (TILE - HALO))
        stores.append(pltpu.make_async_copy(laid.at[side], out.at[:, near[side]], sems.at[side]))
        stores[-1].start()
    for store in stores:
        store.wait()


def call(kernel, tables, arrays, kept, out, scratch, sems, vmem):
    smem = pl.BlockSpec(memory_space=pltpu.SMEM)
    local = pl.BlockSpec(memory_space=pltpu.VMEM)
    far = pl.BlockSpec(memory_space=pltpu.HBM)
    given = len(tables) + len(arrays)
    return pl.pallas_call(
        kernel,
        out_shape=pltpu.HBM(out, jnp.float32),
        in_specs=[smem] * len(tables) + [local] * len(arrays) + [far] * len(kept),
        out_specs=far,
        scratch_shapes=[pltpu.VMEM(shape, jnp.float32) for shape in scratch] + [sems],
        input_output_aliases={given + i: i for i in range(len(kept))},
        compiler_params=pltpu.CompilerParams(vmem_limit_bytes=vmem << 20),
    )(*tables, *arrays, *[pltpu.with_memory_space_constraint(k, pltpu.HBM) for k in kept])


def from_neighbours(first, last, axis):
    peers = lax.axis_size(axis)
    forth = [(i, i + 1) for i in range(peers - 1)]
    back = [(j, i) for i, j in forth]
    return lax.ppermute(last, axis, forth), lax.ppermute(first, axis, back)


def shards(fields, offsets, fractions, coefs):
    shape = fields.shape
    rows, width = shape[2], shape[3]
    steps = offsets.shape[0]
    blocks = fields.reshape(-1, rows, width)
    factors = coefs / 12.0

    main = lax.all_to_all(blocks, "azi", 0, 0, tiled=True)

    packed = jnp.concatenate([offsets.astype(jnp.float32), fractions, factors[None]])
    before, after = from_neighbours(packed[:, :HALO], packed[:, rows - HALO :], "rad")
    packed = jnp.concatenate([before, packed, after], axis=1)
    halo = jnp.concatenate(from_neighbours(blocks[:, :HALO], blocks[:, rows - HALO :], "rad"), axis=1)
    halo = lax.all_to_all(halo, "azi", 0, 0, tiled=True)

    members, per = blocks.shape[0], width // LANES

    def single(count):
        return (count, per, members, LANES)

    def double(count):
        return (count, per, 2 * members, LANES)

    inside = rows - 2 * HALO
    done = call(
        inner_kernel,
        (offsets, fractions, factors),
        (main,),
        (),
        main.shape,
        [single(rows), double(rows - 2 * REACH), double(inside), main.shape],
        pltpu.SemaphoreType.DMA,
        16,
    )
    tables = (packed[:steps].astype(jnp.int32), packed[steps : 2 * steps], packed[2 * steps])
    done = call(
        edge_kernel,
        tables,
        (halo, main),
        (done,),
        main.shape,
        [single(3 * HALO), double(HALO + 2 * REACH), double(2 * HALO), (2, members, TILE, width)],
        pltpu.SemaphoreType.DMA((2,)),
        4,
    )
    return lax.all_to_all(done, "azi", 0, 0, tiled=True).reshape(shape)


def solution(mesh):
    placed = (P(None, None, "rad", "azi"), P(None, "rad"), P(None, "rad"), P("rad"))
    return jax.shard_map(
        shards, mesh=mesh, in_specs=placed, out_specs=P(None, None, "rad", "azi"), check_vma=False
    )
```

time: 470 us -> 96.2 us (0.20); the launches traced: 464 us -> 95.8 us
  waiting for transfers between devices: 369 us -> 19.5 us
  other arithmetic: 35.4 us -> 0.86 us
  blocking collectives: 0 us -> 32.4 us
  starting transfers between devices: 53.6 us -> 26 us
  Pallas kernels: 0 us -> 14.4 us
    ppermute x16 -> x4, waiting for transfers between devices: 369 us -> 19.5 us  [from_neighbours(): return (lax.ppermute(last, axis, forth), lax.ppermute(first, axis, back))]
    ppermute x16 -> x4, starting transfers between devices: 53.6 us -> 12.4 us  [from_neighbours(): return (lax.ppermute(last, axis, forth), lax.ppermute(first, axis, back))]
    all_to_all x0 -> x1, blocking collectives: none -> 32.4 us  [shards(): return lax.all_to_all(done, 'azi', 0, 0, tiled=True).reshape(shape)]
    select_n x26 -> x0, other arithmetic: 28.5 us -> none  [the longest x18 24.2 us: slide_rows(): values = jnp.where(picked[None, None, :, None], moved, values)]
    pallas_call x0 -> x2, Pallas kernels: none -> 14.4 us  [call(): pl.pallas_call(kernel, out_shape=pltpu.HBM(out, jnp.float32), in_specs=[s...]
    all_to_all x0 -> x2, starting transfers between devices: none -> 13.6 us  [the longest x1 7.06 us: shards(): main = lax.all_to_all(blocks, 'azi', 0, 0, tiled=True)]
    add x4 -> x0, other arithmetic: 5.24 us -> none  [the longest x2 2.76 us: shards(): state = (1.0 - weight) * first + weight * behind]
  transfers between devices with their start and end apart: 16 -> 6, of which waited for: 13 -> 2; matrix products, arithmetic and copies ran while one was open for 1% -> 2% of each run, Pallas kernels for 0% -> 12%
where the time goes in v2:
time: 96.2 us; the launch traced here: 95.8 us
  blocking collectives  32.4 us (34%)
  starting transfers between devices  26 us (27%)
  waiting for transfers between devices  19.5 us (20%)
  Pallas kernels  14.4 us (15%)
  local copies, waits for them, and re-layouts  2.49 us (3%)
    all_to_all x1, blocking collectives, shards(): return lax.all_to_all(done, 'azi', 0, 0, tiled=True).reshape(shape)  32.4 us
    ppermute x4, waiting for transfers between devices, from_neighbours(): return (lax.ppermute(last, axis, forth), lax.ppermute(first, axis, back))  19.5 us
    pallas_call x2, Pallas kernels, call(): pl.pallas_call(kernel, out_shape=pltpu.HBM(out, jnp.float32), in_specs=[s...  14.4 us
    ppermute x4, starting transfers between devices, from_neighbours(): return (lax.ppermute(last, axis, forth), lax.ppermute(first, axis, back))  12.4 us
    all_to_all x1, starting transfers between devices, shards(): main = lax.all_to_all(blocks, 'azi', 0, 0, tiled=True)  7.06 us
    all_to_all x1, starting transfers between devices, shards(): halo = lax.all_to_all(halo, 'azi', 0, 0, tiled=True)  6.5 us
  transfers between devices with their start and end apart: 6, of which 2 were waited for; matrix products, arithmetic and copies ran while one was open for 2% of the time, Pallas kernels for 12%

profile of v2, /device:TPU:1, one launch (start us, length us, event | category | flops | bytes accessed | tf_op | source)
XLA Modules:
  0.0 95.8 jit_solution(16069799049496380053)
XLA Ops:
  0.0 0.0 copy-start.1
  0.0 0.0 copy-start.2
  0.0 0.0 copy-start
  0.0 7.1 %all-to-all-start.1 = ((f32[16,64,512]{2,1,0:T(8,128)}), f32[16,64,512]{2,1,0:T(8,128)S(1)}, u32[]{:S(2)}, u32[]{:S(2)}) async-start(f32[16,64,512]{2,1,0:T(8,128)} %bitcast.7), calls=%async_computation.1 | async-start | bytes 4194304 | tf_op jit(solution)/shard_map/all_to_all | solution.py:167
  7.1 1.1 %fusion.1 = (f32[16,4,512]{2,1,0:T(4,128)S(1)}, f32[16,4,512]{2,1,0:T(4,128)S(1)}) fusion(f32[16,64,512]{2,1,0:T(8,128)} %bitcast.8), kind=kLoop, calls=%fused_computation.7 | loop fusion | bytes 524288 | tf_op jit(solution)/shard_map/slice | solution.py:172
  8.1 4.4 %collective-permute-start.2 = (f32[16,4,512]{2,1,0:T(4,128)S(1)}, f32[16,4,512]{2,1,0:T(4,128)S(1)}, u32[]{:S(2)}, u32[]{:S(2)}) collective-permute-start(f32[16,4,512]{2,1,0:T(4,128)S(1)} %get-tuple-element.5), channel_id=1, source_target_pairs={{0,16},{16,32},{32,48},{48,64},{64,80},{80,96},{96,112},{1,17},{17... | collective-permute-start | bytes 393224 | tf_op jit(solution)/shard_map/ppermute | solution.py:157
  12.5 1.3 %collective-permute-start.3 = (f32[16,4,512]{2,1,0:T(4,128)S(1)}, f32[16,4,512]{2,1,0:T(4,128)S(1)}, u32[]{:S(2)}, u32[]{:S(2)}) collective-permute-start(f32[16,4,512]{2,1,0:T(4,128)S(1)} %get-tuple-element.6), channel_id=1, source_target_pairs={{16,0},{32,16},{48,32},{64,48},{80,64},{96,80},{112,96},{17,1},{33... | collective-permute-start | bytes 393224 | tf_op jit(solution)/shard_map/ppermute | solution.py:157
  13.8 0.0 copy-done.1
  13.9 0.0 copy-done.2
  13.9 0.0 copy-done
  13.9 0.1 fusion.3
  14.0 5.5 %collective-permute-start = (f32[5,4]{1,0:T(8,128)S(1)}, f32[5,4]{1,0:T(8,128)S(1)}, u32[]{:S(2)}, u32[]{:S(2)}) collective-permute-start(f32[5,4]{1,0:T(8,128)S(1)} %get-tuple-element.9), channel_id=1, source_target_pairs={{0,16},{16,32},{32,48},{48,64},{64,80},{80,96},{96,112},{1,17},{17... | collective-permute-start | bytes 248 | tf_op jit(solution)/shard_map/ppermute | solution.py:157
  19.5 1.3 %collective-permute-start.1 = (f32[5,4]{1,0:T(8,128)S(1)}, f32[5,4]{1,0:T(8,128)S(1)}, u32[]{:S(2)}, u32[]{:S(2)}) collective-permute-start(f32[5,4]{1,0:T(8,128)S(1)} %get-tuple-element.10), channel_id=1, source_target_pairs={{16,0},{32,16},{48,32},{64,48},{80,64},{96,80},{112,96},{17,1},{33... | collective-permute-start | bytes 248 | tf_op jit(solution)/shard_map/ppermute | solution.py:157
  20.8 13.4 %collective-permute-done = f32[5,4]{1,0:T(8,128)S(1)} collective-permute-done((f32[5,4]{1,0:T(8,128)S(1)}, f32[5,4]{1,0:T(8,128)S(1)}, u32[]{:S(2)}, u32[]{:S(2)}) %collective-permute-start) | collective-permute-done | bytes 112 | tf_op jit(solution)/shard_map/ppermute | solution.py:157
  34.2 6.1 %collective-permute-done.1 = f32[5,4]{1,0:T(8,128)S(1)} collective-permute-done((f32[5,4]{1,0:T(8,128)S(1)}, f32[5,4]{1,0:T(8,128)S(1)}, u32[]{:S(2)}, u32[]{:S(2)}) %collective-permute-start.1) | collective-permute-done | bytes 112 | tf_op jit(solution)/shard_map/ppermute | solution.py:157
  40.3 0.1 pad_maximum_fusion.2
  40.4 0.0 collective-permute-done.2
  40.4 0.0 collective-permute-done.3
  40.4 0.8 pad_maximum_fusion
  41.1 0.0 all-to-all-done.1.main
  41.1 6.5 %all-to-all-start = ((f32[16,8,512]{2,1,0:T(8,128)}), f32[16,8,512]{2,1,0:T(8,128)S(1)}, u32[]{:S(2)}, u32[]{:S(2)}) async-start(f32[16,8,512]{2,1,0:T(8,128)} %pad_maximum_fusion), calls=%async_computation | async-start | bytes 524288 | tf_op jit(solution)/shard_map/all_to_all | solution.py:173
  47.7 11.2 %shard_map.46.given = f32[16,64,512]{2,1,0:T(8,128)} custom-call(s32[2,64]{1,0:T(2,128)S(1)} %copy-done.1, f32[2,64]{1,0:T(2,128)S(1)} %copy-done, f32[64]{0:T(128)S(1)} %get-tuple-element.11.factors, f32[16,64,512]{2,1,0:T(8,128)S(1)} %all-to-all-done.1.main), custom_call_target="tpu_custom_call" | custom-call | tf_op jit(solution)/shard_map/pallas_call | solution.py:142
  58.9 0.0 all-to-all-done.halo
  58.9 3.2 %shard_map.47 = f32[16,64,512]{2,1,0:T(8,128)} custom-call(s32[2,72]{1,0:T(2,128)S(1)} %get-tuple-element.8.offsets, f32[2,72]{1,0:T(2,128)S(1)} %get-tuple-element.7.fractions, f32[72]{0:T(128)S(1)} %slice_bitcast_fusion.factors, f32[16,8,512]{2,1,0:T(8,128)S(1)} %all-to-all-done.halo, ...), custom_call_target="tpu_custom_call", output_to_operand_aliasing={{}: (5, {})} | custom-call | tf_op jit(solution)/shard_map/pallas_call | solution.py:142
  62.1 32.4 %all_to_all.15 = f32[16,64,512]{2,1,0:T(8,128)S(1)} all-to-all(f32[16,64,512]{2,1,0:T(8,128)} %shard_map.47), channel_id=1, replica_groups=mesh['rad'=8,'azi'=16] {'azi'}, dimensions={0} | all-to-all | bytes 4194304 | tf_op jit(solution)/shard_map/all_to_all | solution.py:205
  94.4 1.3 %copy.8 = f32[8,2,64,512]{3,2,1,0:T(8,128)} copy(f32[8,2,64,512]{3,2,1,0:T(8,128)S(1)} %bitcast.6) | data formatting | bytes 4194304
  (5 shorter events, 0.0 us)
Async XLA Ops:
  0.0 13.8 %copy-start.1 = (s32[2,64]{1,0:T(2,128)S(1)}, s32[2,64]{1,0:T(2,128)}, u32[]{:S(2)}) copy-start(s32[2,64]{1,0:T(2,128)} %offsets.1) | copy-start | bytes 1540
  0.0 13.9 %copy-start.2 = (f32[64]{0:T(128)S(1)}, f32[64]{0:T(128)}, u32[]{:S(2)}) copy-start(f32[64]{0:T(128)} %param.7) | copy-start | bytes 772
  0.0 13.9 %copy-start = (f32[2,64]{1,0:T(2,128)S(1)}, f32[2,64]{1,0:T(2,128)}, u32[]{:S(2)}) copy-start(f32[2,64]{1,0:T(2,128)} %fractions.1) | copy-start | bytes 1540
  0.0 41.1 %all-to-all-start.1 = ((f32[16,64,512]{2,1,0:T(8,128)}), f32[16,64,512]{2,1,0:T(8,128)S(1)}, u32[]{:S(2)}, u32[]{:S(2)}) async-start(f32[16,64,512]{2,1,0:T(8,128)} %bitcast.7), calls=%async_computation.1 | async-start | bytes 4194304 | tf_op jit(solution)/shard_map/all_to_all | solution.py:167
  8.1 32.2 %collective-permute-start.2 = (f32[16,4,512]{2,1,0:T(4,128)S(1)}, f32[16,4,512]{2,1,0:T(4,128)S(1)}, u32[]{:S(2)}, u32[]{:S(2)}) collective-permute-start(f32[16,4,512]{2,1,0:T(4,128)S(1)} %get-tuple-element.5), channel_id=1, source_target_pairs={{0,16},{16,32},{32,48},{48,64},{64,80},{80,96},{96,112},{1,17},{17... | collective-permute-start | bytes 393224 | tf_op jit(solution)/shard_map/ppermute | solution.py:157
  12.5 27.8 %collective-permute-start.3 = (f32[16,4,512]{2,1,0:T(4,128)S(1)}, f32[16,4,512]{2,1,0:T(4,128)S(1)}, u32[]{:S(2)}, u32[]{:S(2)}) collective-permute-start(f32[16,4,512]{2,1,0:T(4,128)S(1)} %get-tuple-element.6), channel_id=1, source_target_pairs={{16,0},{32,16},{48,32},{64,48},{80,64},{96,80},{112,96},{17,1},{33... | collective-permute-start | bytes 393224 | tf_op jit(solution)/shard_map/ppermute | solution.py:157
  14.0 20.2 %collective-permute-start = (f32[5,4]{1,0:T(8,128)S(1)}, f32[5,4]{1,0:T(8,128)S(1)}, u32[]{:S(2)}, u32[]{:S(2)}) collective-permute-start(f32[5,4]{1,0:T(8,128)S(1)} %get-tuple-element.9), channel_id=1, source_target_pairs={{0,16},{16,32},{32,48},{48,64},{64,80},{80,96},{96,112},{1,17},{17... | collective-permute-start | bytes 248 | tf_op jit(solution)/shard_map/ppermute | solution.py:157
  19.5 20.8 %collective-permute-start.1 = (f32[5,4]{1,0:T(8,128)S(1)}, f32[5,4]{1,0:T(8,128)S(1)}, u32[]{:S(2)}, u32[]{:S(2)}) collective-permute-start(f32[5,4]{1,0:T(8,128)S(1)} %get-tuple-element.10), channel_id=1, source_target_pairs={{16,0},{32,16},{48,32},{64,48},{80,64},{96,80},{112,96},{17,1},{33... | collective-permute-start | bytes 248 | tf_op jit(solution)/shard_map/ppermute | solution.py:157
  41.1 17.7 %all-to-all-start = ((f32[16,8,512]{2,1,0:T(8,128)}), f32[16,8,512]{2,1,0:T(8,128)S(1)}, u32[]{:S(2)}, u32[]{:S(2)}) async-start(f32[16,8,512]{2,1,0:T(8,128)} %pad_maximum_fusion), calls=%async_computation | async-start | bytes 524288 | tf_op jit(solution)/shard_map/all_to_all | solution.py:173

commit v3 on v2

v3 whole, which is shorter than its diff:
```python
import jax
import jax.numpy as jnp
from jax import lax
from jax.experimental import pallas as pl
from jax.experimental.pallas import tpu as pltpu
from jax.sharding import PartitionSpec as P

LANES = 128
REACH = 2
HALO = 2 * REACH


def diffused(far_up, up, here, down, far_down, factor):
    return here + factor * (16.0 * (up + down) - (far_up + far_down) - 30.0 * here)


def partly_shifted(row, shift, weight):
    part = shift & (LANES - 1)
    lane = lax.broadcasted_iota(jnp.int32, row[0].shape, 1)
    own_first, own_behind = lane >= part, lane > part
    first = [pltpu.roll(line, part, 1) for line in row]
    behind = [pltpu.roll(line, (part + 1) & (LANES - 1), 1) for line in row]
    first = [pltpu.roll(first[-1], 1, 0)] + first
    behind = [pltpu.roll(behind[-1], 1, 0)] + behind
    return [
        (1.0 - weight) * jnp.where(own_first, first[c + 1], first[c])
        + weight * jnp.where(own_behind, behind[c + 1], behind[c])
        for c in range(len(row))
    ]


def keep(ref, i, row):
    blocks = row[0].shape[0]
    for c, line in enumerate(row):
        ref[i, c, pl.ds(0, blocks)] = line
        ref[i, c, pl.ds(blocks, blocks)] = line


def moved(ref, i, shift):
    per, blocks = ref.shape[1], ref.shape[2] // 2
    lines = shift // LANES
    some, whole = lines % per, lines // per
    row = []
    for c in range(per):
        wraps = (c < some).astype(jnp.int32)
        row.append(ref[i, c - some + wraps * per, pl.ds(blocks - whole - wraps, blocks)])
    return row


def in_groups(count, size, body):
    size = next(s for s in range(size, 0, -1) if count % s == 0)

    def group(t, carry):
        body(t * size, size)
        return carry

    lax.fori_loop(0, count // size, group, 0)


def advance_kernel(offsets, fractions, factors, main, out, grid, once, twice):
    rows, per = out.shape[1], grid.shape[1]

    def relay(at, row):
        line = main[:, row, :]
        for c in range(per):
            grid[at, c] = line[:, c * LANES : (c + 1) * LANES]

    def relay_group(start, size):
        for u in range(size):
            relay(HALO + start + u, start + u)

    def first_step(start, size):
        for u in range(size):
            i = start + u
            at = REACH + i
            row = [diffused(*[grid[i + j, c] for j in range(2 * REACH + 1)], factors[at]) for c in range(per)]
            keep(once, i, partly_shifted(row, offsets[0, at], fractions[0, at]))

    def second_step(start, size):
        lines = [moved(once, start + j, offsets[0, REACH + start + j]) for j in range(size + 2 * REACH)]
        for u in range(size):
            i = start + u
            at = HALO + i
            row = [diffused(*[lines[u + j][c] for j in range(2 * REACH + 1)], factors[at]) for c in range(per)]
            keep(twice, i, partly_shifted(row, offsets[1, at], fractions[1, at]))

    def write(start, size):
        for u in range(size):
            i = start + u
            out[:, i, :] = jnp.concatenate(moved(twice, i, offsets[1, HALO + i]), axis=1)

    for r in range(HALO):
        relay(r, rows + r)
        relay(HALO + rows + r, rows + HALO + r)
    in_groups(rows, 4, relay_group)
    in_groups(rows + 2 * REACH, 4, first_step)
    in_groups(rows, 4, second_step)
    in_groups(rows, 4, write)


def advance(offsets, fractions, factors, main):
    members, extended, width = main.shape
    rows, per = extended - 2 * HALO, width // LANES
    smem = pl.BlockSpec(memory_space=pltpu.SMEM)
    vmem = pl.BlockSpec(memory_space=pltpu.VMEM)
    return pl.pallas_call(
        advance_kernel,
        out_shape=jax.ShapeDtypeStruct((members, rows, width), jnp.float32),
        in_specs=[smem] * 3 + [vmem],
        out_specs=vmem,
        scratch_shapes=[
            pltpu.VMEM((extended, per, members, LANES), jnp.float32),
            pltpu.VMEM((rows + 2 * REACH, per, 2 * members, LANES), jnp.float32),
            pltpu.VMEM((rows, per, 2 * members, LANES), jnp.float32),
        ],
        compiler_params=pltpu.CompilerParams(vmem_limit_bytes=16 << 20),
    )(offsets, fractions, factors, main)


def from_neighbours(first, last, axis):
    peers = lax.axis_size(axis)
    forth = [(i, i + 1) for i in range(peers - 1)]
    back = [(j, i) for i, j in forth]
    return lax.ppermute(last, axis, forth), lax.ppermute(first, axis, back)


def shards(fields, offsets, fractions, coefs):
    shape = fields.shape
    rows, width = shape[2], shape[3]
    steps = offsets.shape[0]
    blocks = fields.reshape(-1, rows, width)
    before, after = from_neighbours(blocks[:, :HALO], blocks[:, rows - HALO :], "rad")
    main = jnp.concatenate([blocks, before, after], axis=1)

    table = jnp.concatenate([offsets.astype(jnp.float32), fractions, coefs[None] / 12.0])
    table = lax.all_gather(table, "rad", axis=1, tiled=True)
    table = jnp.pad(table, ((0, 0), (HALO, HALO)))
    table = lax.dynamic_slice_in_dim(table, lax.axis_index("rad") * rows, rows + 2 * HALO, axis=1)

    main = lax.all_to_all(main, "azi", 0, 0, tiled=True)
    done = advance(table[:steps].astype(jnp.int32), table[steps : 2 * steps], table[2 * steps], main)
    return lax.all_to_all(done, "azi", 0, 0, tiled=True).reshape(shape)


def solution(mesh):
    placed = (P(None, None, "rad", "azi"), P(None, "rad"), P(None, "rad"), P("rad"))
    return jax.shard_map(
        shards, mesh=mesh, in_specs=placed, out_specs=P(None, None, "rad", "azi"), check_vma=False
    )
```

time: 96.2 us -> 130 us (1.35)
  blocking collectives: 32.4 us -> 92.7 us
  waiting for transfers between devices: 19.5 us -> 5.92 us
  starting transfers between devices: 26 us -> 13.9 us
  Pallas kernels: 14.4 us -> 11.1 us
  other arithmetic: 0.86 us -> 3.36 us
    all_gather x0 -> x1, blocking collectives: none -> 54.2 us  [shards(): table = lax.all_gather(table, 'rad', axis=1, tiled=True)]
    ppermute x4 -> x2, waiting for transfers between devices: 19.5 us -> 5.92 us  [from_neighbours(): return (lax.ppermute(last, axis, forth), lax.ppermute(first, axis, back))]
    all_to_all x2 -> x1, starting transfers between devices: 13.6 us -> 7.13 us  [shards(): main = lax.all_to_all(main, 'azi', 0, 0, tiled=True)]
    all_to_all x1, blocking collectives: 32.4 us -> 38.5 us  [shards(): return lax.all_to_all(done, 'azi', 0, 0, tiled=True).reshape(shape)]
    ppermute x4 -> x2, starting transfers between devices: 12.4 us -> 6.78 us  [from_neighbours(): return (lax.ppermute(last, axis, forth), lax.ppermute(first, axis, back))]
    pallas_call x2 -> x1, Pallas kernels: 14.4 us -> 11.1 us  [advance(): pl.pallas_call(advance_kernel, out_shape=jax.ShapeDtypeStruct((members, r...]
    concatenate x3 -> x1, other arithmetic: 0.85 us -> 3.33 us  [shards(): main = jnp.concatenate([blocks, before, after], axis=1)]
  transfers between devices with their start and end apart: 6 -> 3, of which waited for: 2 -> 2; matrix products, arithmetic and copies ran while one was open for 2% -> 0% of each run, Pallas kernels for 12% -> 0%
where the time goes in v3:
time: 130 us
  blocking collectives  92.7 us (71%)
  starting transfers between devices  13.9 us (11%)
  Pallas kernels  11.1 us (9%)
  waiting for transfers between devices  5.92 us (5%)
  other arithmetic  3.36 us (3%)
  local copies, waits for them, and re-layouts  2.57 us (2%)
    all_gather x1, blocking collectives, shards(): table = lax.all_gather(table, 'rad', axis=1, tiled=True)  54.2 us
    all_to_all x1, blocking collectives, shards(): return lax.all_to_all(done, 'azi', 0, 0, tiled=True).reshape(shape)  38.5 us
    pallas_call x1, Pallas kernels, advance(): pl.pallas_call(advance_kernel, out_shape=jax.ShapeDtypeStruct((members, r...  11.1 us
    all_to_all x1, starting transfers between devices, shards(): main = lax.all_to_all(main, 'azi', 0, 0, tiled=True)  7.13 us
    ppermute x2, starting transfers between devices, from_neighbours(): return (lax.ppermute(last, axis, forth), lax.ppermute(first, axis, back))  6.78 us
    ppermute x2, waiting for transfers between devices, from_neighbours(): return (lax.ppermute(last, axis, forth), lax.ppermute(first, axis, back))  5.92 us
    concatenate x1, other arithmetic, shards(): main = jnp.concatenate([blocks, before, after], axis=1)  3.33 us
  transfers between devices with their start and end apart: 3, of which 2 were waited for; matrix products, arithmetic and copies ran while one was open for 0% of the time, Pallas kernels for 0%

profile of v3, /device:TPU:1, one launch (start us, length us, event | category | flops | bytes accessed | tf_op | source)
XLA Modules:
  0.0 129.7 jit_solution(296011592446770291)
XLA Ops:
  0.0 1.1 fusion
  1.1 5.5 %collective-permute-start = (f32[16,4,512]{2,1,0:T(4,128)S(1)}, f32[16,4,512]{2,1,0:T(4,128)S(1)}, u32[]{:S(2)}, u32[]{:S(2)}) collective-permute-start(f32[16,4,512]{2,1,0:T(4,128)S(1)} %get-tuple-element.5), channel_id=1, source_target_pairs={{0,16},{16,32},{32,48},{48,64},{64,80},{80,96},{96,112},{1,17},{17... | collective-permute-start | bytes 393224 | tf_op jit(solution)/shard_map/ppermute | solution.py:124
  6.6 1.3 collective-permute-start.1
  7.9 0.8 collective-permute-done
  8.7 5.1 %collective-permute-done.1 = f32[16,4,512]{2,1,0:T(4,128)S(1)} collective-permute-done((f32[16,4,512]{2,1,0:T(4,128)S(1)}, f32[16,4,512]{2,1,0:T(4,128)S(1)}, u32[]{:S(2)}, u32[]{:S(2)}) %collective-permute-start.1) | collective-permute-done | bytes 131104 | tf_op jit(solution)/shard_map/ppermute | solution.py:124
  13.8 3.3 %pad_maximum_fusion = f32[16,72,512]{2,1,0:T(8,128)} fusion(f32[16,4,512]{2,1,0:T(4,128)S(1)} %collective-permute-done.1, f32[16,4,512]{2,1,0:T(4,128)S(1)} %collective-permute-done, f32[16,64,512]{2,1,0:T(8,128)} %bitcast.15), kind=kLoop, calls=%fused_computation | loop fusion | flops 1179648 | bytes 4718592 | tf_op jit(solution)/shard_map/concatenate | solution.py:133
  17.1 0.0 copy-start
  17.1 0.0 copy-start.2
  17.1 0.0 copy-start.1
  17.1 7.1 %all-to-all-start = ((f32[16,72,512]{2,1,0:T(8,128)}), f32[16,72,512]{2,1,0:T(8,128)S(1)}, u32[]{:S(2)}, u32[]{:S(2)}) async-start(f32[16,72,512]{2,1,0:T(8,128)} %pad_maximum_fusion), calls=%async_computation | async-start | bytes 4718592 | tf_op jit(solution)/shard_map/all_to_all | solution.py:140
  24.3 0.0 copy-done
  24.3 0.0 copy-done.2
  24.3 0.0 copy-done.1
  24.3 54.2 %all-gather = f32[8,64,5]{1,2,0:T(8,128)S(1)} all-gather(f32[1,64,5]{1,2,0:T(8,128)S(1)} %maximum_bitcast_fusion), channel_id=1, replica_groups=mesh['rad'=8,'azi'=16] {'rad'}, dimensions={0}, use_global_device_ids=true | all-gather | bytes 11520 | tf_op jit(solution)/shard_map/all_gather | solution.py:136
  78.6 0.1 reshape.10
  78.6 0.1 pad_dynamic-slice_fusion
  78.7 0.0 all-to-all-done.main
  78.7 11.1 %shard_map.46 = f32[16,64,512]{2,1,0:T(8,128)S(1)} custom-call(s32[2,72]{1,0:T(2,128)S(1)} %get-tuple-element.8.offsets, f32[2,72]{1,0:T(2,128)S(1)} %get-tuple-element.7.fractions, f32[72]{0:T(128)S(1)} %slice_bitcast_fusion.factors, f32[16,72,512]{2,1,0:T(8,128)S(1)} %all-to-all-done.main), custom_call_target="tpu_custom_call" | custom-call | tf_op jit(solution)/shard_map/pallas_call | solution.py:106
  89.9 38.5 %all_to_all.10 = f32[16,64,512]{2,1,0:T(8,128)S(1)} all-to-all(f32[16,64,512]{2,1,0:T(8,128)S(1)} %shard_map.46), channel_id=1, replica_groups=mesh['rad'=8,'azi'=16] {'azi'}, dimensions={0} | all-to-all | bytes 4194304 | tf_op jit(solution)/shard_map/all_to_all | solution.py:142
  128.4 1.3 %copy.8 = f32[8,2,64,512]{3,2,1,0:T(8,128)} copy(f32[8,2,64,512]{3,2,1,0:T(8,128)S(1)} %bitcast.13) | data formatting | bytes 4194304
  (6 shorter events, 0.0 us)
Async XLA Ops:
  1.1 7.6 %collective-permute-start = (f32[16,4,512]{2,1,0:T(4,128)S(1)}, f32[16,4,512]{2,1,0:T(4,128)S(1)}, u32[]{:S(2)}, u32[]{:S(2)}) collective-permute-start(f32[16,4,512]{2,1,0:T(4,128)S(1)} %get-tuple-element.5), channel_id=1, source_target_pairs={{0,16},{16,32},{32,48},{48,64},{64,80},{80,96},{96,112},{1,17},{17... | collective-permute-start | bytes 393224 | tf_op jit(solution)/shard_map/ppermute | solution.py:124
  6.6 7.2 %collective-permute-start.1 = (f32[16,4,512]{2,1,0:T(4,128)S(1)}, f32[16,4,512]{2,1,0:T(4,128)S(1)}, u32[]{:S(2)}, u32[]{:S(2)}) collective-permute-start(f32[16,4,512]{2,1,0:T(4,128)S(1)} %get-tuple-element.6), channel_id=1, source_target_pairs={{16,0},{32,16},{48,32},{64,48},{80,64},{96,80},{112,96},{17,1},{33... | collective-permute-start | bytes 393224 | tf_op jit(solution)/shard_map/ppermute | solution.py:124
  17.1 7.1 %copy-start = (s32[2,64]{1,0:T(2,128)S(1)}, s32[2,64]{1,0:T(2,128)}, u32[]{:S(2)}) copy-start(s32[2,64]{1,0:T(2,128)} %param.5) | copy-start | bytes 1540
  17.1 7.2 %copy-start.2 = (f32[64]{0:T(128)S(1)}, f32[64]{0:T(128)}, u32[]{:S(2)}) copy-start(f32[64]{0:T(128)} %param.7) | copy-start | bytes 772
  17.1 7.2 %copy-start.1 = (f32[2,64]{1,0:T(2,128)S(1)}, f32[2,64]{1,0:T(2,128)}, u32[]{:S(2)}) copy-start(f32[2,64]{1,0:T(2,128)} %param.6) | copy-start | bytes 1540
  17.1 61.6 %all-to-all-start = ((f32[16,72,512]{2,1,0:T(8,128)}), f32[16,72,512]{2,1,0:T(8,128)S(1)}, u32[]{:S(2)}, u32[]{:S(2)}) async-start(f32[16,72,512]{2,1,0:T(8,128)} %pad_maximum_fusion), calls=%async_computation | async-start | bytes 4718592 | tf_op jit(solution)/shard_map/all_to_all | solution.py:140

commit v4 on v2

--- a/solution.py
+++ b/solution.py
@@ -39,8 +39,8 @@
 
 def moved(ref, i, shift):
     per, blocks = ref.shape[1], ref.shape[2] // 2
-    lines = shift // LANES
-    some, whole = lines % per, lines // per
+    lines = shift >> 7
+    some, whole = lines & (per - 1), lines >> (per.bit_length() - 1)
     row = []
     for c in range(per):
         wraps = (c < some).astype(jnp.int32)
@@ -96,7 +96,7 @@
         grid[at, c] = line[:, c * LANES : (c + 1) * LANES]
 
 
-def inner_kernel(offsets, fractions, factors, main, out, grid, once, twice, laid, sem):
+def inner_kernel(offsets, fractions, factors, main, out, grid, once, twice, laid, sems):
     rows = main.shape[1]
 
     def relay(start, size):
@@ -105,13 +105,18 @@
 
     in_groups(rows, 4, relay)
     two_steps(offsets, fractions, factors, 0, grid, once, twice, 0)
-    write(offsets, HALO, twice, 0, rows - 2 * HALO, laid, HALO)
-    copy = pltpu.make_async_copy(laid, out, sem)
-    copy.start()
-    copy.wait()
-
-
-def edge_kernel(offsets, fractions, factors, halo, main, given, out, grid, once, twice, laid, sems):
+    copies = []
+    for tile in range(rows // TILE):
+        lo, hi = max(tile * TILE, HALO), min((tile + 1) * TILE, rows - HALO)
+        write(offsets, lo, twice, lo - HALO, hi - lo, laid, lo)
+        here = pl.ds(tile * TILE, TILE)
+        copies.append(pltpu.make_async_copy(laid.at[:, here], out.at[:, here], sems.at[tile]))
+        copies[-1].start()
+    for copy in copies:
+        copy.wait()
+
+
+def edge_kernel(offsets, fractions, factors, before, after, main, given, out, grid, once, twice, laid, sems):
     rows = main.shape[1]
     inside = rows - 2 * HALO
     near = [pl.ds(0, TILE), pl.ds(rows - TILE, TILE)]
@@ -122,7 +127,7 @@
     for side in range(2):
         base = side * (inside + HALO)
         for r in range(HALO):
-            load(grid, r + side * 2 * HALO, halo, side * HALO + r)
+            load(grid, r + side * 2 * HALO, (before, after)[side], r)
         for r in range(2 * HALO):
             load(grid, r + (1 - side) * HALO, main, r + side * inside)
         two_steps(offsets, fractions, factors, base, grid, once, twice, side * HALO)
@@ -165,12 +170,11 @@
     factors = coefs / 12.0
 
     main = lax.all_to_all(blocks, "azi", 0, 0, tiled=True)
-
-    packed = jnp.concatenate([offsets.astype(jnp.float32), fractions, factors[None]])
-    before, after = from_neighbours(packed[:, :HALO], packed[:, rows - HALO :], "rad")
-    packed = jnp.concatenate([before, packed, after], axis=1)
-    halo = jnp.concatenate(from_neighbours(blocks[:, :HALO], blocks[:, rows - HALO :], "rad"), axis=1)
-    halo = lax.all_to_all(halo, "azi", 0, 0, tiled=True)
+    halo = from_neighbours(main[:, :HALO], main[:, rows - HALO :], "rad")
+
+    table = jnp.concatenate([offsets.astype(jnp.float32), fractions, factors[None]])
+    before, after = from_neighbours(table[:, :HALO], table[:, rows - HALO :], "rad")
+    table = jnp.concatenate([before, table, after], axis=1)
 
     members, per = blocks.shape[0], width // LANES
 
@@ -188,14 +192,14 @@
         (),
         main.shape,
         [single(rows), double(rows - 2 * REACH), double(inside), main.shape],
-        pltpu.SemaphoreType.DMA,
+        pltpu.SemaphoreType.DMA((rows // TILE,)),
         16,
     )
-    tables = (packed[:steps].astype(jnp.int32), packed[steps : 2 * steps], packed[2 * steps])
+    tables = (table[:steps].astype(jnp.int32), table[steps : 2 * steps], table[2 * steps])
     done = call(
         edge_kernel,
         tables,
-        (halo, main),
+        (*halo, main),
         (done,),
         main.shape,
         [single(3 * HALO), double(HALO + 2 * REACH), double(2 * HALO), (2, members, TILE, width)],

time: 96.2 us -> 89.8 us (0.933)
  starting transfers between devices: 26 us -> 19.5 us
  waiting for transfers between devices: 19.5 us -> 22.1 us
  Pallas kernels: 14.4 us -> 12 us
  blocking collectives: 32.4 us -> 33.5 us
  local copies, waits for them, and re-layouts: 2.49 us -> 1.46 us
    all_to_all x1 -> x0, starting transfers between devices: 6.5 us -> none  [shards(): halo = lax.all_to_all(halo, 'azi', 0, 0, tiled=True)]
    pallas_call x2, Pallas kernels: 14.4 us -> 12 us  [call(): pl.pallas_call(kernel, out_shape=pltpu.HBM(out, jnp.float32), in_specs=[s...]
    ppermute x4, waiting for transfers between devices: 19.5 us -> 21.8 us  [from_neighbours(): return (lax.ppermute(last, axis, forth), lax.ppermute(first, axis, back))]
    all_to_all x1, blocking collectives: 32.4 us -> 33.5 us  [shards(): return lax.all_to_all(done, 'azi', 0, 0, tiled=True).reshape(shape)]
    slice x2, local copies, waits for them, and re-layouts: 1.15 us -> 0.12 us  [the longest x1 0.07 us: shards(): table[:, rows - HALO:]]
  transfers between devices with their start and end apart: 6 -> 5, of which waited for: 2 -> 3; matrix products, arithmetic and copies ran while one was open for 2% -> 0% of each run, Pallas kernels for 12% -> 10%
where the time goes in v4:
time: 89.8 us; the launch traced here: 88.8 us
  blocking collectives  33.5 us (37%)
  waiting for transfers between devices  22.1 us (25%)
  starting transfers between devices  19.5 us (22%)
  Pallas kernels  12 us (13%)
  local copies, waits for them, and re-layouts  1.46 us (2%)
    all_to_all x1, blocking collectives, shards(): return lax.all_to_all(done, 'azi', 0, 0, tiled=True).reshape(shape)  33.5 us
    ppermute x4, waiting for transfers between devices, from_neighbours(): return (lax.ppermute(last, axis, forth), lax.ppermute(first, axis, back))  21.8 us
    ppermute x4, starting transfers between devices, from_neighbours(): return (lax.ppermute(last, axis, forth), lax.ppermute(first, axis, back))  12.4 us
    pallas_call x2, Pallas kernels, call(): pl.pallas_call(kernel, out_shape=pltpu.HBM(out, jnp.float32), in_specs=[s...  12 us
    all_to_all x1, starting transfers between devices, shards(): main = lax.all_to_all(blocks, 'azi', 0, 0, tiled=True)  7.06 us
  transfers between devices with their start and end apart: 5, of which 3 were waited for; matrix products, arithmetic and copies ran while one was open for 0% of the time, Pallas kernels for 10%

profile of v4, /device:TPU:1, one launch (start us, length us, event | category | flops | bytes accessed | tf_op | source)
XLA Modules:
  0.0 88.8 jit_solution(62899907599966145)
XLA Ops:
  0.0 0.0 copy-start.1
  0.0 0.0 copy-start.2
  0.0 0.0 copy-start
  0.0 7.1 %all-to-all-start = ((f32[16,64,512]{2,1,0:T(8,128)}), f32[16,64,512]{2,1,0:T(8,128)S(1)}, u32[]{:S(2)}, u32[]{:S(2)}) async-start(f32[16,64,512]{2,1,0:T(8,128)} %bitcast.7), calls=%async_computation | async-start | bytes 4194304 | tf_op jit(solution)/shard_map/all_to_all | solution.py:172
  7.1 0.0 copy-done.1
  7.1 0.0 copy-done.2
  7.1 0.0 copy-done
  7.1 0.1 fusion.3
  7.2 4.4 %collective-permute-start = (f32[5,4]{1,0:T(8,128)S(1)}, f32[5,4]{1,0:T(8,128)S(1)}, u32[]{:S(2)}, u32[]{:S(2)}) collective-permute-start(f32[5,4]{1,0:T(8,128)S(1)} %get-tuple-element.9), channel_id=1, source_target_pairs={{0,16},{16,32},{32,48},{48,64},{64,80},{80,96},{96,112},{1,17},{17... | collective-permute-start | bytes 248 | tf_op jit(solution)/shard_map/ppermute | solution.py:162
  11.6 1.3 %collective-permute-start.1 = (f32[5,4]{1,0:T(8,128)S(1)}, f32[5,4]{1,0:T(8,128)S(1)}, u32[]{:S(2)}, u32[]{:S(2)}) collective-permute-start(f32[5,4]{1,0:T(8,128)S(1)} %get-tuple-element.10), channel_id=1, source_target_pairs={{16,0},{32,16},{48,32},{64,48},{80,64},{96,80},{112,96},{17,1},{33... | collective-permute-start | bytes 248 | tf_op jit(solution)/shard_map/ppermute | solution.py:162
  12.9 18.5 %collective-permute-done = f32[5,4]{1,0:T(8,128)S(1)} collective-permute-done((f32[5,4]{1,0:T(8,128)S(1)}, f32[5,4]{1,0:T(8,128)S(1)}, u32[]{:S(2)}, u32[]{:S(2)}) %collective-permute-start) | collective-permute-done | bytes 112 | tf_op jit(solution)/shard_map/ppermute | solution.py:162
  31.4 3.3 %collective-permute-done.1 = f32[5,4]{1,0:T(8,128)S(1)} collective-permute-done((f32[5,4]{1,0:T(8,128)S(1)}, f32[5,4]{1,0:T(8,128)S(1)}, u32[]{:S(2)}, u32[]{:S(2)}) %collective-permute-start.1) | collective-permute-done | bytes 112 | tf_op jit(solution)/shard_map/ppermute | solution.py:162
  34.7 0.1 pad_maximum_fusion.1
  34.7 0.3 all-to-all-done.main
  35.1 0.1 fusion.1
  35.1 1.3 %collective-permute-start.3 = (f32[16,4,512]{2,1,0:T(4,128)S(1)}, f32[16,4,512]{2,1,0:T(4,128)S(1)}, u32[]{:S(2)}, u32[]{:S(2)}) collective-permute-start(f32[16,4,512]{2,1,0:T(4,128)S(1)} %get-tuple-element.5), channel_id=1, source_target_pairs={{16,0},{32,16},{48,32},{64,48},{80,64},{96,80},{112,96},{17,1},{33... | collective-permute-start | bytes 393224 | tf_op jit(solution)/shard_map/ppermute | solution.py:162
  36.4 5.5 %collective-permute-start.2 = (f32[16,4,512]{2,1,0:T(4,128)S(1)}, f32[16,4,512]{2,1,0:T(4,128)S(1)}, u32[]{:S(2)}, u32[]{:S(2)}) collective-permute-start(f32[16,4,512]{2,1,0:T(4,128)S(1)} %get-tuple-element.6), channel_id=1, source_target_pairs={{0,16},{16,32},{32,48},{48,64},{64,80},{80,96},{96,112},{1,17},{17... | collective-permute-start | bytes 393224 | tf_op jit(solution)/shard_map/ppermute | solution.py:162
  41.9 8.9 %shard_map.46.given = f32[16,64,512]{2,1,0:T(8,128)} custom-call(s32[2,64]{1,0:T(2,128)S(1)} %copy-done.1, f32[2,64]{1,0:T(2,128)S(1)} %copy-done, f32[64]{0:T(128)S(1)} %get-tuple-element.11.factors, f32[16,64,512]{2,1,0:T(8,128)S(1)} %all-to-all-done.main), custom_call_target="tpu_custom_call" | custom-call | tf_op jit(solution)/shard_map/pallas_call | solution.py:147
  50.9 0.0 collective-permute-done.3.after
  50.9 0.0 collective-permute-done.2.before
  50.9 3.1 %shard_map.47 = f32[16,64,512]{2,1,0:T(8,128)} custom-call(s32[2,72]{1,0:T(2,128)S(1)} %get-tuple-element.8.offsets, f32[2,72]{1,0:T(2,128)S(1)} %get-tuple-element.7.fractions, f32[72]{0:T(128)S(1)} %slice_bitcast_fusion.factors, f32[16,4,512]{2,1,0:T(4,128)S(1)} %collective-permute-done.2.before, ...), custom_call_target="tpu_custom_call", output_to_operand_aliasing={{}: (6, {})} | custom-call | tf_op jit(solution)/shard_map/pallas_call | solution.py:147
  54.0 33.5 %all_to_all.10 = f32[16,64,512]{2,1,0:T(8,128)S(1)} all-to-all(f32[16,64,512]{2,1,0:T(8,128)} %shard_map.47), channel_id=1, replica_groups=mesh['rad'=8,'azi'=16] {'azi'}, dimensions={0} | all-to-all | bytes 4194304 | tf_op jit(solution)/shard_map/all_to_all | solution.py:209
  87.5 1.3 %copy.8 = f32[8,2,64,512]{3,2,1,0:T(8,128)} copy(f32[8,2,64,512]{3,2,1,0:T(8,128)S(1)} %bitcast.6) | data formatting | bytes 4194304
  (5 shorter events, 0.0 us)
Async XLA Ops:
  0.0 7.1 %copy-start.1 = (s32[2,64]{1,0:T(2,128)S(1)}, s32[2,64]{1,0:T(2,128)}, u32[]{:S(2)}) copy-start(s32[2,64]{1,0:T(2,128)} %offsets.1) | copy-start | bytes 1540
  0.0 7.1 %copy-start.2 = (f32[64]{0:T(128)S(1)}, f32[64]{0:T(128)}, u32[]{:S(2)}) copy-start(f32[64]{0:T(128)} %param.7) | copy-start | bytes 772
  0.0 7.1 %copy-start = (f32[2,64]{1,0:T(2,128)S(1)}, f32[2,64]{1,0:T(2,128)}, u32[]{:S(2)}) copy-start(f32[2,64]{1,0:T(2,128)} %fractions.1) | copy-start | bytes 1540
  0.0 35.0 %all-to-all-start = ((f32[16,64,512]{2,1,0:T(8,128)}), f32[16,64,512]{2,1,0:T(8,128)S(1)}, u32[]{:S(2)}, u32[]{:S(2)}) async-start(f32[16,64,512]{2,1,0:T(8,128)} %bitcast.7), calls=%async_computation | async-start | bytes 4194304 | tf_op jit(solution)/shard_map/all_to_all | solution.py:172
  7.2 24.2 %collective-permute-start = (f32[5,4]{1,0:T(8,128)S(1)}, f32[5,4]{1,0:T(8,128)S(1)}, u32[]{:S(2)}, u32[]{:S(2)}) collective-permute-start(f32[5,4]{1,0:T(8,128)S(1)} %get-tuple-element.9), channel_id=1, source_target_pairs={{0,16},{16,32},{32,48},{48,64},{64,80},{80,96},{96,112},{1,17},{17... | collective-permute-start | bytes 248 | tf_op jit(solution)/shard_map/ppermute | solution.py:162
  11.6 23.1 %collective-permute-start.1 = (f32[5,4]{1,0:T(8,128)S(1)}, f32[5,4]{1,0:T(8,128)S(1)}, u32[]{:S(2)}, u32[]{:S(2)}) collective-permute-start(f32[5,4]{1,0:T(8,128)S(1)} %get-tuple-element.10), channel_id=1, source_target_pairs={{16,0},{32,16},{48,32},{64,48},{80,64},{96,80},{112,96},{17,1},{33... | collective-permute-start | bytes 248 | tf_op jit(solution)/shard_map/ppermute | solution.py:162
  35.1 15.8 %collective-permute-start.3 = (f32[16,4,512]{2,1,0:T(4,128)S(1)}, f32[16,4,512]{2,1,0:T(4,128)S(1)}, u32[]{:S(2)}, u32[]{:S(2)}) collective-permute-start(f32[16,4,512]{2,1,0:T(4,128)S(1)} %get-tuple-element.5), channel_id=1, source_target_pairs={{16,0},{32,16},{48,32},{64,48},{80,64},{96,80},{112,96},{17,1},{33... | collective-permute-start | bytes 393224 | tf_op jit(solution)/shard_map/ppermute | solution.py:162
  36.4 14.5 %collective-permute-start.2 = (f32[16,4,512]{2,1,0:T(4,128)S(1)}, f32[16,4,512]{2,1,0:T(4,128)S(1)}, u32[]{:S(2)}, u32[]{:S(2)}) collective-permute-start(f32[16,4,512]{2,1,0:T(4,128)S(1)} %get-tuple-element.6), channel_id=1, source_target_pairs={{0,16},{16,32},{32,48},{48,64},{64,80},{80,96},{96,112},{1,17},{17... | collective-permute-start | bytes 393224 | tf_op jit(solution)/shard_map/ppermute | solution.py:162

commit v5 on v4

v5 whole, which is shorter than its diff:
```python
import jax
import jax.numpy as jnp
from jax import lax
from jax.experimental import pallas as pl
from jax.experimental.pallas import tpu as pltpu
from jax.sharding import PartitionSpec as P

LANES = 128
TILE = 8
REACH = 2
HALO = 2 * REACH


def diffused(far_up, up, here, down, far_down, factor):
    return here + factor * (16.0 * (up + down) - (far_up + far_down) - 30.0 * here)


def partly_shifted(row, shift, weight):
    part = shift & (LANES - 1)
    lane = lax.broadcasted_iota(jnp.int32, row[0].shape, 1)
    own_first, own_behind = lane >= part, lane > part
    first = [pltpu.roll(line, part, 1) for line in row]
    behind = [pltpu.roll(line, (part + 1) & (LANES - 1), 1) for line in row]
    first = [pltpu.roll(first[-1], 1, 0)] + first
    behind = [pltpu.roll(behind[-1], 1, 0)] + behind
    return [
        (1.0 - weight) * jnp.where(own_first, first[c + 1], first[c])
        + weight * jnp.where(own_behind, behind[c + 1], behind[c])
        for c in range(len(row))
    ]


def keep(ref, i, row):
    blocks = row[0].shape[0]
    for c, line in enumerate(row):
        ref[i, c, pl.ds(0, blocks)] = line
        ref[i, c, pl.ds(blocks, blocks)] = line


def moved(ref, i, shift):
    per, blocks = ref.shape[1], ref.shape[2] // 2
    lines = shift >> 7
    some, whole = lines & (per - 1), lines >> (per.bit_length() - 1)
    row = []
    for c in range(per):
        wraps = (c < some).astype(jnp.int32)
        row.append(ref[i, c - some + wraps * per, pl.ds(blocks - whole - wraps, blocks)])
    return row


def in_groups(count, size, body):
    size = next(s for s in range(size, 0, -1) if count % s == 0)

    def group(t, carry):
        body(t * size, size)
        return carry

    lax.fori_loop(0, count // size, group, 0)


def at_once(count, size, body):
    body(0, count)


def two_steps(loop, offset, fraction, factor, grid, once, twice):
    per = grid.shape[1]
    rows = grid.shape[0] - 2 * HALO

    def first_step(start, size):
        for u in range(size):
            i = start + u
            at = i + REACH
            row = [diffused(*[grid[i + j, c] for j in range(2 * REACH + 1)], factor(at)) for c in range(per)]
            keep(once, i, partly_shifted(row, offset(0, at), fraction(0, at)))

    def second_step(start, size):
        lines = [moved(once, start + j, offset(0, start + j + REACH)) for j in range(size + 2 * REACH)]
        for u in range(size):
            i = start + u
            at = i + HALO
            row = [diffused(*[lines[u + j][c] for j in range(2 * REACH + 1)], factor(at)) for c in range(per)]
            keep(twice, i, partly_shifted(row, offset(1, at), fraction(1, at)))

    loop(rows + 2 * REACH, 4, first_step)
    loop(rows, 4, second_step)


def write(loop, offset, twice, start, count, out, to):
    def some(first, size):
        for u in range(size):
            i = first + u
            out[:, to + i, :] = jnp.concatenate(moved(twice, start + i, offset(start + i)), axis=1)

    loop(count, 4, some)


def load(grid, at, source, row):
    line = source[pl.ds(0, grid.shape[2]), row, :]
    for c in range(grid.shape[1]):
        grid[at, c] = line[:, c * LANES : (c + 1) * LANES]


def edge_radii_kernel(main, table, first, last):
    members, rows, _ = main.shape
    first[pl.ds(0, members)] = main[:, :HALO]
    first[members] = table[0]
    last[pl.ds(0, members)] = main[:, rows - HALO :]
    last[members] = table[1]


def inner_kernel(offsets, fractions, factors, main, out, grid, once, twice, laid, sems):
    rows = main.shape[1]

    def relay(start, size):
        for u in range(size):
            load(grid, start + u, main, start + u)

    in_groups(rows, 4, relay)
    two_steps(
        in_groups,
        lambda step, at: offsets[step, at],
        lambda step, at: fractions[step, at],
        lambda at: factors[at],
        grid,
        once,
        twice,
    )
    copies = []
    for tile in range(rows // TILE):
        lo, hi = max(tile * TILE, HALO), min((tile + 1) * TILE, rows - HALO)
        write(in_groups, lambda i: offsets[1, i + HALO], twice, lo - HALO, hi - lo, laid, lo)
        here = pl.ds(tile * TILE, TILE)
        copies.append(pltpu.make_async_copy(laid.at[:, here], out.at[:, here], sems.at[tile]))
        copies[-1].start()
    for copy in copies:
        copy.wait()


def edge_kernel(offsets, fractions, factors, before, after, main, given, out, grid, once, twice, laid, table, sems):
    members, rows, _ = main.shape
    steps = offsets.shape[0]
    near = [pl.ds(0, TILE), pl.ds(rows - TILE, TILE)]
    tables = [
        pltpu.make_async_copy(halo.at[members, :, pl.ds(0, LANES)], table.at[side], sems.at[side])
        for side, halo in enumerate((before, after))
    ]
    fetches = [pltpu.make_async_copy(given.at[:, near[side]], laid.at[side], sems.at[2 + side]) for side in range(2)]
    for copy in tables + fetches:
        copy.start()

    for side, halo in enumerate((before, after)):
        for r in range(HALO):
            load(grid.at[side], r + side * 2 * HALO, halo, r)
        for r in range(2 * HALO):
            load(grid.at[side], r + (1 - side) * HALO, main, r + side * (rows - 2 * HALO))
    for copy in tables:
        copy.wait()

    stores = []
    for side in range(2):

        def entry(own, column, at, side=side):
            own_row = at - HALO if side == 0 else at + rows - 2 * HALO
            if 0 <= own_row < rows:
                return own(own_row)
            return table[side, own_row + HALO if side == 0 else own_row - rows, column]

        def offset(step, at, entry=entry):
            return entry(lambda r: offsets[step, r], step, at)

        def fraction(step, at, entry=entry):
            return entry(lambda r: fractions[step, r], steps + step, at)

        def factor(at, entry=entry):
            return entry(lambda r: factors[r], 2 * steps, at)

        def whole(step, at, offset=offset):
            return offset(step, at).astype(jnp.int32)

        two_steps(at_once, whole, fraction, factor, grid.at[side], once.at[side], twice.at[side])
        fetches[side].wait()
        write(
            at_once,
            lambda i, whole=whole: whole(1, i + HALO),
            twice.at[side],
            0,
            HALO,
            laid.at[side],
            side * (TILE - HALO),
        )
        stores.append(pltpu.make_async_copy(laid.at[side], out.at[:, near[side]], sems.at[2 + side]))
        stores[-1].start()
    for store in stores:
        store.wait()


SMEM = pl.BlockSpec(memory_space=pltpu.SMEM)
VMEM = pl.BlockSpec(memory_space=pltpu.VMEM)
FAR = pl.BlockSpec(memory_space=pltpu.HBM)


def grant(mebibytes):
    return pltpu.CompilerParams(vmem_limit_bytes=mebibytes << 20)


def edge_radii(main, table):
    members, _, width = main.shape
    side = jax.ShapeDtypeStruct((members + 1, HALO, width), jnp.float32)
    return pl.pallas_call(
        edge_radii_kernel,
        out_shape=[side, side],
        in_specs=[VMEM, VMEM],
        out_specs=[VMEM, VMEM],
        compiler_params=grant(2),
    )(main, table)


def inner(offsets, fractions, factors, main):
    members, rows, width = main.shape
    per = width // LANES
    return pl.pallas_call(
        inner_kernel,
        out_shape=pltpu.HBM(main.shape, jnp.float32),
        in_specs=[SMEM] * 3 + [VMEM],
        out_specs=FAR,
        scratch_shapes=[
            pltpu.VMEM((rows, per, members, LANES), jnp.float32),
            pltpu.VMEM((rows - 2 * REACH, per, 2 * members, LANES), jnp.float32),
            pltpu.VMEM((rows - 2 * HALO, per, 2 * members, LANES), jnp.float32),
            pltpu.VMEM(main.shape, jnp.float32),
            pltpu.SemaphoreType.DMA((rows // TILE,)),
        ],
        compiler_params=grant(16),
    )(offsets, fractions, factors, main)


def edges(offsets, fractions, factors, before, after, main, done):
    members, _, width = main.shape
    per = width // LANES
    return pl.pallas_call(
        edge_kernel,
        out_shape=pltpu.HBM(main.shape, jnp.float32),
        in_specs=[SMEM] * 3 + [VMEM] * 3 + [FAR],
        out_specs=FAR,
        scratch_shapes=[
            pltpu.VMEM((2, 3 * HALO, per, members, LANES), jnp.float32),
            pltpu.VMEM((2, HALO + 2 * REACH, per, 2 * members, LANES), jnp.float32),
            pltpu.VMEM((2, HALO, per, 2 * members, LANES), jnp.float32),
            pltpu.VMEM((2, members, TILE, width), jnp.float32),
            pltpu.SMEM((2, HALO, LANES), jnp.float32),
            pltpu.SemaphoreType.DMA((4,)),
        ],
        input_output_aliases={6: 0},
        compiler_params=grant(6),
    )(offsets, fractions, factors, before, after, main, pltpu.with_memory_space_constraint(done, pltpu.HBM))


def from_neighbours(first, last, axis):
    peers = lax.axis_size(axis)
    forth = [(i, i + 1) for i in range(peers - 1)]
    back = [(j, i) for i, j in forth]
    return lax.ppermute(last, axis, forth), lax.ppermute(first, axis, back)


def shards(fields, offsets, fractions, coefs):
    shape = fields.shape
    rows, width = shape[2], shape[3]
    blocks = fields.reshape(-1, rows, width)
    factors = coefs / 12.0
    main = lax.all_to_all(blocks, "azi", 0, 0, tiled=True)

    table = jnp.concatenate([offsets.astype(jnp.float32), fractions, factors[None]]).T
    table = jnp.stack([table[:HALO], table[rows - HALO :]])
    table = jnp.pad(table, ((0, 0), (0, 0), (0, width - table.shape[2])))

    before, after = from_neighbours(*edge_radii(main, table), "rad")
    done = inner(offsets, fractions, factors, main)
    done = edges(offsets, fractions, factors, before, after, main, done)
    return lax.all_to_all(done, "azi", 0, 0, tiled=True).reshape(shape)


def solution(mesh):
    placed = (P(None, None, "rad", "azi"), P(None, "rad"), P(None, "rad"), P("rad"))
    return jax.shard_map(
        shards, mesh=mesh, in_specs=placed, out_specs=P(None, None, "rad", "azi"), check_vma=False
    )
```

time: 89.8 us -> 89.2 us (level)
  the two profiles are of different devices: /device:TPU:1 before, /device:TPU:32 now
where the time goes in v5:
time: 89.2 us; the launch traced here: 89 us
  blocking collectives  33.2 us (37%)
  waiting for transfers between devices  28.4 us (32%)
  starting transfers between devices  13.9 us (16%)
  Pallas kernels  11.7 us (13%)
  local copies, waits for them, and re-layouts  1.59 us (2%)
    all_to_all x1, blocking collectives, shards(): return lax.all_to_all(done, 'azi', 0, 0, tiled=True).reshape(shape)  33.2 us
    all_to_all x1, waiting for transfers between devices, shards(): main = lax.all_to_all(blocks, 'azi', 0, 0, tiled=True)  28.4 us
    pallas_call x1, Pallas kernels, inner(): pl.pallas_call(inner_kernel, out_shape=pltpu.HBM(main.shape, jnp.float32)...  8.94 us
    ppermute x2, starting transfers between devices, from_neighbours(): return (lax.ppermute(last, axis, forth), lax.ppermute(first, axis, back))  8.25 us
    all_to_all x1, starting transfers between devices, shards(): main = lax.all_to_all(blocks, 'azi', 0, 0, tiled=True)  5.65 us
    pallas_call x1, Pallas kernels, edges(): pl.pallas_call(edge_kernel, out_shape=pltpu.HBM(main.shape, jnp.float32),...  2.7 us
  transfers between devices with their start and end apart: 3, of which 1 were waited for; matrix products, arithmetic and copies ran while one was open for 0% of the time, Pallas kernels for 10%

profile of v5, /device:TPU:32, one launch (start us, length us, event | category | flops | bytes accessed | tf_op | source)
XLA Modules:
  0.0 89.0 jit_solution(7927140223652369623)
XLA Ops:
  0.0 0.0 copy-start
  0.0 0.0 copy-start.2
  0.0 0.0 copy-start.1
  0.0 5.6 %all-to-all-start = ((f32[16,64,512]{2,1,0:T(8,128)}), f32[16,64,512]{2,1,0:T(8,128)S(1)}, u32[]{:S(2)}, u32[]{:S(2)}) async-start(f32[16,64,512]{2,1,0:T(8,128)} %bitcast.9), calls=%async_computation | async-start | bytes 4194304 | tf_op jit(solution)/shard_map/all_to_all | solution.py:270
  5.7 0.0 copy-done
  5.7 0.0 copy-done.2
  5.7 0.0 copy-done.1
  5.7 0.1 fusion.1
  5.8 0.1 copy.6
  5.9 0.1 copy.7
  6.0 28.4 %all-to-all-done.main = f32[16,64,512]{2,1,0:T(8,128)S(1)} async-done(((f32[16,64,512]{2,1,0:T(8,128)}), f32[16,64,512]{2,1,0:T(8,128)S(1)}, u32[]{:S(2)}, u32[]{:S(2)}) %all-to-all-start) | async-done | bytes 2097184 | tf_op jit(solution)/shard_map/all_to_all | solution.py:270
  34.4 4.6 %collective-permute-start = (f32[17,4,512]{2,1,0:T(4,128)S(1)}, f32[17,4,512]{2,1,0:T(4,128)S(1)}, u32[]{:S(2)}, u32[]{:S(2)}) collective-permute-start(f32[17,4,512]{2,1,0:T(4,128)S(1)} %get-tuple-element.7), channel_id=1, source_target_pairs={{0,16},{16,32},{32,48},{48,64},{64,80},{80,96},{96,112},{1,17},{17... | collective-permute-start | bytes 417800 | tf_op jit(solution)/shard_map/ppermute | solution.py:262
  39.1 3.6 %collective-permute-start.1 = (f32[17,4,512]{2,1,0:T(4,128)S(1)}, f32[17,4,512]{2,1,0:T(4,128)S(1)}, u32[]{:S(2)}, u32[]{:S(2)}) collective-permute-start(f32[17,4,512]{2,1,0:T(4,128)S(1)} %get-tuple-element.8), channel_id=1, source_target_pairs={{16,0},{32,16},{48,32},{64,48},{80,64},{96,80},{112,96},{17,1},{33... | collective-permute-start | bytes 417800 | tf_op jit(solution)/shard_map/ppermute | solution.py:262
  42.7 8.9 %shard_map.47.given = f32[16,64,512]{2,1,0:T(8,128)} custom-call(s32[2,64]{1,0:T(2,128)S(1)} %copy-done, f32[2,64]{1,0:T(2,128)S(1)} %copy-done.1, f32[64]{0:T(128)S(1)} %get-tuple-element.12.factors, f32[16,64,512]{2,1,0:T(8,128)S(1)} %all-to-all-done.main), custom_call_target="tpu_custom_call" | custom-call | tf_op jit(solution)/shard_map/pallas_call | solution.py:221
  51.7 0.0 collective-permute-done.before
  51.7 0.0 collective-permute-done.1.after
  51.7 2.7 %shard_map.48 = f32[16,64,512]{2,1,0:T(8,128)} custom-call(s32[2,64]{1,0:T(2,128)S(1)} %copy-done, f32[2,64]{1,0:T(2,128)S(1)} %copy-done.1, f32[64]{0:T(128)S(1)} %get-tuple-element.12.factors, f32[17,4,512]{2,1,0:T(4,128)S(1)} %collective-permute-done.before, f32[17,4,512]{2,1,0:T(4,128)S(1)} %collective-permute-done.1.after, ...), custom_call_target="tpu_custom_call", output_to_operand_aliasing={{}: (6, {})} | custom-call | tf_op jit(solution)/shard_map/pallas_call | solution.py:240
  54.4 33.2 %all_to_all.10 = f32[16,64,512]{2,1,0:T(8,128)S(1)} all-to-all(f32[16,64,512]{2,1,0:T(8,128)} %shard_map.48), channel_id=1, replica_groups=mesh['rad'=8,'azi'=16] {'azi'}, dimensions={0} | all-to-all | bytes 4194304 | tf_op jit(solution)/shard_map/all_to_all | solution.py:279
  87.6 1.3 %copy.10 = f32[8,2,64,512]{3,2,1,0:T(8,128)} copy(f32[8,2,64,512]{3,2,1,0:T(8,128)S(1)} %bitcast.8) | data formatting | bytes 4194304
  (5 shorter events, 0.0 us)
Async XLA Ops:
  0.0 5.7 %copy-start = (s32[2,64]{1,0:T(2,128)S(1)}, s32[2,64]{1,0:T(2,128)}, u32[]{:S(2)}) copy-start(s32[2,64]{1,0:T(2,128)} %offsets.3) | copy-start | bytes 1540
  0.0 5.7 %copy-start.2 = (f32[64]{0:T(128)S(1)}, f32[64]{0:T(128)}, u32[]{:S(2)}) copy-start(f32[64]{0:T(128)} %param.7) | copy-start | bytes 772
  0.0 5.7 %copy-start.1 = (f32[2,64]{1,0:T(2,128)S(1)}, f32[2,64]{1,0:T(2,128)}, u32[]{:S(2)}) copy-start(f32[2,64]{1,0:T(2,128)} %fractions.3) | copy-start | bytes 1540
  0.0 34.4 %all-to-all-start = ((f32[16,64,512]{2,1,0:T(8,128)}), f32[16,64,512]{2,1,0:T(8,128)S(1)}, u32[]{:S(2)}, u32[]{:S(2)}) async-start(f32[16,64,512]{2,1,0:T(8,128)} %bitcast.9), calls=%async_computation | async-start | bytes 4194304 | tf_op jit(solution)/shard_map/all_to_all | solution.py:270
  34.4 17.2 %collective-permute-start = (f32[17,4,512]{2,1,0:T(4,128)S(1)}, f32[17,4,512]{2,1,0:T(4,128)S(1)}, u32[]{:S(2)}, u32[]{:S(2)}) collective-permute-start(f32[17,4,512]{2,1,0:T(4,128)S(1)} %get-tuple-element.7), channel_id=1, source_target_pairs={{0,16},{16,32},{32,48},{48,64},{64,80},{80,96},{96,112},{1,17},{17... | collective-permute-start | bytes 417800 | tf_op jit(solution)/shard_map/ppermute | solution.py:262
  39.1 12.6 %collective-permute-start.1 = (f32[17,4,512]{2,1,0:T(4,128)S(1)}, f32[17,4,512]{2,1,0:T(4,128)S(1)}, u32[]{:S(2)}, u32[]{:S(2)}) collective-permute-start(f32[17,4,512]{2,1,0:T(4,128)S(1)} %get-tuple-element.8), channel_id=1, source_target_pairs={{16,0},{32,16},{48,32},{64,48},{80,64},{96,80},{112,96},{17,1},{33... | collective-permute-start | bytes 417800 | tf_op jit(solution)/shard_map/ppermute | solution.py:262

commit v6 on v5

--- a/solution.py
+++ b/solution.py
@@ -9,6 +9,7 @@
 TILE = 8
 REACH = 2
 HALO = 2 * REACH
+RELAY, FIRST = 16, 60
 
 
 def diffused(far_up, up, here, down, far_down, factor):
@@ -37,15 +38,16 @@
         ref[i, c, pl.ds(blocks, blocks)] = line
 
 
-def moved(ref, i, shift):
+def moved_line(ref, i, shift, c):
     per, blocks = ref.shape[1], ref.shape[2] // 2
     lines = shift >> 7
     some, whole = lines & (per - 1), lines >> (per.bit_length() - 1)
-    row = []
-    for c in range(per):
-        wraps = (c < some).astype(jnp.int32)
-        row.append(ref[i, c - some + wraps * per, pl.ds(blocks - whole - wraps, blocks)])
-    return row
+    wraps = (c < some).astype(jnp.int32)
+    return ref[i, c - some + wraps * per, pl.ds(blocks - whole - wraps, blocks)]
+
+
+def moved(ref, i, shift):
+    return [moved_line(ref, i, shift, c) for c in range(ref.shape[1])]
 
 
 def in_groups(count, size, body):
@@ -58,40 +60,31 @@
     lax.fori_loop(0, count // size, group, 0)
 
 
-def at_once(count, size, body):
-    body(0, count)
-
-
-def two_steps(loop, offset, fraction, factor, grid, once, twice):
+def two_steps(offset, fraction, factor, grid, once, twice):
     per = grid.shape[1]
-    rows = grid.shape[0] - 2 * HALO
+
+    def diffuse(start, size, at, number, line, out):
+        rows = [[] for _ in range(size)]
+        for c in range(per):
+            read = [line(start + j, c) for j in range(size + 2 * REACH)]
+            for u in range(size):
+                rows[u].append(diffused(*read[u : u + 2 * REACH + 1], factor(start + u + at)))
+        for u in range(size):
+            here = start + u + at
+            keep(out, start + u, partly_shifted(rows[u], offset(number, here), fraction(number, here)))
 
     def first_step(start, size):
-        for u in range(size):
-            i = start + u
-            at = i + REACH
-            row = [diffused(*[grid[i + j, c] for j in range(2 * REACH + 1)], factor(at)) for c in range(per)]
-            keep(once, i, partly_shifted(row, offset(0, at), fraction(0, at)))
+        diffuse(start, size, REACH, 0, lambda i, c: grid[i, c], once)
 
     def second_step(start, size):
-        lines = [moved(once, start + j, offset(0, start + j + REACH)) for j in range(size + 2 * REACH)]
-        for u in range(size):
-            i = start + u
-            at = i + HALO
-            row = [diffused(*[lines[u + j][c] for j in range(2 * REACH + 1)], factor(at)) for c in range(per)]
-            keep(twice, i, partly_shifted(row, offset(1, at), fraction(1, at)))
-
-    loop(rows + 2 * REACH, 4, first_step)
-    loop(rows, 4, second_step)
-
-
-def write(loop, offset, twice, start, count, out, to):
-    def some(first, size):
-        for u in range(size):
-            i = first + u
-            out[:, to + i, :] = jnp.concatenate(moved(twice, start + i, offset(start + i)), axis=1)
-
-    loop(count, 4, some)
+        diffuse(start, size, HALO, 1, lambda i, c: moved_line(once, i, offset(0, i + REACH), c), twice)
+
+    return first_step, second_step
+
+
+def write(offset, twice, start, count, out, to):
+    for i in range(count):
+        out[:, to + i, :] = jnp.concatenate(moved(twice, start + i, offset(start + i)), axis=1)
 
 
 def load(grid, at, source, row):
@@ -115,9 +108,7 @@
         for u in range(size):
             load(grid, start + u, main, start + u)
 
-    in_groups(rows, 4, relay)
-    two_steps(
-        in_groups,
+    first_step, second_step = two_steps(
         lambda step, at: offsets[step, at],
         lambda step, at: fractions[step, at],
         lambda at: factors[at],
@@ -125,10 +116,13 @@
         once,
         twice,
     )
+    in_groups(rows, RELAY, relay)
+    in_groups(rows - 2 * REACH, FIRST, first_step)
     copies = []
     for tile in range(rows // TILE):
         lo, hi = max(tile * TILE, HALO), min((tile + 1) * TILE, rows - HALO)
-        write(in_groups, lambda i: offsets[1, i + HALO], twice, lo - HALO, hi - lo, laid, lo)
+        second_step(lo - HALO, hi - lo)
+        write(lambda i: offsets[1, i + HALO], twice, lo - HALO, hi - lo, laid, lo)
         here = pl.ds(tile * TILE, TILE)
         copies.append(pltpu.make_async_copy(laid.at[:, here], out.at[:, here], sems.at[tile]))
         copies[-1].start()
@@ -156,38 +150,35 @@
     for copy in tables:
         copy.wait()
 
+    def side_steps(side):
+        def entry(own, column, at):
+            row = at - HALO if side == 0 else at + rows - 2 * HALO
+            if 0 <= row < rows:
+                return own(row)
+            return table[side, row + HALO if side == 0 else row - rows, column]
+
+        def offset(step, at):
+            return entry(lambda row: offsets[step, row], step, at).astype(jnp.int32)
+
+        def fraction(step, at):
+            return entry(lambda row: fractions[step, row], steps + step, at)
+
+        def factor(at):
+            return entry(lambda row: factors[row], 2 * steps, at)
+
+        first_step, second_step = two_steps(offset, fraction, factor, grid.at[side], once.at[side], twice.at[side])
+        return offset, first_step, second_step
+
+    sides = [side_steps(side) for side in range(2)]
+    for _, first_step, _ in sides:
+        first_step(0, HALO + 2 * REACH)
+    for _, _, second_step in sides:
+        second_step(0, HALO)
+    for fetch in fetches:
+        fetch.wait()
     stores = []
-    for side in range(2):
-
-        def entry(own, column, at, side=side):
-            own_row = at - HALO if side == 0 else at + rows - 2 * HALO
-            if 0 <= own_row < rows:
-                return own(own_row)
-            return table[side, own_row + HALO if side == 0 else own_row - rows, column]
-
-        def offset(step, at, entry=entry):
-            return entry(lambda r: offsets[step, r], step, at)
-
-        def fraction(step, at, entry=entry):
-            return entry(lambda r: fractions[step, r], steps + step, at)
-
-        def factor(at, entry=entry):
-            return entry(lambda r: factors[r], 2 * steps, at)
-
-        def whole(step, at, offset=offset):
-            return offset(step, at).astype(jnp.int32)
-
-        two_steps(at_once, whole, fraction, factor, grid.at[side], once.at[side], twice.at[side])
-        fetches[side].wait()
-        write(
-            at_once,
-            lambda i, whole=whole: whole(1, i + HALO),
-            twice.at[side],
-            0,
-            HALO,
-            laid.at[side],
-            side * (TILE - HALO),
-        )
+    for side, (offset, _, _) in enumerate(sides):
+        write(lambda i, offset=offset: offset(1, i + HALO), twice.at[side], 0, HALO, laid.at[side], side * (TILE - HALO))
         stores.append(pltpu.make_async_copy(laid.at[side], out.at[:, near[side]], sems.at[2 + side]))
         stores[-1].start()
     for store in stores:

time: 89.2 us -> 86.2 us (0.966)
  the two profiles are of different devices: /device:TPU:32 before, /device:TPU:1 now
where the time goes in v6:
time: 86.2 us; the launch traced here: 85.6 us
  blocking collectives  34.9 us (40%)
  waiting for transfers between devices  27.9 us (32%)
  starting transfers between devices  12.7 us (15%)
  Pallas kernels  8.35 us (10%)
  local copies, waits for them, and re-layouts  1.59 us (2%)
    all_to_all x1, blocking collectives, shards(): return lax.all_to_all(done, 'azi', 0, 0, tiled=True).reshape(shape)  34.9 us
    all_to_all x1, waiting for transfers between devices, shards(): main = lax.all_to_all(blocks, 'azi', 0, 0, tiled=True)  27.7 us
    all_to_all x1, starting transfers between devices, shards(): main = lax.all_to_all(blocks, 'azi', 0, 0, tiled=True)  7.06 us
    pallas_call x1, Pallas kernels, inner(): pl.pallas_call(inner_kernel, out_shape=pltpu.HBM(main.shape, jnp.float32)...  5.7 us
    ppermute x2, starting transfers between devices, from_neighbours(): return (lax.ppermute(last, axis, forth), lax.ppermute(first, axis, back))  5.65 us
    pallas_call x1, Pallas kernels, edges(): pl.pallas_call(edge_kernel, out_shape=pltpu.HBM(main.shape, jnp.float32),...  2.63 us
  transfers between devices with their start and end apart: 3, of which 2 were waited for; matrix products, arithmetic and copies ran while one was open for 0% of the time, Pallas kernels for 7%

profile of v6, /device:TPU:1, one launch (start us, length us, event | category | flops | bytes accessed | tf_op | source)
XLA Modules:
  0.0 85.6 jit_solution(6252715372350277155)
XLA Ops:
  0.0 0.0 copy-start
  0.0 0.0 copy-start.2
  0.0 0.0 copy-start.1
  0.0 7.1 %all-to-all-start = ((f32[16,64,512]{2,1,0:T(8,128)}), f32[16,64,512]{2,1,0:T(8,128)S(1)}, u32[]{:S(2)}, u32[]{:S(2)}) async-start(f32[16,64,512]{2,1,0:T(8,128)} %bitcast.9), calls=%async_computation | async-start | bytes 4194304 | tf_op jit(solution)/shard_map/all_to_all | solution.py:261
  7.1 0.0 copy-done
  7.1 0.0 copy-done.2
  7.1 0.0 copy-done.1
  7.1 0.1 fusion.1
  7.2 0.1 copy.6
  7.3 0.1 copy.7
  7.4 27.7 %all-to-all-done.main = f32[16,64,512]{2,1,0:T(8,128)S(1)} async-done(((f32[16,64,512]{2,1,0:T(8,128)}), f32[16,64,512]{2,1,0:T(8,128)S(1)}, u32[]{:S(2)}, u32[]{:S(2)}) %all-to-all-start) | async-done | bytes 2097184 | tf_op jit(solution)/shard_map/all_to_all | solution.py:261
  35.1 4.4 %collective-permute-start = (f32[17,4,512]{2,1,0:T(4,128)S(1)}, f32[17,4,512]{2,1,0:T(4,128)S(1)}, u32[]{:S(2)}, u32[]{:S(2)}) collective-permute-start(f32[17,4,512]{2,1,0:T(4,128)S(1)} %get-tuple-element.7), channel_id=1, source_target_pairs={{0,16},{16,32},{32,48},{48,64},{64,80},{80,96},{96,112},{1,17},{17... | collective-permute-start | bytes 417800 | tf_op jit(solution)/shard_map/ppermute | solution.py:253
  39.5 1.3 %collective-permute-start.1 = (f32[17,4,512]{2,1,0:T(4,128)S(1)}, f32[17,4,512]{2,1,0:T(4,128)S(1)}, u32[]{:S(2)}, u32[]{:S(2)}) collective-permute-start(f32[17,4,512]{2,1,0:T(4,128)S(1)} %get-tuple-element.8), channel_id=1, source_target_pairs={{16,0},{32,16},{48,32},{64,48},{80,64},{96,80},{112,96},{17,1},{33... | collective-permute-start | bytes 417800 | tf_op jit(solution)/shard_map/ppermute | solution.py:253
  40.8 5.7 %shard_map.47.given = f32[16,64,512]{2,1,0:T(8,128)} custom-call(s32[2,64]{1,0:T(2,128)S(1)} %copy-done, f32[2,64]{1,0:T(2,128)S(1)} %copy-done.1, f32[64]{0:T(128)S(1)} %get-tuple-element.12.factors, f32[16,64,512]{2,1,0:T(8,128)S(1)} %all-to-all-done.main), custom_call_target="tpu_custom_call" | custom-call | tf_op jit(solution)/shard_map/pallas_call | solution.py:212
  46.5 0.0 collective-permute-done.before
  46.5 0.3 collective-permute-done.1.after
  46.8 2.6 %shard_map.48 = f32[16,64,512]{2,1,0:T(8,128)} custom-call(s32[2,64]{1,0:T(2,128)S(1)} %copy-done, f32[2,64]{1,0:T(2,128)S(1)} %copy-done.1, f32[64]{0:T(128)S(1)} %get-tuple-element.12.factors, f32[17,4,512]{2,1,0:T(4,128)S(1)} %collective-permute-done.before, f32[17,4,512]{2,1,0:T(4,128)S(1)} %collective-permute-done.1.after, ...), custom_call_target="tpu_custom_call", output_to_operand_aliasing={{}: (6, {})} | custom-call | tf_op jit(solution)/shard_map/pallas_call | solution.py:231
  49.4 34.9 %all_to_all.10 = f32[16,64,512]{2,1,0:T(8,128)S(1)} all-to-all(f32[16,64,512]{2,1,0:T(8,128)} %shard_map.48), channel_id=1, replica_groups=mesh['rad'=8,'azi'=16] {'azi'}, dimensions={0} | all-to-all | bytes 4194304 | tf_op jit(solution)/shard_map/all_to_all | solution.py:270
  84.3 1.3 %copy.10 = f32[8,2,64,512]{3,2,1,0:T(8,128)} copy(f32[8,2,64,512]{3,2,1,0:T(8,128)S(1)} %bitcast.8) | data formatting | bytes 4194304
  (5 shorter events, 0.0 us)
Async XLA Ops:
  0.0 7.1 %copy-start = (s32[2,64]{1,0:T(2,128)S(1)}, s32[2,64]{1,0:T(2,128)}, u32[]{:S(2)}) copy-start(s32[2,64]{1,0:T(2,128)} %offsets.3) | copy-start | bytes 1540
  0.0 7.1 %copy-start.2 = (f32[64]{0:T(128)S(1)}, f32[64]{0:T(128)}, u32[]{:S(2)}) copy-start(f32[64]{0:T(128)} %param.7) | copy-start | bytes 772
  0.0 7.1 %copy-start.1 = (f32[2,64]{1,0:T(2,128)S(1)}, f32[2,64]{1,0:T(2,128)}, u32[]{:S(2)}) copy-start(f32[2,64]{1,0:T(2,128)} %fractions.3) | copy-start | bytes 1540
  0.0 35.0 %all-to-all-start = ((f32[16,64,512]{2,1,0:T(8,128)}), f32[16,64,512]{2,1,0:T(8,128)S(1)}, u32[]{:S(2)}, u32[]{:S(2)}) async-start(f32[16,64,512]{2,1,0:T(8,128)} %bitcast.9), calls=%async_computation | async-start | bytes 4194304 | tf_op jit(solution)/shard_map/all_to_all | solution.py:261
  35.1 11.4 %collective-permute-start = (f32[17,4,512]{2,1,0:T(4,128)S(1)}, f32[17,4,512]{2,1,0:T(4,128)S(1)}, u32[]{:S(2)}, u32[]{:S(2)}) collective-permute-start(f32[17,4,512]{2,1,0:T(4,128)S(1)} %get-tuple-element.7), channel_id=1, source_target_pairs={{0,16},{16,32},{32,48},{48,64},{64,80},{80,96},{96,112},{1,17},{17... | collective-permute-start | bytes 417800 | tf_op jit(solution)/shard_map/ppermute | solution.py:253
  39.5 7.3 %collective-permute-start.1 = (f32[17,4,512]{2,1,0:T(4,128)S(1)}, f32[17,4,512]{2,1,0:T(4,128)S(1)}, u32[]{:S(2)}, u32[]{:S(2)}) collective-permute-start(f32[17,4,512]{2,1,0:T(4,128)S(1)} %get-tuple-element.8), channel_id=1, source_target_pairs={{16,0},{32,16},{48,32},{64,48},{80,64},{96,80},{112,96},{17,1},{33... | collective-permute-start | bytes 417800 | tf_op jit(solution)/shard_map/ppermute | solution.py:253

commit v7 on v6

--- a/solution.py
+++ b/solution.py
@@ -1,3 +1,5 @@
+import functools
+
 import jax
 import jax.numpy as jnp
 from jax import lax
@@ -6,10 +8,9 @@
 from jax.sharding import PartitionSpec as P
 
 LANES = 128
-TILE = 8
 REACH = 2
 HALO = 2 * REACH
-RELAY, FIRST = 16, 60
+RELAY, FIRST, GROUP = 16, 60, 8
 
 
 def diffused(far_up, up, here, down, far_down, factor):
@@ -87,8 +88,10 @@
         out[:, to + i, :] = jnp.concatenate(moved(twice, start + i, offset(start + i)), axis=1)
 
 
-def load(grid, at, source, row):
+def load(grid, at, source, row, turn=0):
     line = source[pl.ds(0, grid.shape[2]), row, :]
+    if turn:
+        line = jnp.concatenate([line[turn:], line[:turn]])
     for c in range(grid.shape[1]):
         grid[at, c] = line[:, c * LANES : (c + 1) * LANES]
 
@@ -101,7 +104,7 @@
     last[members] = table[1]
 
 
-def inner_kernel(offsets, fractions, factors, main, out, grid, once, twice, laid, sems):
+def inner_kernel(offsets, fractions, factors, main, out, grid, once, twice):
     rows = main.shape[1]
 
     def relay(start, size):
@@ -118,33 +121,25 @@
     )
     in_groups(rows, RELAY, relay)
     in_groups(rows - 2 * REACH, FIRST, first_step)
-    copies = []
-    for tile in range(rows // TILE):
-        lo, hi = max(tile * TILE, HALO), min((tile + 1) * TILE, rows - HALO)
-        second_step(lo - HALO, hi - lo)
-        write(lambda i: offsets[1, i + HALO], twice, lo - HALO, hi - lo, laid, lo)
-        here = pl.ds(tile * TILE, TILE)
-        copies.append(pltpu.make_async_copy(laid.at[:, here], out.at[:, here], sems.at[tile]))
-        copies[-1].start()
-    for copy in copies:
-        copy.wait()
-
-
-def edge_kernel(offsets, fractions, factors, before, after, main, given, out, grid, once, twice, laid, table, sems):
+    for lo in range(HALO, rows - HALO, GROUP):
+        second_step(lo - HALO, GROUP)
+        write(lambda i: offsets[1, i + HALO], twice, lo - HALO, GROUP, out, lo)
+
+
+def edge_kernel(offsets, fractions, factors, before, after, main, given, out, grid, once, twice, table, sems):
+    del given
     members, rows, _ = main.shape
     steps = offsets.shape[0]
-    near = [pl.ds(0, TILE), pl.ds(rows - TILE, TILE)]
     tables = [
         pltpu.make_async_copy(halo.at[members, :, pl.ds(0, LANES)], table.at[side], sems.at[side])
         for side, halo in enumerate((before, after))
     ]
-    fetches = [pltpu.make_async_copy(given.at[:, near[side]], laid.at[side], sems.at[2 + side]) for side in range(2)]
-    for copy in tables + fetches:
+    for copy in tables:
         copy.start()
 
     for side, halo in enumerate((before, after)):
         for r in range(HALO):
-            load(grid.at[side], r + side * 2 * HALO, halo, r)
+            load(grid.at[side], r + side * 2 * HALO, halo, r, members // 2)
         for r in range(2 * HALO):
             load(grid.at[side], r + (1 - side) * HALO, main, r + side * (rows - 2 * HALO))
     for copy in tables:
@@ -174,20 +169,13 @@
         first_step(0, HALO + 2 * REACH)
     for _, _, second_step in sides:
         second_step(0, HALO)
-    for fetch in fetches:
-        fetch.wait()
-    stores = []
     for side, (offset, _, _) in enumerate(sides):
-        write(lambda i, offset=offset: offset(1, i + HALO), twice.at[side], 0, HALO, laid.at[side], side * (TILE - HALO))
-        stores.append(pltpu.make_async_copy(laid.at[side], out.at[:, near[side]], sems.at[2 + side]))
-        stores[-1].start()
-    for store in stores:
-        store.wait()
+        whole = functools.partial(offset, 1)
+        write(lambda i, whole=whole: whole(i + HALO), twice.at[side], 0, HALO, out, side * (rows - HALO))
 
 
 SMEM = pl.BlockSpec(memory_space=pltpu.SMEM)
 VMEM = pl.BlockSpec(memory_space=pltpu.VMEM)
-FAR = pl.BlockSpec(memory_space=pltpu.HBM)
 
 
 def grant(mebibytes):
@@ -211,15 +199,13 @@
     per = width // LANES
     return pl.pallas_call(
         inner_kernel,
-        out_shape=pltpu.HBM(main.shape, jnp.float32),
+        out_shape=pltpu.VMEM(main.shape, jnp.float32),
         in_specs=[SMEM] * 3 + [VMEM],
-        out_specs=FAR,
+        out_specs=VMEM,
         scratch_shapes=[
             pltpu.VMEM((rows, per, members, LANES), jnp.float32),
             pltpu.VMEM((rows - 2 * REACH, per, 2 * members, LANES), jnp.float32),
             pltpu.VMEM((rows - 2 * HALO, per, 2 * members, LANES), jnp.float32),
-            pltpu.VMEM(main.shape, jnp.float32),
-            pltpu.SemaphoreType.DMA((rows // TILE,)),
         ],
         compiler_params=grant(16),
     )(offsets, fractions, factors, main)
@@ -230,27 +216,34 @@
     per = width // LANES
     return pl.pallas_call(
         edge_kernel,
-        out_shape=pltpu.HBM(main.shape, jnp.float32),
-        in_specs=[SMEM] * 3 + [VMEM] * 3 + [FAR],
-        out_specs=FAR,
+        out_shape=pltpu.VMEM(main.shape, jnp.float32),
+        in_specs=[SMEM] * 3 + [VMEM] * 4,
+        out_specs=VMEM,
         scratch_shapes=[
             pltpu.VMEM((2, 3 * HALO, per, members, LANES), jnp.float32),
             pltpu.VMEM((2, HALO + 2 * REACH, per, 2 * members, LANES), jnp.float32),
             pltpu.VMEM((2, HALO, per, 2 * members, LANES), jnp.float32),
-            pltpu.VMEM((2, members, TILE, width), jnp.float32),
             pltpu.SMEM((2, HALO, LANES), jnp.float32),
-            pltpu.SemaphoreType.DMA((4,)),
+            pltpu.SemaphoreType.DMA((2,)),
         ],
         input_output_aliases={6: 0},
         compiler_params=grant(6),
-    )(offsets, fractions, factors, before, after, main, pltpu.with_memory_space_constraint(done, pltpu.HBM))
-
-
-def from_neighbours(first, last, axis):
-    peers = lax.axis_size(axis)
-    forth = [(i, i + 1) for i in range(peers - 1)]
+    )(offsets, fractions, factors, before, after, main, pltpu.with_memory_space_constraint(done, pltpu.VMEM))
+
+
+def owners(parts, members):
+    half = members // 2
+    return [[part * members + (m + part % 2 * half) % members for m in range(members)] for part in range(parts)]
+
+
+def exchanged(blocks, devices):
+    return lax.all_to_all(blocks, ("rad", "azi"), 0, 0, axis_index_groups=devices, tiled=True)
+
+
+def from_neighbours(first, last, devices):
+    forth = [pair for part, after in zip(devices, devices[1:]) for pair in zip(part, after)]
     back = [(j, i) for i, j in forth]
-    return lax.ppermute(last, axis, forth), lax.ppermute(first, axis, back)
+    return lax.ppermute(last, ("rad", "azi"), forth), lax.ppermute(first, ("rad", "azi"), back)
 
 
 def shards(fields, offsets, fractions, coefs):
@@ -258,16 +251,17 @@
     rows, width = shape[2], shape[3]
     blocks = fields.reshape(-1, rows, width)
     factors = coefs / 12.0
-    main = lax.all_to_all(blocks, "azi", 0, 0, tiled=True)
+    devices = owners(lax.axis_size("rad"), lax.axis_size("azi"))
+    main = exchanged(blocks, devices)
 
     table = jnp.concatenate([offsets.astype(jnp.float32), fractions, factors[None]]).T
     table = jnp.stack([table[:HALO], table[rows - HALO :]])
     table = jnp.pad(table, ((0, 0), (0, 0), (0, width - table.shape[2])))
 
-    before, after = from_neighbours(*edge_radii(main, table), "rad")
+    before, after = from_neighbours(*edge_radii(main, table), devices)
     done = inner(offsets, fractions, factors, main)
     done = edges(offsets, fractions, factors, before, after, main, done)
-    return lax.all_to_all(done, "azi", 0, 0, tiled=True).reshape(shape)
+    return exchanged(done, devices).reshape(shape)
 
 
 def solution(mesh):

time: 86.2 us -> 84.2 us (0.977)
  waiting for transfers between devices: 27.9 us -> 29.7 us
  Pallas kernels: 8.35 us -> 6.85 us
  blocking collectives: 34.9 us -> 33.6 us
    ppermute x2, waiting for transfers between devices: 0.29 us -> 2 us  [the longest x1 2 us: from_neighbours(): lax.ppermute(first, ('rad', 'azi'), back)]
    pallas_call x2, Pallas kernels: 8.33 us -> 6.83 us  [the longest x1 5 us: inner(): pl.pallas_call(inner_kernel, out_shape=pltpu.VMEM(main.shape, jnp.float32...]
    all_to_all x1, blocking collectives: 34.9 us -> 33.6 us  [exchanged(): lax.all_to_all(blocks, ('rad', 'azi'), 0, 0, axis_index_groups=devices, t...]
  transfers between devices with their start and end apart: 3 -> 3, of which waited for: 2 -> 2; matrix products, arithmetic and copies ran while one was open for 0% -> 0% of each run, Pallas kernels for 7% -> 6%
where the time goes in v7:
time: 84.2 us; the launch traced here: 83.9 us
  blocking collectives  33.6 us (40%)
  waiting for transfers between devices  29.7 us (35%)
  starting transfers between devices  12.1 us (14%)
  Pallas kernels  6.85 us (8%)
  local copies, waits for them, and re-layouts  1.59 us (2%)
    all_to_all x1, blocking collectives, exchanged(): lax.all_to_all(blocks, ('rad', 'azi'), 0, 0, axis_index_groups=devices, t...  33.6 us
    all_to_all x1, waiting for transfers between devices, exchanged(): lax.all_to_all(blocks, ('rad', 'azi'), 0, 0, axis_index_groups=devices, t...  27.7 us
    all_to_all x1, starting transfers between devices, exchanged(): lax.all_to_all(blocks, ('rad', 'azi'), 0, 0, axis_index_groups=devices, t...  7.06 us
    pallas_call x1, Pallas kernels, inner(): pl.pallas_call(inner_kernel, out_shape=pltpu.VMEM(main.shape, jnp.float32...  5 us
    ppermute x1, starting transfers between devices, from_neighbours(): lax.ppermute(last, ('rad', 'azi'), forth)  3.73 us
    ppermute x1, waiting for transfers between devices, from_neighbours(): lax.ppermute(first, ('rad', 'azi'), back)  2 us
    pallas_call x1, Pallas kernels, edges(): pl.pallas_call(edge_kernel, out_shape=pltpu.VMEM(main.shape, jnp.float32)...  1.83 us
  transfers between devices with their start and end apart: 3, of which 2 were waited for; matrix products, arithmetic and copies ran while one was open for 0% of the time, Pallas kernels for 6%

profile of v7, /device:TPU:1, one launch (start us, length us, event | category | flops | bytes accessed | tf_op | source)
XLA Modules:
  0.0 83.9 jit_solution(12216371092270396846)
XLA Ops:
  0.0 0.0 copy-start
  0.0 0.0 copy-start.2
  0.0 0.0 copy-start.1
  0.0 7.1 %all-to-all-start = ((f32[16,64,512]{2,1,0:T(8,128)}), f32[16,64,512]{2,1,0:T(8,128)S(1)}, u32[]{:S(2)}, u32[]{:S(2)}) async-start(f32[16,64,512]{2,1,0:T(8,128)} %bitcast.9), calls=%async_computation | async-start | bytes 4194304 | tf_op jit(solution)/shard_map/all_to_all | solution.py:240
  7.1 0.0 copy-done
  7.1 0.0 copy-done.2
  7.1 0.0 copy-done.1
  7.1 0.1 fusion.1
  7.2 0.1 copy.6
  7.3 0.1 copy.7
  7.4 27.7 %all-to-all-done.main = f32[16,64,512]{2,1,0:T(8,128)S(1)} async-done(((f32[16,64,512]{2,1,0:T(8,128)}), f32[16,64,512]{2,1,0:T(8,128)S(1)}, u32[]{:S(2)}, u32[]{:S(2)}) %all-to-all-start) | async-done | bytes 2097184 | tf_op jit(solution)/shard_map/all_to_all | solution.py:240
  35.1 3.7 %collective-permute-start = (f32[17,4,512]{2,1,0:T(4,128)S(1)}, f32[17,4,512]{2,1,0:T(4,128)S(1)}, u32[]{:S(2)}, u32[]{:S(2)}) collective-permute-start(f32[17,4,512]{2,1,0:T(4,128)S(1)} %get-tuple-element.7), channel_id=1, source_target_pairs={{0,24},{1,25},{2,26},{3,27},{4,28},{5,29},{6,30},{7,31},{8,16},{9,... | collective-permute-start | bytes 417800 | tf_op jit(solution)/shard_map/ppermute | solution.py:246
  38.8 1.3 %collective-permute-start.1 = (f32[17,4,512]{2,1,0:T(4,128)S(1)}, f32[17,4,512]{2,1,0:T(4,128)S(1)}, u32[]{:S(2)}, u32[]{:S(2)}) collective-permute-start(f32[17,4,512]{2,1,0:T(4,128)S(1)} %get-tuple-element.8), channel_id=1, source_target_pairs={{24,0},{25,1},{26,2},{27,3},{28,4},{29,5},{30,6},{31,7},{16,8},{17... | collective-permute-start | bytes 417800 | tf_op jit(solution)/shard_map/ppermute | solution.py:246
  40.1 5.0 %shard_map.47.given = f32[16,64,512]{2,1,0:T(8,128)S(1)} custom-call(s32[2,64]{1,0:T(2,128)S(1)} %copy-done, f32[2,64]{1,0:T(2,128)S(1)} %copy-done.1, f32[64]{0:T(128)S(1)} %get-tuple-element.12.factors, f32[16,64,512]{2,1,0:T(8,128)S(1)} %all-to-all-done.main), custom_call_target="tpu_custom_call" | custom-call | tf_op jit(solution)/shard_map/pallas_call | solution.py:200
  45.1 0.0 collective-permute-done.before
  45.1 2.0 %collective-permute-done.1.after = f32[17,4,512]{2,1,0:T(4,128)S(1)} collective-permute-done((f32[17,4,512]{2,1,0:T(4,128)S(1)}, f32[17,4,512]{2,1,0:T(4,128)S(1)}, u32[]{:S(2)}, u32[]{:S(2)}) %collective-permute-start.1) | collective-permute-done | bytes 139296 | tf_op jit(solution)/shard_map/ppermute | solution.py:246
  47.1 1.8 %shard_map.48 = f32[16,64,512]{2,1,0:T(8,128)S(1)} custom-call(s32[2,64]{1,0:T(2,128)S(1)} %copy-done, f32[2,64]{1,0:T(2,128)S(1)} %copy-done.1, f32[64]{0:T(128)S(1)} %get-tuple-element.12.factors, f32[17,4,512]{2,1,0:T(4,128)S(1)} %collective-permute-done.before, f32[17,4,512]{2,1,0:T(4,128)S(1)} %collective-permute-done.1.after, ...), custom_call_target="tpu_custom_call", output_to_operand_aliasing={{}: (6, {})} | custom-call | tf_op jit(solution)/shard_map/pallas_call | solution.py:217
  49.0 33.6 %all_to_all.10 = f32[16,64,512]{2,1,0:T(8,128)S(1)} all-to-all(f32[16,64,512]{2,1,0:T(8,128)S(1)} %shard_map.48), channel_id=1, replica_groups={{0,1,2,3,4,5,6,7,8,9,10,11,12,13,14,15},{24,25,26,27,28,29,30,31,16,17,..., dimensions={0} | all-to-all | bytes 4194304 | tf_op jit(solution)/shard_map/all_to_all | solution.py:240
  82.6 1.3 %copy.10 = f32[8,2,64,512]{3,2,1,0:T(8,128)} copy(f32[8,2,64,512]{3,2,1,0:T(8,128)S(1)} %bitcast.8) | data formatting | bytes 4194304
  (5 shorter events, 0.0 us)
Async XLA Ops:
  0.0 7.1 %copy-start = (s32[2,64]{1,0:T(2,128)S(1)}, s32[2,64]{1,0:T(2,128)}, u32[]{:S(2)}) copy-start(s32[2,64]{1,0:T(2,128)} %offsets.3) | copy-start | bytes 1540
  0.0 7.1 %copy-start.2 = (f32[64]{0:T(128)S(1)}, f32[64]{0:T(128)}, u32[]{:S(2)}) copy-start(f32[64]{0:T(128)} %param.7) | copy-start | bytes 772
  0.0 7.1 %copy-start.1 = (f32[2,64]{1,0:T(2,128)S(1)}, f32[2,64]{1,0:T(2,128)}, u32[]{:S(2)}) copy-start(f32[2,64]{1,0:T(2,128)} %fractions.3) | copy-start | bytes 1540
  0.0 35.0 %all-to-all-start = ((f32[16,64,512]{2,1,0:T(8,128)}), f32[16,64,512]{2,1,0:T(8,128)S(1)}, u32[]{:S(2)}, u32[]{:S(2)}) async-start(f32[16,64,512]{2,1,0:T(8,128)} %bitcast.9), calls=%async_computation | async-start | bytes 4194304 | tf_op jit(solution)/shard_map/all_to_all | solution.py:240
  35.1 10.1 %collective-permute-start = (f32[17,4,512]{2,1,0:T(4,128)S(1)}, f32[17,4,512]{2,1,0:T(4,128)S(1)}, u32[]{:S(2)}, u32[]{:S(2)}) collective-permute-start(f32[17,4,512]{2,1,0:T(4,128)S(1)} %get-tuple-element.7), channel_id=1, source_target_pairs={{0,24},{1,25},{2,26},{3,27},{4,28},{5,29},{6,30},{7,31},{8,16},{9,... | collective-permute-start | bytes 417800 | tf_op jit(solution)/shard_map/ppermute | solution.py:246
  38.8 8.3 %collective-permute-start.1 = (f32[17,4,512]{2,1,0:T(4,128)S(1)}, f32[17,4,512]{2,1,0:T(4,128)S(1)}, u32[]{:S(2)}, u32[]{:S(2)}) collective-permute-start(f32[17,4,512]{2,1,0:T(4,128)S(1)} %get-tuple-element.8), channel_id=1, source_target_pairs={{24,0},{25,1},{26,2},{27,3},{28,4},{29,5},{30,6},{31,7},{16,8},{17... | collective-permute-start | bytes 417800 | tf_op jit(solution)/shard_map/ppermute | solution.py:246

commit v8 on v7

--- a/solution.py
+++ b/solution.py
@@ -96,12 +96,13 @@
         grid[at, c] = line[:, c * LANES : (c + 1) * LANES]
 
 
-def edge_radii_kernel(main, table, first, last):
+def edge_radii_kernel(inside, main, table, first, last):
     members, rows, _ = main.shape
-    first[pl.ds(0, members)] = main[:, :HALO]
-    first[members] = table[0]
-    last[pl.ds(0, members)] = main[:, rows - HALO :]
-    last[members] = table[1]
+    for side, (out, start) in enumerate(((first, 0), (last, rows - HALO))):
+        sent = inside[side] > 0
+        radii = main[:, start : start + HALO]
+        out[pl.ds(0, members)] = jnp.where(sent, radii, jnp.zeros_like(radii))
+        out[members] = jnp.where(sent, table[side], jnp.zeros_like(table[side]))
 
 
 def inner_kernel(offsets, fractions, factors, main, out, grid, once, twice):
@@ -182,16 +183,16 @@
     return pltpu.CompilerParams(vmem_limit_bytes=mebibytes << 20)
 
 
-def edge_radii(main, table):
+def edge_radii(inside, main, table):
     members, _, width = main.shape
     side = jax.ShapeDtypeStruct((members + 1, HALO, width), jnp.float32)
     return pl.pallas_call(
         edge_radii_kernel,
         out_shape=[side, side],
-        in_specs=[VMEM, VMEM],
+        in_specs=[SMEM, VMEM, VMEM],
         out_specs=[VMEM, VMEM],
         compiler_params=grant(2),
-    )(main, table)
+    )(inside, main, table)
 
 
 def inner(offsets, fractions, factors, main):
@@ -241,7 +242,7 @@
 
 
 def from_neighbours(first, last, devices):
-    forth = [pair for part, after in zip(devices, devices[1:]) for pair in zip(part, after)]
+    forth = [pair for part, after in zip(devices, devices[1:] + devices[:1]) for pair in zip(part, after)]
     back = [(j, i) for i, j in forth]
     return lax.ppermute(last, ("rad", "azi"), forth), lax.ppermute(first, ("rad", "azi"), back)
 
@@ -258,7 +259,9 @@
     table = jnp.stack([table[:HALO], table[rows - HALO :]])
     table = jnp.pad(table, ((0, 0), (0, 0), (0, width - table.shape[2])))
 
-    before, after = from_neighbours(*edge_radii(main, table), devices)
+    part = lax.axis_index("rad")
+    inside = jnp.stack([part > 0, part < len(devices) - 1]).astype(jnp.int32)
+    before, after = from_neighbours(*edge_radii(inside, main, table), devices)
     done = inner(offsets, fractions, factors, main)
     done = edges(offsets, fractions, factors, before, after, main, done)
     return exchanged(done, devices).reshape(shape)

time: 84.2 us -> 82.9 us (0.985)
  waiting for transfers between devices: 29.7 us -> 27.6 us
    ppermute x1, starting transfers between devices: 1.29 us -> 3.55 us  [from_neighbours(): lax.ppermute(first, ('rad', 'azi'), back)]
    ppermute x1, waiting for transfers between devices: 2 us -> 0.01 us  [from_neighbours(): lax.ppermute(first, ('rad', 'azi'), back)]
    ppermute x1, starting transfers between devices: 3.73 us -> 1.89 us  [from_neighbours(): lax.ppermute(last, ('rad', 'azi'), forth)]
  transfers between devices with their start and end apart: 3 -> 3, of which waited for: 2 -> 1; matrix products, arithmetic and copies ran while one was open for 0% -> 0% of each run, Pallas kernels for 6% -> 6%
where the time goes in v8:
time: 82.9 us; the launch traced here: 82.7 us
  blocking collectives  33.4 us (40%)
  waiting for transfers between devices  27.6 us (33%)
  starting transfers between devices  12.5 us (15%)
  Pallas kernels  7.42 us (9%)
  local copies, waits for them, and re-layouts  1.59 us (2%)
    all_to_all x1, blocking collectives, exchanged(): lax.all_to_all(blocks, ('rad', 'azi'), 0, 0, axis_index_groups=devices, t...  33.4 us
    all_to_all x1, waiting for transfers between devices, exchanged(): lax.all_to_all(blocks, ('rad', 'azi'), 0, 0, axis_index_groups=devices, t...  27.6 us
    all_to_all x1, starting transfers between devices, exchanged(): lax.all_to_all(blocks, ('rad', 'azi'), 0, 0, axis_index_groups=devices, t...  7.06 us
    pallas_call x1, Pallas kernels, inner(): pl.pallas_call(inner_kernel, out_shape=pltpu.VMEM(main.shape, jnp.float32...  5 us
    ppermute x1, starting transfers between devices, from_neighbours(): lax.ppermute(first, ('rad', 'azi'), back)  3.55 us
    ppermute x1, starting transfers between devices, from_neighbours(): lax.ppermute(last, ('rad', 'azi'), forth)  1.89 us
    pallas_call x1, Pallas kernels, edges(): pl.pallas_call(edge_kernel, out_shape=pltpu.VMEM(main.shape, jnp.float32)...  1.84 us
  transfers between devices with their start and end apart: 3, of which 1 were waited for; matrix products, arithmetic and copies ran while one was open for 0% of the time, Pallas kernels for 6%

profile of v8, /device:TPU:1, one launch (start us, length us, event | category | flops | bytes accessed | tf_op | source)
XLA Modules:
  0.0 82.7 jit_solution(9172149532933133770)
XLA Ops:
  0.0 0.0 copy-start
  0.0 0.0 copy-start.2
  0.0 0.0 copy-start.1
  0.0 7.1 %all-to-all-start = ((f32[16,64,512]{2,1,0:T(8,128)}), f32[16,64,512]{2,1,0:T(8,128)S(1)}, u32[]{:S(2)}, u32[]{:S(2)}) async-start(f32[16,64,512]{2,1,0:T(8,128)} %bitcast.11), calls=%async_computation | async-start | bytes 4194304 | tf_op jit(solution)/shard_map/all_to_all | solution.py:241
  7.1 0.0 copy-done
  7.1 0.0 copy-done.2
  7.1 0.0 copy-done.1
  7.1 0.1 fusion.1
  7.2 0.1 copy.6
  7.3 0.1 copy.7
  7.4 0.1 add_convert_fusion.inside
  7.5 27.6 %all-to-all-done.main = f32[16,64,512]{2,1,0:T(8,128)S(1)} async-done(((f32[16,64,512]{2,1,0:T(8,128)}), f32[16,64,512]{2,1,0:T(8,128)S(1)}, u32[]{:S(2)}, u32[]{:S(2)}) %all-to-all-start) | async-done | bytes 2097184 | tf_op jit(solution)/shard_map/all_to_all | solution.py:241
  35.1 0.6 shard_map.46
  35.7 1.9 %collective-permute-start = (f32[17,4,512]{2,1,0:T(4,128)S(1)}, f32[17,4,512]{2,1,0:T(4,128)S(1)}, u32[]{:S(2)}, u32[]{:S(2)}) collective-permute-start(f32[17,4,512]{2,1,0:T(4,128)S(1)} %get-tuple-element.7), channel_id=1, source_target_pairs={{0,24},{1,25},{2,26},{3,27},{4,28},{5,29},{6,30},{7,31},{8,16},{9,... | collective-permute-start | bytes 417800 | tf_op jit(solution)/shard_map/ppermute | solution.py:247
  37.5 3.6 %collective-permute-start.1 = (f32[17,4,512]{2,1,0:T(4,128)S(1)}, f32[17,4,512]{2,1,0:T(4,128)S(1)}, u32[]{:S(2)}, u32[]{:S(2)}) collective-permute-start(f32[17,4,512]{2,1,0:T(4,128)S(1)} %get-tuple-element.8), channel_id=1, source_target_pairs={{24,0},{25,1},{26,2},{27,3},{28,4},{29,5},{30,6},{31,7},{16,8},{17... | collective-permute-start | bytes 417800 | tf_op jit(solution)/shard_map/ppermute | solution.py:247
  41.1 5.0 %shard_map.47.given = f32[16,64,512]{2,1,0:T(8,128)S(1)} custom-call(s32[2,64]{1,0:T(2,128)S(1)} %copy-done, f32[2,64]{1,0:T(2,128)S(1)} %copy-done.1, f32[64]{0:T(128)S(1)} %get-tuple-element.12.factors, f32[16,64,512]{2,1,0:T(8,128)S(1)} %all-to-all-done.main), custom_call_target="tpu_custom_call" | custom-call | tf_op jit(solution)/shard_map/pallas_call | solution.py:201
  46.1 0.0 collective-permute-done.before
  46.1 0.0 collective-permute-done.1.after
  46.1 1.8 %shard_map.48 = f32[16,64,512]{2,1,0:T(8,128)S(1)} custom-call(s32[2,64]{1,0:T(2,128)S(1)} %copy-done, f32[2,64]{1,0:T(2,128)S(1)} %copy-done.1, f32[64]{0:T(128)S(1)} %get-tuple-element.12.factors, f32[17,4,512]{2,1,0:T(4,128)S(1)} %collective-permute-done.before, f32[17,4,512]{2,1,0:T(4,128)S(1)} %collective-permute-done.1.after, ...), custom_call_target="tpu_custom_call", output_to_operand_aliasing={{}: (6, {})} | custom-call | tf_op jit(solution)/shard_map/pallas_call | solution.py:218
  48.0 33.4 %all_to_all.10 = f32[16,64,512]{2,1,0:T(8,128)S(1)} all-to-all(f32[16,64,512]{2,1,0:T(8,128)S(1)} %shard_map.48), channel_id=1, replica_groups={{0,1,2,3,4,5,6,7,8,9,10,11,12,13,14,15},{24,25,26,27,28,29,30,31,16,17,..., dimensions={0} | all-to-all | bytes 4194304 | tf_op jit(solution)/shard_map/all_to_all | solution.py:241
  81.3 1.3 %copy.10 = f32[8,2,64,512]{3,2,1,0:T(8,128)} copy(f32[8,2,64,512]{3,2,1,0:T(8,128)S(1)} %bitcast.10) | data formatting | bytes 4194304
  (4 shorter events, 0.0 us)
Async XLA Ops:
  0.0 7.1 %copy-start = (s32[2,64]{1,0:T(2,128)S(1)}, s32[2,64]{1,0:T(2,128)}, u32[]{:S(2)}) copy-start(s32[2,64]{1,0:T(2,128)} %offsets.3) | copy-start | bytes 1540
  0.0 7.1 %copy-start.2 = (f32[64]{0:T(128)S(1)}, f32[64]{0:T(128)}, u32[]{:S(2)}) copy-start(f32[64]{0:T(128)} %param.7) | copy-start | bytes 772
  0.0 7.1 %copy-start.1 = (f32[2,64]{1,0:T(2,128)S(1)}, f32[2,64]{1,0:T(2,128)}, u32[]{:S(2)}) copy-start(f32[2,64]{1,0:T(2,128)} %fractions.3) | copy-start | bytes 1540
  0.0 35.0 %all-to-all-start = ((f32[16,64,512]{2,1,0:T(8,128)}), f32[16,64,512]{2,1,0:T(8,128)S(1)}, u32[]{:S(2)}, u32[]{:S(2)}) async-start(f32[16,64,512]{2,1,0:T(8,128)} %bitcast.11), calls=%async_computation | async-start | bytes 4194304 | tf_op jit(solution)/shard_map/all_to_all | solution.py:241
  35.7 10.4 %collective-permute-start = (f32[17,4,512]{2,1,0:T(4,128)S(1)}, f32[17,4,512]{2,1,0:T(4,128)S(1)}, u32[]{:S(2)}, u32[]{:S(2)}) collective-permute-start(f32[17,4,512]{2,1,0:T(4,128)S(1)} %get-tuple-element.7), channel_id=1, source_target_pairs={{0,24},{1,25},{2,26},{3,27},{4,28},{5,29},{6,30},{7,31},{8,16},{9,... | collective-permute-start | bytes 417800 | tf_op jit(solution)/shard_map/ppermute | solution.py:247
  37.5 8.6 %collective-permute-start.1 = (f32[17,4,512]{2,1,0:T(4,128)S(1)}, f32[17,4,512]{2,1,0:T(4,128)S(1)}, u32[]{:S(2)}, u32[]{:S(2)}) collective-permute-start(f32[17,4,512]{2,1,0:T(4,128)S(1)} %get-tuple-element.8), channel_id=1, source_target_pairs={{24,0},{25,1},{26,2},{27,3},{28,4},{29,5},{30,6},{31,7},{16,8},{17... | collective-permute-start | bytes 417800 | tf_op jit(solution)/shard_map/ppermute | solution.py:247

commit v9 on v8

--- a/solution.py
+++ b/solution.py
@@ -10,6 +10,7 @@
 LANES = 128
 REACH = 2
 HALO = 2 * REACH
+PER_DIFFERENCE = 1.0 / 12.0
 RELAY, FIRST, GROUP = 16, 60, 8
 
 
@@ -96,16 +97,26 @@
         grid[at, c] = line[:, c * LANES : (c + 1) * LANES]
 
 
-def edge_radii_kernel(inside, main, table, first, last):
-    members, rows, _ = main.shape
-    for side, (out, start) in enumerate(((first, 0), (last, rows - HALO))):
-        sent = inside[side] > 0
+def edge_radii_kernel(offsets, fractions, coefs, main, first, last):
+    members, rows, width = main.shape
+    steps = offsets.shape[0]
+    part, parts = lax.axis_index("rad"), lax.axis_size("rad")
+    lane = lax.broadcasted_iota(jnp.int32, (1, width), 1)
+    for out, start, sent in ((first, 0, part > 0), (last, rows - HALO, part < parts - 1)):
         radii = main[:, start : start + HALO]
         out[pl.ds(0, members)] = jnp.where(sent, radii, jnp.zeros_like(radii))
-        out[members] = jnp.where(sent, table[side], jnp.zeros_like(table[side]))
-
-
-def inner_kernel(offsets, fractions, factors, main, out, grid, once, twice):
+        for r in range(HALO):
+            at = start + r
+            entries = [offsets[step, at].astype(jnp.float32) for step in range(steps)]
+            entries += [fractions[step, at] for step in range(steps)]
+            entries.append(coefs[at])
+            line = jnp.zeros((1, width), jnp.float32)
+            for column, entry in enumerate(entries):
+                line = jnp.where(lane == column, jnp.where(sent, entry, 0.0), line)
+            out[members, pl.ds(r, 1)] = line
+
+
+def inner_kernel(offsets, fractions, coefs, main, out, grid, once, twice):
     rows = main.shape[1]
 
     def relay(start, size):
@@ -115,7 +126,7 @@
     first_step, second_step = two_steps(
         lambda step, at: offsets[step, at],
         lambda step, at: fractions[step, at],
-        lambda at: factors[at],
+        lambda at: coefs[at] * PER_DIFFERENCE,
         grid,
         once,
         twice,
@@ -127,7 +138,7 @@
         write(lambda i: offsets[1, i + HALO], twice, lo - HALO, GROUP, out, lo)
 
 
-def edge_kernel(offsets, fractions, factors, before, after, main, given, out, grid, once, twice, table, sems):
+def edge_kernel(offsets, fractions, coefs, before, after, main, given, out, grid, once, twice, table, sems):
     del given
     members, rows, _ = main.shape
     steps = offsets.shape[0]
@@ -160,7 +171,7 @@
             return entry(lambda row: fractions[step, row], steps + step, at)
 
         def factor(at):
-            return entry(lambda row: factors[row], 2 * steps, at)
+            return entry(lambda row: coefs[row], 2 * steps, at) * PER_DIFFERENCE
 
         first_step, second_step = two_steps(offset, fraction, factor, grid.at[side], once.at[side], twice.at[side])
         return offset, first_step, second_step
@@ -183,19 +194,19 @@
     return pltpu.CompilerParams(vmem_limit_bytes=mebibytes << 20)
 
 
-def edge_radii(inside, main, table):
+def edge_radii(offsets, fractions, coefs, main):
     members, _, width = main.shape
     side = jax.ShapeDtypeStruct((members + 1, HALO, width), jnp.float32)
     return pl.pallas_call(
         edge_radii_kernel,
         out_shape=[side, side],
-        in_specs=[SMEM, VMEM, VMEM],
+        in_specs=[SMEM] * 3 + [VMEM],
         out_specs=[VMEM, VMEM],
         compiler_params=grant(2),
-    )(inside, main, table)
-
-
-def inner(offsets, fractions, factors, main):
+    )(offsets, fractions, coefs, main)
+
+
+def inner(offsets, fractions, coefs, main):
     members, rows, width = main.shape
     per = width // LANES
     return pl.pallas_call(
@@ -209,10 +220,10 @@
             pltpu.VMEM((rows - 2 * HALO, per, 2 * members, LANES), jnp.float32),
         ],
         compiler_params=grant(16),
-    )(offsets, fractions, factors, main)
-
-
-def edges(offsets, fractions, factors, before, after, main, done):
+    )(offsets, fractions, coefs, main)
+
+
+def edges(offsets, fractions, coefs, before, after, main, done):
     members, _, width = main.shape
     per = width // LANES
     return pl.pallas_call(
@@ -229,7 +240,7 @@
         ],
         input_output_aliases={6: 0},
         compiler_params=grant(6),
-    )(offsets, fractions, factors, before, after, main, pltpu.with_memory_space_constraint(done, pltpu.VMEM))
+    )(offsets, fractions, coefs, before, after, main, pltpu.with_memory_space_constraint(done, pltpu.VMEM))
 
 
 def owners(parts, members):
@@ -251,19 +262,12 @@
     shape = fields.shape
     rows, width = shape[2], shape[3]
     blocks = fields.reshape(-1, rows, width)
-    factors = coefs / 12.0
     devices = owners(lax.axis_size("rad"), lax.axis_size("azi"))
     main = exchanged(blocks, devices)
 
-    table = jnp.concatenate([offsets.astype(jnp.float32), fractions, factors[None]]).T
-    table = jnp.stack([table[:HALO], table[rows - HALO :]])
-    table = jnp.pad(table, ((0, 0), (0, 0), (0, width - table.shape[2])))
-
-    part = lax.axis_index("rad")
-    inside = jnp.stack([part > 0, part < len(devices) - 1]).astype(jnp.int32)
-    before, after = from_neighbours(*edge_radii(inside, main, table), devices)
-    done = inner(offsets, fractions, factors, main)
-    done = edges(offsets, fractions, factors, before, after, main, done)
+    before, after = from_neighbours(*edge_radii(offsets, fractions, coefs, main), devices)
+    done = inner(offsets, fractions, coefs, main)
+    done = edges(offsets, fractions, coefs, before, after, main, done)
     return exchanged(done, devices).reshape(shape)
 
 

time: 82.9 us -> 79.1 us (0.954)
  blocking collectives: 33.4 us -> 64.6 us
  waiting for transfers between devices: 27.6 us -> 0.01 us
  starting transfers between devices: 12.5 us -> 5.44 us
    all_to_all x1 -> x2, blocking collectives: 33.4 us -> 64.6 us  [exchanged(): lax.all_to_all(blocks, ('rad', 'azi'), 0, 0, axis_index_groups=devices, t...]
    all_to_all x1 -> x0, waiting for transfers between devices: 27.6 us -> none  [exchanged(): lax.all_to_all(blocks, ('rad', 'azi'), 0, 0, axis_index_groups=devices, t...]
    all_to_all x1 -> x0, starting transfers between devices: 7.06 us -> none  [exchanged(): lax.all_to_all(blocks, ('rad', 'azi'), 0, 0, axis_index_groups=devices, t...]
  transfers between devices with their start and end apart: 3 -> 2, of which waited for: 1 -> 0; matrix products, arithmetic and copies ran while one was open for 0% -> 0% of each run, Pallas kernels for 6% -> 6%
where the time goes in v9:
time: 79.1 us; the launch traced here: 78.9 us
  blocking collectives  64.6 us (82%)
  Pallas kernels  7.46 us (9%)
  starting transfers between devices  5.44 us (7%)
  local copies, waits for them, and re-layouts  1.33 us (2%)
    all_to_all x2, blocking collectives, exchanged(): lax.all_to_all(blocks, ('rad', 'azi'), 0, 0, axis_index_groups=devices, t...  64.6 us
    pallas_call x1, Pallas kernels, inner(): pl.pallas_call(inner_kernel, out_shape=pltpu.VMEM(main.shape, jnp.float32...  4.99 us
    ppermute x1, starting transfers between devices, from_neighbours(): lax.ppermute(first, ('rad', 'azi'), back)  3.55 us
    ppermute x1, starting transfers between devices, from_neighbours(): lax.ppermute(last, ('rad', 'azi'), forth)  1.89 us
    pallas_call x1, Pallas kernels, edges(): pl.pallas_call(edge_kernel, out_shape=pltpu.VMEM(main.shape, jnp.float32)...  1.84 us
  transfers between devices with their start and end apart: 2, of which 0 were waited for; matrix products, arithmetic and copies ran while one was open for 0% of the time, Pallas kernels for 6%

profile of v9, /device:TPU:1, one launch (start us, length us, event | category | flops | bytes accessed | tf_op | source)
XLA Modules:
  0.0 78.9 jit_solution(13950609815567142502)
XLA Ops:
  0.0 0.0 copy-start
  0.0 0.0 copy-start.1
  0.0 0.0 copy-start.2
  0.0 33.7 %all_to_all.10.main = f32[16,64,512]{2,1,0:T(8,128)S(1)} all-to-all(f32[16,64,512]{2,1,0:T(8,128)} %bitcast.3), channel_id=1, replica_groups={{0,1,2,3,4,5,6,7,8,9,10,11,12,13,14,15},{24,25,26,27,28,29,30,31,16,17,..., dimensions={0} | all-to-all | bytes 4194304 | tf_op jit(solution)/shard_map/all_to_all | solution.py:252
  33.7 0.0 copy-done
  33.7 0.0 copy-done.1
  33.7 0.0 copy-done.2
  33.7 0.6 shard_map.46
  34.4 1.9 %collective-permute-start = (f32[17,4,512]{2,1,0:T(4,128)S(1)}, f32[17,4,512]{2,1,0:T(4,128)S(1)}, u32[]{:S(2)}, u32[]{:S(2)}) collective-permute-start(f32[17,4,512]{2,1,0:T(4,128)S(1)} %get-tuple-element.7), channel_id=1, source_target_pairs={{0,24},{1,25},{2,26},{3,27},{4,28},{5,29},{6,30},{7,31},{8,16},{9,... | collective-permute-start | bytes 417800 | tf_op jit(solution)/shard_map/ppermute | solution.py:258
  36.3 3.6 %collective-permute-start.1 = (f32[17,4,512]{2,1,0:T(4,128)S(1)}, f32[17,4,512]{2,1,0:T(4,128)S(1)}, u32[]{:S(2)}, u32[]{:S(2)}) collective-permute-start(f32[17,4,512]{2,1,0:T(4,128)S(1)} %get-tuple-element.8), channel_id=1, source_target_pairs={{24,0},{25,1},{26,2},{27,3},{28,4},{29,5},{30,6},{31,7},{16,8},{17... | collective-permute-start | bytes 417800 | tf_op jit(solution)/shard_map/ppermute | solution.py:258
  39.8 5.0 %shard_map.47.given = f32[16,64,512]{2,1,0:T(8,128)S(1)} custom-call(s32[2,64]{1,0:T(2,128)S(1)} %copy-done, f32[2,64]{1,0:T(2,128)S(1)} %copy-done.1, f32[64]{0:T(128)S(1)} %copy-done.2, f32[16,64,512]{2,1,0:T(8,128)S(1)} %all_to_all.10.main), custom_call_target="tpu_custom_call" | custom-call | tf_op jit(solution)/shard_map/pallas_call | solution.py:212
  44.8 0.0 collective-permute-done.before
  44.8 0.0 collective-permute-done.1.after
  44.8 1.8 %shard_map.48 = f32[16,64,512]{2,1,0:T(8,128)S(1)} custom-call(s32[2,64]{1,0:T(2,128)S(1)} %copy-done, f32[2,64]{1,0:T(2,128)S(1)} %copy-done.1, f32[64]{0:T(128)S(1)} %copy-done.2, f32[17,4,512]{2,1,0:T(4,128)S(1)} %collective-permute-done.before, f32[17,4,512]{2,1,0:T(4,128)S(1)} %collective-permute-done.1.after, ...), custom_call_target="tpu_custom_call", output_to_operand_aliasing={{}: (6, {})} | custom-call | tf_op jit(solution)/shard_map/pallas_call | solution.py:229
  46.7 30.9 %all_to_all.11 = f32[16,64,512]{2,1,0:T(8,128)S(1)} all-to-all(f32[16,64,512]{2,1,0:T(8,128)S(1)} %shard_map.48), channel_id=1, replica_groups={{0,1,2,3,4,5,6,7,8,9,10,11,12,13,14,15},{24,25,26,27,28,29,30,31,16,17,..., dimensions={0} | all-to-all | bytes 4194304 | tf_op jit(solution)/shard_map/all_to_all | solution.py:252
  77.6 1.3 %copy.8 = f32[8,2,64,512]{3,2,1,0:T(8,128)} copy(f32[8,2,64,512]{3,2,1,0:T(8,128)S(1)} %bitcast.2) | data formatting | bytes 4194304
Async XLA Ops:
  0.0 33.7 %copy-start = (s32[2,64]{1,0:T(2,128)S(1)}, s32[2,64]{1,0:T(2,128)}, u32[]{:S(2)}) copy-start(s32[2,64]{1,0:T(2,128)} %offsets.5) | copy-start | bytes 1540
  0.0 33.7 %copy-start.1 = (f32[2,64]{1,0:T(2,128)S(1)}, f32[2,64]{1,0:T(2,128)}, u32[]{:S(2)}) copy-start(f32[2,64]{1,0:T(2,128)} %fractions.5) | copy-start | bytes 1540
  0.0 33.7 %copy-start.2 = (f32[64]{0:T(128)S(1)}, f32[64]{0:T(128)}, u32[]{:S(2)}) copy-start(f32[64]{0:T(128)} %coefs.5) | copy-start | bytes 772
  34.4 10.4 %collective-permute-start = (f32[17,4,512]{2,1,0:T(4,128)S(1)}, f32[17,4,512]{2,1,0:T(4,128)S(1)}, u32[]{:S(2)}, u32[]{:S(2)}) collective-permute-start(f32[17,4,512]{2,1,0:T(4,128)S(1)} %get-tuple-element.7), channel_id=1, source_target_pairs={{0,24},{1,25},{2,26},{3,27},{4,28},{5,29},{6,30},{7,31},{8,16},{9,... | collective-permute-start | bytes 417800 | tf_op jit(solution)/shard_map/ppermute | solution.py:258
  36.3 8.6 %collective-permute-start.1 = (f32[17,4,512]{2,1,0:T(4,128)S(1)}, f32[17,4,512]{2,1,0:T(4,128)S(1)}, u32[]{:S(2)}, u32[]{:S(2)}) collective-permute-start(f32[17,4,512]{2,1,0:T(4,128)S(1)} %get-tuple-element.8), channel_id=1, source_target_pairs={{24,0},{25,1},{26,2},{27,3},{28,4},{29,5},{30,6},{31,7},{16,8},{17... | collective-permute-start | bytes 417800 | tf_op jit(solution)/shard_map/ppermute | solution.py:258

commit v10 on v9

--- a/solution.py
+++ b/solution.py
@@ -138,52 +138,38 @@
         write(lambda i: offsets[1, i + HALO], twice, lo - HALO, GROUP, out, lo)
 
 
-def edge_kernel(offsets, fractions, coefs, before, after, main, given, out, grid, once, twice, table, sems):
+def edge_kernel(side, offsets, fractions, coefs, halo, main, given, out, grid, once, twice, table, sem):
     del given
     members, rows, _ = main.shape
     steps = offsets.shape[0]
-    tables = [
-        pltpu.make_async_copy(halo.at[members, :, pl.ds(0, LANES)], table.at[side], sems.at[side])
-        for side, halo in enumerate((before, after))
-    ]
-    for copy in tables:
-        copy.start()
-
-    for side, halo in enumerate((before, after)):
-        for r in range(HALO):
-            load(grid.at[side], r + side * 2 * HALO, halo, r, members // 2)
-        for r in range(2 * HALO):
-            load(grid.at[side], r + (1 - side) * HALO, main, r + side * (rows - 2 * HALO))
-    for copy in tables:
-        copy.wait()
-
-    def side_steps(side):
-        def entry(own, column, at):
-            row = at - HALO if side == 0 else at + rows - 2 * HALO
-            if 0 <= row < rows:
-                return own(row)
-            return table[side, row + HALO if side == 0 else row - rows, column]
-
-        def offset(step, at):
-            return entry(lambda row: offsets[step, row], step, at).astype(jnp.int32)
-
-        def fraction(step, at):
-            return entry(lambda row: fractions[step, row], steps + step, at)
-
-        def factor(at):
-            return entry(lambda row: coefs[row], 2 * steps, at) * PER_DIFFERENCE
-
-        first_step, second_step = two_steps(offset, fraction, factor, grid.at[side], once.at[side], twice.at[side])
-        return offset, first_step, second_step
-
-    sides = [side_steps(side) for side in range(2)]
-    for _, first_step, _ in sides:
-        first_step(0, HALO + 2 * REACH)
-    for _, _, second_step in sides:
-        second_step(0, HALO)
-    for side, (offset, _, _) in enumerate(sides):
-        whole = functools.partial(offset, 1)
-        write(lambda i, whole=whole: whole(i + HALO), twice.at[side], 0, HALO, out, side * (rows - HALO))
+    copy = pltpu.make_async_copy(halo.at[members, :, pl.ds(0, LANES)], table, sem)
+    copy.start()
+    for r in range(HALO):
+        load(grid, r + side * 2 * HALO, halo, r, members // 2)
+    for r in range(2 * HALO):
+        load(grid, r + (1 - side) * HALO, main, r + side * (rows - 2 * HALO))
+
+    def entry(own, column, at):
+        row = at - HALO if side == 0 else at + rows - 2 * HALO
+        if 0 <= row < rows:
+            return own(row)
+        return table[row + HALO if side == 0 else row - rows, column]
+
+    def offset(step, at):
+        return entry(lambda row: offsets[step, row], step, at).astype(jnp.int32)
+
+    def fraction(step, at):
+        return entry(lambda row: fractions[step, row], steps + step, at)
+
+    def factor(at):
+        return entry(lambda row: coefs[row], 2 * steps, at) * PER_DIFFERENCE
+
+    first_step, second_step = two_steps(offset, fraction, factor, grid, once, twice)
+    first_step(REACH * (1 - side), HALO + REACH)
+    copy.wait()
+    first_step((HALO + REACH) * side, REACH)
+    second_step(0, HALO)
+    write(lambda i: offset(1, i + HALO), twice, 0, HALO, out, side * (rows - HALO))
 
 
 SMEM = pl.BlockSpec(memory_space=pltpu.SMEM)
@@ -223,24 +209,24 @@
     )(offsets, fractions, coefs, main)
 
 
-def edges(offsets, fractions, coefs, before, after, main, done):
+def edge(side, offsets, fractions, coefs, halo, main, done):
     members, _, width = main.shape
     per = width // LANES
     return pl.pallas_call(
-        edge_kernel,
+        functools.partial(edge_kernel, side),
         out_shape=pltpu.VMEM(main.shape, jnp.float32),
-        in_specs=[SMEM] * 3 + [VMEM] * 4,
+        in_specs=[SMEM] * 3 + [VMEM] * 3,
         out_specs=VMEM,
         scratch_shapes=[
-            pltpu.VMEM((2, 3 * HALO, per, members, LANES), jnp.float32),
-            pltpu.VMEM((2, HALO + 2 * REACH, per, 2 * members, LANES), jnp.float32),
-            pltpu.VMEM((2, HALO, per, 2 * members, LANES), jnp.float32),
-            pltpu.SMEM((2, HALO, LANES), jnp.float32),
-            pltpu.SemaphoreType.DMA((2,)),
+            pltpu.VMEM((3 * HALO, per, members, LANES), jnp.float32),
+            pltpu.VMEM((HALO + 2 * REACH, per, 2 * members, LANES), jnp.float32),
+            pltpu.VMEM((HALO, per, 2 * members, LANES), jnp.float32),
+            pltpu.SMEM((HALO, LANES), jnp.float32),
+            pltpu.SemaphoreType.DMA,
         ],
-        input_output_aliases={6: 0},
+        input_output_aliases={5: 0},
         compiler_params=grant(6),
-    )(offsets, fractions, coefs, before, after, main, pltpu.with_memory_space_constraint(done, pltpu.VMEM))
+    )(offsets, fractions, coefs, halo, main, pltpu.with_memory_space_constraint(done, pltpu.VMEM))
 
 
 def owners(parts, members):
@@ -267,7 +253,8 @@
 
     before, after = from_neighbours(*edge_radii(offsets, fractions, coefs, main), devices)
     done = inner(offsets, fractions, coefs, main)
-    done = edges(offsets, fractions, coefs, before, after, main, done)
+    for side, halo in enumerate((before, after)):
+        done = edge(side, offsets, fractions, coefs, halo, main, done)
     return exchanged(done, devices).reshape(shape)
 
 

time: 79.1 us -> 80.3 us (1.015)
  Pallas kernels: 7.46 us -> 8.94 us
    pallas_call x1 -> x2, Pallas kernels: 1.84 us -> 3.32 us  [edge(): pl.pallas_call(functools.partial(edge_kernel, side), out_shape=pltpu.VMEM...]
  transfers between devices with their start and end apart: 2 -> 2, of which waited for: 0 -> 0; matrix products, arithmetic and copies ran while one was open for 0% -> 0% of each run, Pallas kernels for 6% -> 8%
where the time goes in v10:
time: 80.3 us; the launch traced here: 80.1 us
  blocking collectives  64.3 us (80%)
  Pallas kernels  8.94 us (11%)
  starting transfers between devices  5.44 us (7%)
  local copies, waits for them, and re-layouts  1.33 us (2%)
    all_to_all x2, blocking collectives, exchanged(): lax.all_to_all(blocks, ('rad', 'azi'), 0, 0, axis_index_groups=devices, t...  64.3 us
    pallas_call x1, Pallas kernels, inner(): pl.pallas_call(inner_kernel, out_shape=pltpu.VMEM(main.shape, jnp.float32...  4.98 us
    ppermute x1, starting transfers between devices, from_neighbours(): lax.ppermute(first, ('rad', 'azi'), back)  3.55 us
    pallas_call x2, Pallas kernels, edge(): pl.pallas_call(functools.partial(edge_kernel, side), out_shape=pltpu.VMEM...  3.32 us
    ppermute x1, starting transfers between devices, from_neighbours(): lax.ppermute(last, ('rad', 'azi'), forth)  1.89 us
  transfers between devices with their start and end apart: 2, of which 0 were waited for; matrix products, arithmetic and copies ran while one was open for 0% of the time, Pallas kernels for 8%

profile of v10, /device:TPU:1, one launch (start us, length us, event | category | flops | bytes accessed | tf_op | source)
XLA Modules:
  0.0 80.1 jit_solution(3231840545598547799)
XLA Ops:
  0.0 0.0 copy-start
  0.0 0.0 copy-start.1
  0.0 0.0 copy-start.2
  0.0 33.7 %all_to_all.10.main = f32[16,64,512]{2,1,0:T(8,128)S(1)} all-to-all(f32[16,64,512]{2,1,0:T(8,128)} %bitcast.3), channel_id=1, replica_groups={{0,1,2,3,4,5,6,7,8,9,10,11,12,13,14,15},{24,25,26,27,28,29,30,31,16,17,..., dimensions={0} | all-to-all | bytes 4194304 | tf_op jit(solution)/shard_map/all_to_all | solution.py:238
  33.7 0.0 copy-done
  33.7 0.0 copy-done.1
  33.7 0.0 copy-done.2
  33.7 0.6 shard_map.46
  34.4 1.9 %collective-permute-start.1 = (f32[17,4,512]{2,1,0:T(4,128)S(1)}, f32[17,4,512]{2,1,0:T(4,128)S(1)}, u32[]{:S(2)}, u32[]{:S(2)}) collective-permute-start(f32[17,4,512]{2,1,0:T(4,128)S(1)} %get-tuple-element.8), channel_id=1, source_target_pairs={{0,24},{1,25},{2,26},{3,27},{4,28},{5,29},{6,30},{7,31},{8,16},{9,... | collective-permute-start | bytes 417800 | tf_op jit(solution)/shard_map/ppermute | solution.py:244
  36.3 3.6 %collective-permute-start = (f32[17,4,512]{2,1,0:T(4,128)S(1)}, f32[17,4,512]{2,1,0:T(4,128)S(1)}, u32[]{:S(2)}, u32[]{:S(2)}) collective-permute-start(f32[17,4,512]{2,1,0:T(4,128)S(1)} %get-tuple-element.7), channel_id=1, source_target_pairs={{24,0},{25,1},{26,2},{27,3},{28,4},{29,5},{30,6},{31,7},{16,8},{17... | collective-permute-start | bytes 417800 | tf_op jit(solution)/shard_map/ppermute | solution.py:244
  39.8 5.0 %shard_map.47.given = f32[16,64,512]{2,1,0:T(8,128)S(1)} custom-call(s32[2,64]{1,0:T(2,128)S(1)} %copy-done, f32[2,64]{1,0:T(2,128)S(1)} %copy-done.1, f32[64]{0:T(128)S(1)} %copy-done.2, f32[16,64,512]{2,1,0:T(8,128)S(1)} %all_to_all.10.main), custom_call_target="tpu_custom_call" | custom-call | tf_op jit(solution)/shard_map/pallas_call | solution.py:198
  44.8 0.0 collective-permute-done.1.halo
  44.8 1.6 %shard_map.48.given = f32[16,64,512]{2,1,0:T(8,128)S(1)} custom-call(s32[2,64]{1,0:T(2,128)S(1)} %copy-done, f32[2,64]{1,0:T(2,128)S(1)} %copy-done.1, f32[64]{0:T(128)S(1)} %copy-done.2, f32[17,4,512]{2,1,0:T(4,128)S(1)} %collective-permute-done.1.halo, f32[16,64,512]{2,1,0:T(8,128)S(1)} %all_to_all.10.main, ...), custom_call_target="tpu_custom_call", output_to_operand_aliasing={{}: (5, {})} | custom-call | tf_op jit(solution)/shard_map/pallas_call | solution.py:215
  46.4 0.0 collective-permute-done.halo
  46.5 1.7 %shard_map.49 = f32[16,64,512]{2,1,0:T(8,128)S(1)} custom-call(s32[2,64]{1,0:T(2,128)S(1)} %copy-done, f32[2,64]{1,0:T(2,128)S(1)} %copy-done.1, f32[64]{0:T(128)S(1)} %copy-done.2, f32[17,4,512]{2,1,0:T(4,128)S(1)} %collective-permute-done.halo, f32[16,64,512]{2,1,0:T(8,128)S(1)} %all_to_all.10.main, ...), custom_call_target="tpu_custom_call", output_to_operand_aliasing={{}: (5, {})} | custom-call | tf_op jit(solution)/shard_map/pallas_call | solution.py:215
  48.2 30.6 %all_to_all.11 = f32[16,64,512]{2,1,0:T(8,128)S(1)} all-to-all(f32[16,64,512]{2,1,0:T(8,128)S(1)} %shard_map.49), channel_id=1, replica_groups={{0,1,2,3,4,5,6,7,8,9,10,11,12,13,14,15},{24,25,26,27,28,29,30,31,16,17,..., dimensions={0} | all-to-all | bytes 4194304 | tf_op jit(solution)/shard_map/all_to_all | solution.py:238
  78.8 1.3 %copy.10 = f32[8,2,64,512]{3,2,1,0:T(8,128)} copy(f32[8,2,64,512]{3,2,1,0:T(8,128)S(1)} %bitcast.2) | data formatting | bytes 4194304
Async XLA Ops:
  0.0 33.7 %copy-start = (s32[2,64]{1,0:T(2,128)S(1)}, s32[2,64]{1,0:T(2,128)}, u32[]{:S(2)}) copy-start(s32[2,64]{1,0:T(2,128)} %offsets.7) | copy-start | bytes 1540
  0.0 33.7 %copy-start.1 = (f32[2,64]{1,0:T(2,128)S(1)}, f32[2,64]{1,0:T(2,128)}, u32[]{:S(2)}) copy-start(f32[2,64]{1,0:T(2,128)} %fractions.7) | copy-start | bytes 1540
  0.0 33.7 %copy-start.2 = (f32[64]{0:T(128)S(1)}, f32[64]{0:T(128)}, u32[]{:S(2)}) copy-start(f32[64]{0:T(128)} %coefs.7) | copy-start | bytes 772
  34.4 10.4 %collective-permute-start.1 = (f32[17,4,512]{2,1,0:T(4,128)S(1)}, f32[17,4,512]{2,1,0:T(4,128)S(1)}, u32[]{:S(2)}, u32[]{:S(2)}) collective-permute-start(f32[17,4,512]{2,1,0:T(4,128)S(1)} %get-tuple-element.8), channel_id=1, source_target_pairs={{0,24},{1,25},{2,26},{3,27},{4,28},{5,29},{6,30},{7,31},{8,16},{9,... | collective-permute-start | bytes 417800 | tf_op jit(solution)/shard_map/ppermute | solution.py:244
  36.3 10.2 %collective-permute-start = (f32[17,4,512]{2,1,0:T(4,128)S(1)}, f32[17,4,512]{2,1,0:T(4,128)S(1)}, u32[]{:S(2)}, u32[]{:S(2)}) collective-permute-start(f32[17,4,512]{2,1,0:T(4,128)S(1)} %get-tuple-element.7), channel_id=1, source_target_pairs={{24,0},{25,1},{26,2},{27,3},{28,4},{29,5},{30,6},{31,7},{16,8},{17... | collective-permute-start | bytes 417800 | tf_op jit(solution)/shard_map/ppermute | solution.py:244

commit v11 on v9

--- a/solution.py
+++ b/solution.py
@@ -11,6 +11,7 @@
 REACH = 2
 HALO = 2 * REACH
 PER_DIFFERENCE = 1.0 / 12.0
+TILE = 8
 RELAY, FIRST, GROUP = 16, 60, 8
 
 
@@ -62,8 +63,8 @@
     lax.fori_loop(0, count // size, group, 0)
 
 
-def two_steps(offset, fraction, factor, grid, once, twice):
-    per = grid.shape[1]
+def two_steps(offset, fraction, factor, line, once, twice):
+    per = once.shape[1]
 
     def diffuse(start, size, at, number, line, out):
         rows = [[] for _ in range(size)]
@@ -76,7 +77,7 @@
             keep(out, start + u, partly_shifted(rows[u], offset(number, here), fraction(number, here)))
 
     def first_step(start, size):
-        diffuse(start, size, REACH, 0, lambda i, c: grid[i, c], once)
+        diffuse(start, size, REACH, 0, line, once)
 
     def second_step(start, size):
         diffuse(start, size, HALO, 1, lambda i, c: moved_line(once, i, offset(0, i + REACH), c), twice)
@@ -89,31 +90,35 @@
         out[:, to + i, :] = jnp.concatenate(moved(twice, start + i, offset(start + i)), axis=1)
 
 
-def load(grid, at, source, row, turn=0):
-    line = source[pl.ds(0, grid.shape[2]), row, :]
-    if turn:
-        line = jnp.concatenate([line[turn:], line[:turn]])
+def load(grid, at, source, row):
+    line = source[:, row, :]
     for c in range(grid.shape[1]):
         grid[at, c] = line[:, c * LANES : (c + 1) * LANES]
 
 
 def edge_radii_kernel(offsets, fractions, coefs, main, first, last):
     members, rows, width = main.shape
-    steps = offsets.shape[0]
+    steps, per, half = offsets.shape[0], width // LANES, members // 2
     part, parts = lax.axis_index("rad"), lax.axis_size("rad")
-    lane = lax.broadcasted_iota(jnp.int32, (1, width), 1)
+    lane = lax.broadcasted_iota(jnp.int32, (1, LANES), 1)
     for out, start, sent in ((first, 0, part > 0), (last, rows - HALO, part < parts - 1)):
-        radii = main[:, start : start + HALO]
-        out[pl.ds(0, members)] = jnp.where(sent, radii, jnp.zeros_like(radii))
+        for r in range(HALO):
+            radius = main[:, start + r, :]
+            radius = jnp.concatenate([radius[half:], radius[:half]])
+            radius = jnp.where(sent, radius, jnp.zeros_like(radius))
+            for c in range(per):
+                out[pl.ds((r * per + c) * members, members)] = radius[:, c * LANES : (c + 1) * LANES]
+        table = HALO * per * members
+        out[pl.ds(table, TILE)] = jnp.zeros((TILE, LANES), jnp.float32)
         for r in range(HALO):
             at = start + r
             entries = [offsets[step, at].astype(jnp.float32) for step in range(steps)]
             entries += [fractions[step, at] for step in range(steps)]
             entries.append(coefs[at])
-            line = jnp.zeros((1, width), jnp.float32)
+            line = jnp.zeros((1, LANES), jnp.float32)
             for column, entry in enumerate(entries):
                 line = jnp.where(lane == column, jnp.where(sent, entry, 0.0), line)
-            out[members, pl.ds(r, 1)] = line
+            out[pl.ds(table + r, 1)] = line
 
 
 def inner_kernel(offsets, fractions, coefs, main, out, grid, once, twice):
@@ -127,7 +132,7 @@
         lambda step, at: offsets[step, at],
         lambda step, at: fractions[step, at],
         lambda at: coefs[at] * PER_DIFFERENCE,
-        grid,
+        lambda i, c: grid[i, c],
         once,
         twice,
     )
@@ -140,29 +145,34 @@
 
 def edge_kernel(offsets, fractions, coefs, before, after, main, given, out, grid, once, twice, table, sems):
     del given
-    members, rows, _ = main.shape
-    steps = offsets.shape[0]
-    tables = [
-        pltpu.make_async_copy(halo.at[members, :, pl.ds(0, LANES)], table.at[side], sems.at[side])
-        for side, halo in enumerate((before, after))
+    members, rows, width = main.shape
+    steps, per = offsets.shape[0], width // LANES
+    halos = (before, after)
+    copies = [
+        pltpu.make_async_copy(halo.at[pl.ds(HALO * per * members, TILE)], table.at[side], sems.at[side])
+        for side, halo in enumerate(halos)
     ]
-    for copy in tables:
+    for copy in copies:
         copy.start()
-
-    for side, halo in enumerate((before, after)):
-        for r in range(HALO):
-            load(grid.at[side], r + side * 2 * HALO, halo, r, members // 2)
+    for side in range(2):
         for r in range(2 * HALO):
-            load(grid.at[side], r + (1 - side) * HALO, main, r + side * (rows - 2 * HALO))
-    for copy in tables:
-        copy.wait()
+            load(grid.at[side], r, main, r + side * (rows - 2 * HALO))
 
     def side_steps(side):
-        def entry(own, column, at):
-            row = at - HALO if side == 0 else at + rows - 2 * HALO
-            if 0 <= row < rows:
-                return own(row)
-            return table[side, row + HALO if side == 0 else row - rows, column]
+        def own(at):
+            return at - HALO * (1 - side)
+
+        def entry(mine, column, at):
+            row = own(at)
+            if 0 <= row < 2 * HALO:
+                return mine(row + side * (rows - 2 * HALO))
+            return table[side, at - 2 * HALO * side, column]
+
+        def line(at, c):
+            row = own(at)
+            if 0 <= row < 2 * HALO:
+                return grid[side, row, c]
+            return halos[side][pl.ds(((at - 2 * HALO * side) * per + c) * members, members)]
 
         def offset(step, at):
             return entry(lambda row: offsets[step, row], step, at).astype(jnp.int32)
@@ -173,12 +183,15 @@
         def factor(at):
             return entry(lambda row: coefs[row], 2 * steps, at) * PER_DIFFERENCE
 
-        first_step, second_step = two_steps(offset, fraction, factor, grid.at[side], once.at[side], twice.at[side])
-        return offset, first_step, second_step
+        return offset, *two_steps(offset, fraction, factor, line, once.at[side], twice.at[side])
 
     sides = [side_steps(side) for side in range(2)]
-    for _, first_step, _ in sides:
-        first_step(0, HALO + 2 * REACH)
+    for side, (_, first_step, _) in enumerate(sides):
+        first_step(REACH * (1 - side), HALO + REACH)
+    for copy in copies:
+        copy.wait()
+    for side, (_, first_step, _) in enumerate(sides):
+        first_step((HALO + REACH) * side, REACH)
     for _, _, second_step in sides:
         second_step(0, HALO)
     for side, (offset, _, _) in enumerate(sides):
@@ -196,7 +209,7 @@
 
 def edge_radii(offsets, fractions, coefs, main):
     members, _, width = main.shape
-    side = jax.ShapeDtypeStruct((members + 1, HALO, width), jnp.float32)
+    side = jax.ShapeDtypeStruct((HALO * members * width // LANES + TILE, LANES), jnp.float32)
     return pl.pallas_call(
         edge_radii_kernel,
         out_shape=[side, side],
@@ -232,10 +245,10 @@
         in_specs=[SMEM] * 3 + [VMEM] * 4,
         out_specs=VMEM,
         scratch_shapes=[
-            pltpu.VMEM((2, 3 * HALO, per, members, LANES), jnp.float32),
+            pltpu.VMEM((2, 2 * HALO, per, members, LANES), jnp.float32),
             pltpu.VMEM((2, HALO + 2 * REACH, per, 2 * members, LANES), jnp.float32),
             pltpu.VMEM((2, HALO, per, 2 * members, LANES), jnp.float32),
-            pltpu.SMEM((2, HALO, LANES), jnp.float32),
+            pltpu.SMEM((2, TILE, LANES), jnp.float32),
             pltpu.SemaphoreType.DMA((2,)),
         ],
         input_output_aliases={6: 0},

time: 79.1 us -> 79.3 us (level)
  no operation moved by 1% of the time
where the time goes in v11:
time: 79.3 us; the launch traced here: 79.1 us
  blocking collectives  64.4 us (81%)
  Pallas kernels  7.82 us (10%)
  starting transfers between devices  5.44 us (7%)
  local copies, waits for them, and re-layouts  1.33 us (2%)
    all_to_all x2, blocking collectives, exchanged(): lax.all_to_all(blocks, ('rad', 'azi'), 0, 0, axis_index_groups=devices, t...  64.4 us
    pallas_call x1, Pallas kernels, inner(): pl.pallas_call(inner_kernel, out_shape=pltpu.VMEM(main.shape, jnp.float32...  4.98 us
    ppermute x1, starting transfers between devices, from_neighbours(): lax.ppermute(first, ('rad', 'azi'), back)  3.55 us
    pallas_call x1, Pallas kernels, edges(): pl.pallas_call(edge_kernel, out_shape=pltpu.VMEM(main.shape, jnp.float32)...  2.19 us
    ppermute x1, starting transfers between devices, from_neighbours(): lax.ppermute(last, ('rad', 'azi'), forth)  1.89 us
  transfers between devices with their start and end apart: 2, of which 0 were waited for; matrix products, arithmetic and copies ran while one was open for 0% of the time, Pallas kernels for 6%

profile of v11, /device:TPU:1, one launch (start us, length us, event | category | flops | bytes accessed | tf_op | source)
XLA Modules:
  0.0 79.1 jit_solution(6225764625690001153)
XLA Ops:
  0.0 0.0 copy-start
  0.0 0.0 copy-start.1
  0.0 0.0 copy-start.2
  0.0 33.7 %all_to_all.10.main = f32[16,64,512]{2,1,0:T(8,128)S(1)} all-to-all(f32[16,64,512]{2,1,0:T(8,128)} %bitcast.3), channel_id=1, replica_groups={{0,1,2,3,4,5,6,7,8,9,10,11,12,13,14,15},{24,25,26,27,28,29,30,31,16,17,..., dimensions={0} | all-to-all | bytes 4194304 | tf_op jit(solution)/shard_map/all_to_all | solution.py:265
  33.7 0.0 copy-done
  33.7 0.0 copy-done.1
  33.7 0.0 copy-done.2
  33.7 0.6 shard_map.46
  34.4 1.9 %collective-permute-start = (f32[264,128]{1,0:T(8,128)S(1)}, f32[264,128]{1,0:T(8,128)S(1)}, u32[]{:S(2)}, u32[]{:S(2)}) collective-permute-start(f32[264,128]{1,0:T(8,128)S(1)} %get-tuple-element.7), channel_id=1, source_target_pairs={{0,24},{1,25},{2,26},{3,27},{4,28},{5,29},{6,30},{7,31},{8,16},{9,... | collective-permute-start | bytes 405512 | tf_op jit(solution)/shard_map/ppermute | solution.py:271
  36.3 3.6 %collective-permute-start.1 = (f32[264,128]{1,0:T(8,128)S(1)}, f32[264,128]{1,0:T(8,128)S(1)}, u32[]{:S(2)}, u32[]{:S(2)}) collective-permute-start(f32[264,128]{1,0:T(8,128)S(1)} %get-tuple-element.8), channel_id=1, source_target_pairs={{24,0},{25,1},{26,2},{27,3},{28,4},{29,5},{30,6},{31,7},{16,8},{17... | collective-permute-start | bytes 405512 | tf_op jit(solution)/shard_map/ppermute | solution.py:271
  39.8 5.0 %shard_map.47.given = f32[16,64,512]{2,1,0:T(8,128)S(1)} custom-call(s32[2,64]{1,0:T(2,128)S(1)} %copy-done, f32[2,64]{1,0:T(2,128)S(1)} %copy-done.1, f32[64]{0:T(128)S(1)} %copy-done.2, f32[16,64,512]{2,1,0:T(8,128)S(1)} %all_to_all.10.main), custom_call_target="tpu_custom_call" | custom-call | tf_op jit(solution)/shard_map/pallas_call | solution.py:225
  44.8 0.0 collective-permute-done.before
  44.8 0.0 collective-permute-done.1.after
  44.8 2.2 %shard_map.48 = f32[16,64,512]{2,1,0:T(8,128)S(1)} custom-call(s32[2,64]{1,0:T(2,128)S(1)} %copy-done, f32[2,64]{1,0:T(2,128)S(1)} %copy-done.1, f32[64]{0:T(128)S(1)} %copy-done.2, f32[264,128]{1,0:T(8,128)S(1)} %collective-permute-done.before, f32[264,128]{1,0:T(8,128)S(1)} %collective-permute-done.1.after, ...), custom_call_target="tpu_custom_call", output_to_operand_aliasing={{}: (6, {})} | custom-call | tf_op jit(solution)/shard_map/pallas_call | solution.py:242
  47.0 30.7 %all_to_all.11 = f32[16,64,512]{2,1,0:T(8,128)S(1)} all-to-all(f32[16,64,512]{2,1,0:T(8,128)S(1)} %shard_map.48), channel_id=1, replica_groups={{0,1,2,3,4,5,6,7,8,9,10,11,12,13,14,15},{24,25,26,27,28,29,30,31,16,17,..., dimensions={0} | all-to-all | bytes 4194304 | tf_op jit(solution)/shard_map/all_to_all | solution.py:265
  77.8 1.3 %copy.8 = f32[8,2,64,512]{3,2,1,0:T(8,128)} copy(f32[8,2,64,512]{3,2,1,0:T(8,128)S(1)} %bitcast.2) | data formatting | bytes 4194304
Async XLA Ops:
  0.0 33.7 %copy-start = (s32[2,64]{1,0:T(2,128)S(1)}, s32[2,64]{1,0:T(2,128)}, u32[]{:S(2)}) copy-start(s32[2,64]{1,0:T(2,128)} %offsets.5) | copy-start | bytes 1540
  0.0 33.7 %copy-start.1 = (f32[2,64]{1,0:T(2,128)S(1)}, f32[2,64]{1,0:T(2,128)}, u32[]{:S(2)}) copy-start(f32[2,64]{1,0:T(2,128)} %fractions.5) | copy-start | bytes 1540
  0.0 33.7 %copy-start.2 = (f32[64]{0:T(128)S(1)}, f32[64]{0:T(128)}, u32[]{:S(2)}) copy-start(f32[64]{0:T(128)} %coefs.5) | copy-start | bytes 772
  34.4 10.4 %collective-permute-start = (f32[264,128]{1,0:T(8,128)S(1)}, f32[264,128]{1,0:T(8,128)S(1)}, u32[]{:S(2)}, u32[]{:S(2)}) collective-permute-start(f32[264,128]{1,0:T(8,128)S(1)} %get-tuple-element.7), channel_id=1, source_target_pairs={{0,24},{1,25},{2,26},{3,27},{4,28},{5,29},{6,30},{7,31},{8,16},{9,... | collective-permute-start | bytes 405512 | tf_op jit(solution)/shard_map/ppermute | solution.py:271
  36.3 8.6 %collective-permute-start.1 = (f32[264,128]{1,0:T(8,128)S(1)}, f32[264,128]{1,0:T(8,128)S(1)}, u32[]{:S(2)}, u32[]{:S(2)}) collective-permute-start(f32[264,128]{1,0:T(8,128)S(1)} %get-tuple-element.8), channel_id=1, source_target_pairs={{24,0},{25,1},{26,2},{27,3},{28,4},{29,5},{30,6},{31,7},{16,8},{17... | collective-permute-start | bytes 405512 | tf_op jit(solution)/shard_map/ppermute | solution.py:271

commit v12 on v9

--- a/solution.py
+++ b/solution.py
@@ -97,12 +97,19 @@
         grid[at, c] = line[:, c * LANES : (c + 1) * LANES]
 
 
-def edge_radii_kernel(offsets, fractions, coefs, main, first, last):
+def by_parity(even, odd):
+    parity = lax.axis_index("rad") & 1
+    pl.when(parity == 0)(even)
+    pl.when(parity == 1)(odd)
+
+
+def edge_radii_kernel(offsets, fractions, coefs, main, one, two):
     members, rows, width = main.shape
     steps = offsets.shape[0]
     part, parts = lax.axis_index("rad"), lax.axis_size("rad")
     lane = lax.broadcasted_iota(jnp.int32, (1, width), 1)
-    for out, start, sent in ((first, 0, part > 0), (last, rows - HALO, part < parts - 1)):
+
+    def fill(out, start, sent):
         radii = main[:, start : start + HALO]
         out[pl.ds(0, members)] = jnp.where(sent, radii, jnp.zeros_like(radii))
         for r in range(HALO):
@@ -114,6 +121,12 @@
             for column, entry in enumerate(entries):
                 line = jnp.where(lane == column, jnp.where(sent, entry, 0.0), line)
             out[members, pl.ds(r, 1)] = line
+
+    def fill_both(first, last):
+        fill(first, 0, part > 0)
+        fill(last, rows - HALO, part < parts - 1)
+
+    by_parity(lambda: fill_both(two, one), lambda: fill_both(one, two))
 
 
 def inner_kernel(offsets, fractions, coefs, main, out, grid, once, twice):
@@ -138,24 +151,28 @@
         write(lambda i: offsets[1, i + HALO], twice, lo - HALO, GROUP, out, lo)
 
 
-def edge_kernel(offsets, fractions, coefs, before, after, main, given, out, grid, once, twice, table, sems):
+def edge_kernel(offsets, fractions, coefs, one, two, main, given, out, grid, once, twice, table, sems):
     del given
     members, rows, _ = main.shape
     steps = offsets.shape[0]
-    tables = [
-        pltpu.make_async_copy(halo.at[members, :, pl.ds(0, LANES)], table.at[side], sems.at[side])
-        for side, halo in enumerate((before, after))
-    ]
-    for copy in tables:
-        copy.start()
-
-    for side, halo in enumerate((before, after)):
-        for r in range(HALO):
-            load(grid.at[side], r + side * 2 * HALO, halo, r, members // 2)
+
+    def table_copy(side, halo):
+        return pltpu.make_async_copy(halo.at[members, :, pl.ds(0, LANES)], table.at[side], sems.at[side])
+
+    def take(before, after):
+        halos = (before, after)
+        for side, halo in enumerate(halos):
+            table_copy(side, halo).start()
+        for side, halo in enumerate(halos):
+            for r in range(HALO):
+                load(grid.at[side], r + side * 2 * HALO, halo, r, members // 2)
+
+    by_parity(lambda: take(two, one), lambda: take(one, two))
+    for side in range(2):
         for r in range(2 * HALO):
             load(grid.at[side], r + (1 - side) * HALO, main, r + side * (rows - 2 * HALO))
-    for copy in tables:
-        copy.wait()
+    for side in range(2):
+        table_copy(side, one).wait()
 
     def side_steps(side):
         def entry(own, column, at):
@@ -223,7 +240,7 @@
     )(offsets, fractions, coefs, main)
 
 
-def edges(offsets, fractions, coefs, before, after, main, done):
+def edges(offsets, fractions, coefs, one, two, main, done):
     members, _, width = main.shape
     per = width // LANES
     return pl.pallas_call(
@@ -240,7 +257,7 @@
         ],
         input_output_aliases={6: 0},
         compiler_params=grant(6),
-    )(offsets, fractions, coefs, before, after, main, pltpu.with_memory_space_constraint(done, pltpu.VMEM))
+    )(offsets, fractions, coefs, one, two, main, pltpu.with_memory_space_constraint(done, pltpu.VMEM))
 
 
 def owners(parts, members):
@@ -252,10 +269,14 @@
     return lax.all_to_all(blocks, ("rad", "azi"), 0, 0, axis_index_groups=devices, tiled=True)
 
 
-def from_neighbours(first, last, devices):
-    forth = [pair for part, after in zip(devices, devices[1:] + devices[:1]) for pair in zip(part, after)]
-    back = [(j, i) for i, j in forth]
-    return lax.ppermute(last, ("rad", "azi"), forth), lax.ppermute(first, ("rad", "azi"), back)
+def swapped(one, two, devices):
+    after = devices[1:] + devices[:1]
+
+    def partners(start):
+        pairs = [pair for a, b in zip(devices[start::2], after[start::2]) for pair in zip(a, b)]
+        return pairs + [(b, a) for a, b in pairs]
+
+    return lax.ppermute(one, ("rad", "azi"), partners(0)), lax.ppermute(two, ("rad", "azi"), partners(1))
 
 
 def shards(fields, offsets, fractions, coefs):
@@ -265,9 +286,9 @@
     devices = owners(lax.axis_size("rad"), lax.axis_size("azi"))
     main = exchanged(blocks, devices)
 
-    before, after = from_neighbours(*edge_radii(offsets, fractions, coefs, main), devices)
+    one, two = swapped(*edge_radii(offsets, fractions, coefs, main), devices)
     done = inner(offsets, fractions, coefs, main)
-    done = edges(offsets, fractions, coefs, before, after, main, done)
+    done = edges(offsets, fractions, coefs, one, two, main, done)
     return exchanged(done, devices).reshape(shape)
 
 

time: 79.1 us -> 81.3 us (1.028)
  blocking collectives: 64.6 us -> 65.8 us
    all_to_all x2, blocking collectives: 64.6 us -> 65.8 us  [exchanged(): lax.all_to_all(blocks, ('rad', 'azi'), 0, 0, axis_index_groups=devices, t...]
  transfers between devices with their start and end apart: 2 -> 2, of which waited for: 0 -> 1; matrix products, arithmetic and copies ran while one was open for 0% -> 0% of each run, Pallas kernels for 6% -> 6%
where the time goes in v12:
time: 81.3 us; the launch traced here: 81.1 us
  blocking collectives  65.8 us (81%)
  Pallas kernels  7.47 us (9%)
  starting transfers between devices  6.23 us (8%)
  local copies, waits for them, and re-layouts  1.33 us (2%)
    all_to_all x2, blocking collectives, exchanged(): lax.all_to_all(blocks, ('rad', 'azi'), 0, 0, axis_index_groups=devices, t...  65.8 us
    pallas_call x1, Pallas kernels, inner(): pl.pallas_call(inner_kernel, out_shape=pltpu.VMEM(main.shape, jnp.float32...  4.98 us
    ppermute x1, starting transfers between devices, swapped(): lax.ppermute(two, ('rad', 'azi'), partners(1))  4.33 us
    ppermute x1, starting transfers between devices, swapped(): lax.ppermute(one, ('rad', 'azi'), partners(0))  1.9 us
    pallas_call x1, Pallas kernels, edges(): pl.pallas_call(edge_kernel, out_shape=pltpu.VMEM(main.shape, jnp.float32)...  1.85 us
  transfers between devices with their start and end apart: 2, of which 1 were waited for; matrix products, arithmetic and copies ran while one was open for 0% of the time, Pallas kernels for 6%

profile of v12, /device:TPU:1, one launch (start us, length us, event | category | flops | bytes accessed | tf_op | source)
XLA Modules:
  0.0 81.1 jit_solution(102049107714692105)
XLA Ops:
  0.0 0.0 copy-start
  0.0 0.0 copy-start.1
  0.0 0.0 copy-start.2
  0.0 33.7 %all_to_all.10.main = f32[16,64,512]{2,1,0:T(8,128)S(1)} all-to-all(f32[16,64,512]{2,1,0:T(8,128)} %bitcast.3), channel_id=1, replica_groups={{0,1,2,3,4,5,6,7,8,9,10,11,12,13,14,15},{24,25,26,27,28,29,30,31,16,17,..., dimensions={0} | all-to-all | bytes 4194304 | tf_op jit(solution)/shard_map/all_to_all | solution.py:269
  33.7 0.0 copy-done
  33.7 0.0 copy-done.1
  33.7 0.0 copy-done.2
  33.7 0.6 shard_map.46
  34.4 1.9 %collective-permute-start = (f32[17,4,512]{2,1,0:T(4,128)S(1)}, f32[17,4,512]{2,1,0:T(4,128)S(1)}, u32[]{:S(2)}, u32[]{:S(2)}) collective-permute-start(f32[17,4,512]{2,1,0:T(4,128)S(1)} %get-tuple-element.7), channel_id=1, source_target_pairs={{0,24},{1,25},{2,26},{3,27},{4,28},{5,29},{6,30},{7,31},{8,16},{9,... | collective-permute-start | bytes 417800 | tf_op jit(solution)/shard_map/ppermute | solution.py:279
  36.3 4.3 %collective-permute-start.1 = (f32[17,4,512]{2,1,0:T(4,128)S(1)}, f32[17,4,512]{2,1,0:T(4,128)S(1)}, u32[]{:S(2)}, u32[]{:S(2)}) collective-permute-start(f32[17,4,512]{2,1,0:T(4,128)S(1)} %get-tuple-element.8), channel_id=1, source_target_pairs={{24,32},{25,33},{26,34},{27,35},{28,36},{29,37},{30,38},{31,39},{1... | collective-permute-start | bytes 417800 | tf_op jit(solution)/shard_map/ppermute | solution.py:279
  40.6 5.0 %shard_map.47.given = f32[16,64,512]{2,1,0:T(8,128)S(1)} custom-call(s32[2,64]{1,0:T(2,128)S(1)} %copy-done, f32[2,64]{1,0:T(2,128)S(1)} %copy-done.1, f32[64]{0:T(128)S(1)} %copy-done.2, f32[16,64,512]{2,1,0:T(8,128)S(1)} %all_to_all.10.main), custom_call_target="tpu_custom_call" | custom-call | tf_op jit(solution)/shard_map/pallas_call | solution.py:229
  45.6 0.0 collective-permute-done.one
  45.6 0.2 collective-permute-done.1.two
  45.8 1.8 %shard_map.48 = f32[16,64,512]{2,1,0:T(8,128)S(1)} custom-call(s32[2,64]{1,0:T(2,128)S(1)} %copy-done, f32[2,64]{1,0:T(2,128)S(1)} %copy-done.1, f32[64]{0:T(128)S(1)} %copy-done.2, f32[17,4,512]{2,1,0:T(4,128)S(1)} %collective-permute-done.one, f32[17,4,512]{2,1,0:T(4,128)S(1)} %collective-permute-done.1.two, ...), custom_call_target="tpu_custom_call", output_to_operand_aliasing={{}: (6, {})} | custom-call | tf_op jit(solution)/shard_map/pallas_call | solution.py:246
  47.7 32.0 %all_to_all.11 = f32[16,64,512]{2,1,0:T(8,128)S(1)} all-to-all(f32[16,64,512]{2,1,0:T(8,128)S(1)} %shard_map.48), channel_id=1, replica_groups={{0,1,2,3,4,5,6,7,8,9,10,11,12,13,14,15},{24,25,26,27,28,29,30,31,16,17,..., dimensions={0} | all-to-all | bytes 4194304 | tf_op jit(solution)/shard_map/all_to_all | solution.py:269
  79.7 1.3 %copy.8 = f32[8,2,64,512]{3,2,1,0:T(8,128)} copy(f32[8,2,64,512]{3,2,1,0:T(8,128)S(1)} %bitcast.2) | data formatting | bytes 4194304
Async XLA Ops:
  0.0 33.7 %copy-start = (s32[2,64]{1,0:T(2,128)S(1)}, s32[2,64]{1,0:T(2,128)}, u32[]{:S(2)}) copy-start(s32[2,64]{1,0:T(2,128)} %offsets.5) | copy-start | bytes 1540
  0.0 33.7 %copy-start.1 = (f32[2,64]{1,0:T(2,128)S(1)}, f32[2,64]{1,0:T(2,128)}, u32[]{:S(2)}) copy-start(f32[2,64]{1,0:T(2,128)} %fractions.5) | copy-start | bytes 1540
  0.0 33.7 %copy-start.2 = (f32[64]{0:T(128)S(1)}, f32[64]{0:T(128)}, u32[]{:S(2)}) copy-start(f32[64]{0:T(128)} %coefs.5) | copy-start | bytes 772
  34.4 11.2 %collective-permute-start = (f32[17,4,512]{2,1,0:T(4,128)S(1)}, f32[17,4,512]{2,1,0:T(4,128)S(1)}, u32[]{:S(2)}, u32[]{:S(2)}) collective-permute-start(f32[17,4,512]{2,1,0:T(4,128)S(1)} %get-tuple-element.7), channel_id=1, source_target_pairs={{0,24},{1,25},{2,26},{3,27},{4,28},{5,29},{6,30},{7,31},{8,16},{9,... | collective-permute-start | bytes 417800 | tf_op jit(solution)/shard_map/ppermute | solution.py:279
  36.3 9.6 %collective-permute-start.1 = (f32[17,4,512]{2,1,0:T(4,128)S(1)}, f32[17,4,512]{2,1,0:T(4,128)S(1)}, u32[]{:S(2)}, u32[]{:S(2)}) collective-permute-start(f32[17,4,512]{2,1,0:T(4,128)S(1)} %get-tuple-element.8), channel_id=1, source_target_pairs={{24,32},{25,33},{26,34},{27,35},{28,36},{29,37},{30,38},{31,39},{1... | collective-permute-start | bytes 417800 | tf_op jit(solution)/shard_map/ppermute | solution.py:279

commit v13 on v11

--- a/solution.py
+++ b/solution.py
@@ -63,7 +63,7 @@
     lax.fori_loop(0, count // size, group, 0)
 
 
-def two_steps(offset, fraction, factor, line, once, twice):
+def two_steps(offset, fraction, factor, line, once, twice, kept):
     per = once.shape[1]
 
     def diffuse(start, size, at, number, line, out):
@@ -80,7 +80,7 @@
         diffuse(start, size, REACH, 0, line, once)
 
     def second_step(start, size):
-        diffuse(start, size, HALO, 1, lambda i, c: moved_line(once, i, offset(0, i + REACH), c), twice)
+        diffuse(start, size, HALO, 1, lambda i, c: moved_line(*kept(i), offset(0, i + REACH), c), twice)
 
     return first_step, second_step
 
@@ -121,7 +121,7 @@
             out[pl.ds(table + r, 1)] = line
 
 
-def inner_kernel(offsets, fractions, coefs, main, out, grid, once, twice):
+def inner_kernel(offsets, fractions, coefs, main, out, near, stepped, grid, once, twice):
     rows = main.shape[1]
 
     def relay(start, size):
@@ -135,17 +135,24 @@
         lambda i, c: grid[i, c],
         once,
         twice,
+        lambda i: (once, i),
     )
     in_groups(rows, RELAY, relay)
+    for r in range(HALO):
+        near[0, r] = grid[r]
+        near[1, r] = grid[rows - HALO + r]
     in_groups(rows - 2 * REACH, FIRST, first_step)
+    for r in range(HALO):
+        stepped[0, r] = once[r]
+        stepped[1, r] = once[rows - 2 * REACH - HALO + r]
     for lo in range(HALO, rows - HALO, GROUP):
         second_step(lo - HALO, GROUP)
         write(lambda i: offsets[1, i + HALO], twice, lo - HALO, GROUP, out, lo)
 
 
-def edge_kernel(offsets, fractions, coefs, before, after, main, given, out, grid, once, twice, table, sems):
+def edge_kernel(offsets, fractions, coefs, before, after, near, stepped, given, out, once, twice, table, sems):
     del given
-    members, rows, width = main.shape
+    members, rows, width = out.shape
     steps, per = offsets.shape[0], width // LANES
     halos = (before, after)
     copies = [
@@ -154,9 +161,6 @@
     ]
     for copy in copies:
         copy.start()
-    for side in range(2):
-        for r in range(2 * HALO):
-            load(grid.at[side], r, main, r + side * (rows - 2 * HALO))
 
     def side_steps(side):
         def own(at):
@@ -171,8 +175,12 @@
         def line(at, c):
             row = own(at)
             if 0 <= row < 2 * HALO:
-                return grid[side, row, c]
+                return near[side, row - side * HALO, c]
             return halos[side][pl.ds(((at - 2 * HALO * side) * per + c) * members, members)]
+
+        def kept(i):
+            inward = i >= HALO if side == 0 else i < HALO
+            return (stepped.at[side], i % HALO) if inward else (once.at[side], i)
 
         def offset(step, at):
             return entry(lambda row: offsets[step, row], step, at).astype(jnp.int32)
@@ -183,15 +191,13 @@
         def factor(at):
             return entry(lambda row: coefs[row], 2 * steps, at) * PER_DIFFERENCE
 
-        return offset, *two_steps(offset, fraction, factor, line, once.at[side], twice.at[side])
+        return offset, *two_steps(offset, fraction, factor, line, once.at[side], twice.at[side], kept)
 
     sides = [side_steps(side) for side in range(2)]
-    for side, (_, first_step, _) in enumerate(sides):
-        first_step(REACH * (1 - side), HALO + REACH)
     for copy in copies:
         copy.wait()
     for side, (_, first_step, _) in enumerate(sides):
-        first_step((HALO + REACH) * side, REACH)
+        first_step(side * HALO, HALO)
     for _, _, second_step in sides:
         second_step(0, HALO)
     for side, (offset, _, _) in enumerate(sides):
@@ -224,9 +230,13 @@
     per = width // LANES
     return pl.pallas_call(
         inner_kernel,
-        out_shape=pltpu.VMEM(main.shape, jnp.float32),
+        out_shape=[
+            pltpu.VMEM(main.shape, jnp.float32),
+            pltpu.VMEM((2, HALO, per, members, LANES), jnp.float32),
+            pltpu.VMEM((2, HALO, per, 2 * members, LANES), jnp.float32),
+        ],
         in_specs=[SMEM] * 3 + [VMEM],
-        out_specs=VMEM,
+        out_specs=[VMEM] * 3,
         scratch_shapes=[
             pltpu.VMEM((rows, per, members, LANES), jnp.float32),
             pltpu.VMEM((rows - 2 * REACH, per, 2 * members, LANES), jnp.float32),
@@ -236,24 +246,24 @@
     )(offsets, fractions, coefs, main)
 
 
-def edges(offsets, fractions, coefs, before, after, main, done):
-    members, _, width = main.shape
+def edges(offsets, fractions, coefs, before, after, done, near, stepped):
+    members, _, width = done.shape
     per = width // LANES
+    near, stepped, done = (pltpu.with_memory_space_constraint(part, pltpu.VMEM) for part in (near, stepped, done))
     return pl.pallas_call(
         edge_kernel,
-        out_shape=pltpu.VMEM(main.shape, jnp.float32),
-        in_specs=[SMEM] * 3 + [VMEM] * 4,
+        out_shape=pltpu.VMEM(done.shape, jnp.float32),
+        in_specs=[SMEM] * 3 + [VMEM] * 5,
         out_specs=VMEM,
         scratch_shapes=[
-            pltpu.VMEM((2, 2 * HALO, per, members, LANES), jnp.float32),
             pltpu.VMEM((2, HALO + 2 * REACH, per, 2 * members, LANES), jnp.float32),
             pltpu.VMEM((2, HALO, per, 2 * members, LANES), jnp.float32),
             pltpu.SMEM((2, TILE, LANES), jnp.float32),
             pltpu.SemaphoreType.DMA((2,)),
         ],
-        input_output_aliases={6: 0},
+        input_output_aliases={7: 0},
         compiler_params=grant(6),
-    )(offsets, fractions, coefs, before, after, main, pltpu.with_memory_space_constraint(done, pltpu.VMEM))
+    )(offsets, fractions, coefs, before, after, near, stepped, done)
 
 
 def owners(parts, members):
@@ -280,7 +290,7 @@
 
     before, after = from_neighbours(*edge_radii(offsets, fractions, coefs, main), devices)
     done = inner(offsets, fractions, coefs, main)
-    done = edges(offsets, fractions, coefs, before, after, main, done)
+    done = edges(offsets, fractions, coefs, before, after, *done)
     return exchanged(done, devices).reshape(shape)
 
 

time: 79.3 us -> 78.9 us (level)
  no operation moved by 1% of the time
where the time goes in v13:
time: 78.9 us; the launch traced here: 78.7 us
  blocking collectives  64.4 us (82%)
  Pallas kernels  7.4 us (9%)
  starting transfers between devices  5.44 us (7%)
  local copies, waits for them, and re-layouts  1.33 us (2%)
    all_to_all x2, blocking collectives, exchanged(): lax.all_to_all(blocks, ('rad', 'azi'), 0, 0, axis_index_groups=devices, t...  64.4 us
    pallas_call x1, Pallas kernels, inner(): pl.pallas_call(inner_kernel, out_shape=[pltpu.VMEM(main.shape, jnp.float3...  4.99 us
    ppermute x1, starting transfers between devices, from_neighbours(): lax.ppermute(first, ('rad', 'azi'), back)  3.55 us
    ppermute x1, starting transfers between devices, from_neighbours(): lax.ppermute(last, ('rad', 'azi'), forth)  1.89 us
    pallas_call x1, Pallas kernels, edges(): pl.pallas_call(edge_kernel, out_shape=pltpu.VMEM(done.shape, jnp.float32)...  1.77 us
  transfers between devices with their start and end apart: 2, of which 0 were waited for; matrix products, arithmetic and copies ran while one was open for 0% of the time, Pallas kernels for 6%

profile of v13, /device:TPU:1, one launch (start us, length us, event | category | flops | bytes accessed | tf_op | source)
XLA Modules:
  0.0 78.7 jit_solution(16844073957598157822)
XLA Ops:
  0.0 0.0 copy-start
  0.0 0.0 copy-start.1
  0.0 0.0 copy-start.2
  0.0 33.7 %all_to_all.10.main = f32[16,64,512]{2,1,0:T(8,128)S(1)} all-to-all(f32[16,64,512]{2,1,0:T(8,128)} %bitcast.3), channel_id=1, replica_groups={{0,1,2,3,4,5,6,7,8,9,10,11,12,13,14,15},{24,25,26,27,28,29,30,31,16,17,..., dimensions={0} | all-to-all | bytes 4194304 | tf_op jit(solution)/shard_map/all_to_all | solution.py:275
  33.7 0.0 copy-done
  33.7 0.0 copy-done.1
  33.7 0.0 copy-done.2
  33.7 0.6 shard_map.46
  34.4 1.9 %collective-permute-start = (f32[264,128]{1,0:T(8,128)S(1)}, f32[264,128]{1,0:T(8,128)S(1)}, u32[]{:S(2)}, u32[]{:S(2)}) collective-permute-start(f32[264,128]{1,0:T(8,128)S(1)} %get-tuple-element.10), channel_id=1, source_target_pairs={{0,24},{1,25},{2,26},{3,27},{4,28},{5,29},{6,30},{7,31},{8,16},{9,... | collective-permute-start | bytes 405512 | tf_op jit(solution)/shard_map/ppermute | solution.py:281
  36.3 3.6 %collective-permute-start.1 = (f32[264,128]{1,0:T(8,128)S(1)}, f32[264,128]{1,0:T(8,128)S(1)}, u32[]{:S(2)}, u32[]{:S(2)}) collective-permute-start(f32[264,128]{1,0:T(8,128)S(1)} %get-tuple-element.11), channel_id=1, source_target_pairs={{24,0},{25,1},{26,2},{27,3},{28,4},{29,5},{30,6},{31,7},{16,8},{17... | collective-permute-start | bytes 405512 | tf_op jit(solution)/shard_map/ppermute | solution.py:281
  39.8 5.0 %shard_map.47 = (f32[16,64,512]{2,1,0:T(8,128)S(1)}, f32[2,4,4,16,128]{4,3,2,1,0:T(8,128)S(1)}, f32[2,4,4,32,128]{4,3,2,1,0:T(8,128)S(1)}) custom-call(s32[2,64]{1,0:T(2,128)S(1)} %copy-done, f32[2,64]{1,0:T(2,128)S(1)} %copy-done.1, f32[64]{0:T(128)S(1)} %copy-done.2, f32[16,64,512]{2,1,0:T(8,128)S(1)} %all_to_all.10.main), custom_call_target="tpu_custom_call" | custom-call | tf_op jit(solution)/shard_map/pallas_call | solution.py:231
  44.8 0.0 collective-permute-done.before
  44.8 0.0 collective-permute-done.1.after
  44.8 1.8 %shard_map.48 = f32[16,64,512]{2,1,0:T(8,128)S(1)} custom-call(s32[2,64]{1,0:T(2,128)S(1)} %copy-done, f32[2,64]{1,0:T(2,128)S(1)} %copy-done.1, f32[64]{0:T(128)S(1)} %copy-done.2, f32[264,128]{1,0:T(8,128)S(1)} %collective-permute-done.before, f32[264,128]{1,0:T(8,128)S(1)} %collective-permute-done.1.after, ...), custom_call_target="tpu_custom_call", output_to_operand_aliasing={{}: (7, {})} | custom-call | tf_op jit(solution)/shard_map/pallas_call | solution.py:253
  46.6 30.7 %all_to_all.11 = f32[16,64,512]{2,1,0:T(8,128)S(1)} all-to-all(f32[16,64,512]{2,1,0:T(8,128)S(1)} %shard_map.48), channel_id=1, replica_groups={{0,1,2,3,4,5,6,7,8,9,10,11,12,13,14,15},{24,25,26,27,28,29,30,31,16,17,..., dimensions={0} | all-to-all | bytes 4194304 | tf_op jit(solution)/shard_map/all_to_all | solution.py:275
  77.3 1.3 %copy.8 = f32[8,2,64,512]{3,2,1,0:T(8,128)} copy(f32[8,2,64,512]{3,2,1,0:T(8,128)S(1)} %bitcast.2) | data formatting | bytes 4194304
Async XLA Ops:
  0.0 33.7 %copy-start = (s32[2,64]{1,0:T(2,128)S(1)}, s32[2,64]{1,0:T(2,128)}, u32[]{:S(2)}) copy-start(s32[2,64]{1,0:T(2,128)} %offsets.5) | copy-start | bytes 1540
  0.0 33.7 %copy-start.1 = (f32[2,64]{1,0:T(2,128)S(1)}, f32[2,64]{1,0:T(2,128)}, u32[]{:S(2)}) copy-start(f32[2,64]{1,0:T(2,128)} %fractions.5) | copy-start | bytes 1540
  0.0 33.7 %copy-start.2 = (f32[64]{0:T(128)S(1)}, f32[64]{0:T(128)}, u32[]{:S(2)}) copy-start(f32[64]{0:T(128)} %coefs.5) | copy-start | bytes 772
  34.4 10.4 %collective-permute-start = (f32[264,128]{1,0:T(8,128)S(1)}, f32[264,128]{1,0:T(8,128)S(1)}, u32[]{:S(2)}, u32[]{:S(2)}) collective-permute-start(f32[264,128]{1,0:T(8,128)S(1)} %get-tuple-element.10), channel_id=1, source_target_pairs={{0,24},{1,25},{2,26},{3,27},{4,28},{5,29},{6,30},{7,31},{8,16},{9,... | collective-permute-start | bytes 405512 | tf_op jit(solution)/shard_map/ppermute | solution.py:281
  36.3 8.6 %collective-permute-start.1 = (f32[264,128]{1,0:T(8,128)S(1)}, f32[264,128]{1,0:T(8,128)S(1)}, u32[]{:S(2)}, u32[]{:S(2)}) collective-permute-start(f32[264,128]{1,0:T(8,128)S(1)} %get-tuple-element.11), channel_id=1, source_target_pairs={{24,0},{25,1},{26,2},{27,3},{28,4},{29,5},{30,6},{31,7},{16,8},{17... | collective-permute-start | bytes 405512 | tf_op jit(solution)/shard_map/ppermute | solution.py:281

commit v14 on v13

--- a/solution.py
+++ b/solution.py
@@ -150,27 +150,26 @@
         write(lambda i: offsets[1, i + HALO], twice, lo - HALO, GROUP, out, lo)
 
 
-def edge_kernel(offsets, fractions, coefs, before, after, near, stepped, given, out, once, twice, table, sems):
+def edge_kernel(offsets, fractions, coefs, before, after, near, stepped, given, out, once, twice):
     del given
     members, rows, width = out.shape
     steps, per = offsets.shape[0], width // LANES
     halos = (before, after)
-    copies = [
-        pltpu.make_async_copy(halo.at[pl.ds(HALO * per * members, TILE)], table.at[side], sems.at[side])
-        for side, halo in enumerate(halos)
-    ]
-    for copy in copies:
-        copy.start()
+    tables = [halo[pl.ds(HALO * per * members, TILE)] for halo in halos]
 
     def side_steps(side):
         def own(at):
             return at - HALO * (1 - side)
+
+        taken = {}
 
         def entry(mine, column, at):
             row = own(at)
             if 0 <= row < 2 * HALO:
                 return mine(row + side * (rows - 2 * HALO))
-            return table[side, at - 2 * HALO * side, column]
+            if (column, at) not in taken:
+                taken[column, at] = tables[side][at - 2 * HALO * side, column]
+            return taken[column, at]
 
         def line(at, c):
             row = own(at)
@@ -194,8 +193,6 @@
         return offset, *two_steps(offset, fraction, factor, line, once.at[side], twice.at[side], kept)
 
     sides = [side_steps(side) for side in range(2)]
-    for copy in copies:
-        copy.wait()
     for side, (_, first_step, _) in enumerate(sides):
         first_step(side * HALO, HALO)
     for _, _, second_step in sides:
@@ -258,8 +255,6 @@
         scratch_shapes=[
             pltpu.VMEM((2, HALO + 2 * REACH, per, 2 * members, LANES), jnp.float32),
             pltpu.VMEM((2, HALO, per, 2 * members, LANES), jnp.float32),
-            pltpu.SMEM((2, TILE, LANES), jnp.float32),
-            pltpu.SemaphoreType.DMA((2,)),
         ],
         input_output_aliases={7: 0},
         compiler_params=grant(6),

time: 78.9 us -> 78.3 us (level)
  no operation moved by 1% of the time
where the time goes in v14:
time: 78.3 us; the launch traced here: 78.1 us
  blocking collectives  64.4 us (82%)
  Pallas kernels  6.86 us (9%)
  starting transfers between devices  5.44 us (7%)
  local copies, waits for them, and re-layouts  1.33 us (2%)
    all_to_all x2, blocking collectives, exchanged(): lax.all_to_all(blocks, ('rad', 'azi'), 0, 0, axis_index_groups=devices, t...  64.4 us
    pallas_call x1, Pallas kernels, inner(): pl.pallas_call(inner_kernel, out_shape=[pltpu.VMEM(main.shape, jnp.float3...  5 us
    ppermute x1, starting transfers between devices, from_neighbours(): lax.ppermute(first, ('rad', 'azi'), back)  3.55 us
    ppermute x1, starting transfers between devices, from_neighbours(): lax.ppermute(last, ('rad', 'azi'), forth)  1.89 us
  transfers between devices with their start and end apart: 2, of which 0 were waited for; matrix products, arithmetic and copies ran while one was open for 0% of the time, Pallas kernels for 6%

profile of v14, /device:TPU:1, one launch (start us, length us, event | category | flops | bytes accessed | tf_op | source)
XLA Modules:
  0.0 78.1 jit_solution(9307392211473637461)
XLA Ops:
  0.0 0.0 copy-start
  0.0 0.0 copy-start.1
  0.0 0.0 copy-start.2
  0.0 33.7 %all_to_all.10.main = f32[16,64,512]{2,1,0:T(8,128)S(1)} all-to-all(f32[16,64,512]{2,1,0:T(8,128)} %bitcast.3), channel_id=1, replica_groups={{0,1,2,3,4,5,6,7,8,9,10,11,12,13,14,15},{24,25,26,27,28,29,30,31,16,17,..., dimensions={0} | all-to-all | bytes 4194304 | tf_op jit(solution)/shard_map/all_to_all | solution.py:270
  33.7 0.0 copy-done
  33.7 0.0 copy-done.1
  33.7 0.0 copy-done.2
  33.7 0.6 shard_map.46
  34.4 1.9 %collective-permute-start = (f32[264,128]{1,0:T(8,128)S(1)}, f32[264,128]{1,0:T(8,128)S(1)}, u32[]{:S(2)}, u32[]{:S(2)}) collective-permute-start(f32[264,128]{1,0:T(8,128)S(1)} %get-tuple-element.10), channel_id=1, source_target_pairs={{0,24},{1,25},{2,26},{3,27},{4,28},{5,29},{6,30},{7,31},{8,16},{9,... | collective-permute-start | bytes 405512 | tf_op jit(solution)/shard_map/ppermute | solution.py:276
  36.3 3.6 %collective-permute-start.1 = (f32[264,128]{1,0:T(8,128)S(1)}, f32[264,128]{1,0:T(8,128)S(1)}, u32[]{:S(2)}, u32[]{:S(2)}) collective-permute-start(f32[264,128]{1,0:T(8,128)S(1)} %get-tuple-element.11), channel_id=1, source_target_pairs={{24,0},{25,1},{26,2},{27,3},{28,4},{29,5},{30,6},{31,7},{16,8},{17... | collective-permute-start | bytes 405512 | tf_op jit(solution)/shard_map/ppermute | solution.py:276
  39.8 5.0 %shard_map.47 = (f32[16,64,512]{2,1,0:T(8,128)S(1)}, f32[2,4,4,16,128]{4,3,2,1,0:T(8,128)S(1)}, f32[2,4,4,32,128]{4,3,2,1,0:T(8,128)S(1)}) custom-call(s32[2,64]{1,0:T(2,128)S(1)} %copy-done, f32[2,64]{1,0:T(2,128)S(1)} %copy-done.1, f32[64]{0:T(128)S(1)} %copy-done.2, f32[16,64,512]{2,1,0:T(8,128)S(1)} %all_to_all.10.main), custom_call_target="tpu_custom_call" | custom-call | tf_op jit(solution)/shard_map/pallas_call | solution.py:228
  44.8 0.0 collective-permute-done.before
  44.8 0.0 collective-permute-done.1.after
  44.8 1.2 %shard_map.48 = f32[16,64,512]{2,1,0:T(8,128)S(1)} custom-call(s32[2,64]{1,0:T(2,128)S(1)} %copy-done, f32[2,64]{1,0:T(2,128)S(1)} %copy-done.1, f32[64]{0:T(128)S(1)} %copy-done.2, f32[264,128]{1,0:T(8,128)S(1)} %collective-permute-done.before, f32[264,128]{1,0:T(8,128)S(1)} %collective-permute-done.1.after, ...), custom_call_target="tpu_custom_call", output_to_operand_aliasing={{}: (7, {})} | custom-call | tf_op jit(solution)/shard_map/pallas_call | solution.py:250
  46.1 30.7 %all_to_all.11 = f32[16,64,512]{2,1,0:T(8,128)S(1)} all-to-all(f32[16,64,512]{2,1,0:T(8,128)S(1)} %shard_map.48), channel_id=1, replica_groups={{0,1,2,3,4,5,6,7,8,9,10,11,12,13,14,15},{24,25,26,27,28,29,30,31,16,17,..., dimensions={0} | all-to-all | bytes 4194304 | tf_op jit(solution)/shard_map/all_to_all | solution.py:270
  76.8 1.3 %copy.8 = f32[8,2,64,512]{3,2,1,0:T(8,128)} copy(f32[8,2,64,512]{3,2,1,0:T(8,128)S(1)} %bitcast.2) | data formatting | bytes 4194304
Async XLA Ops:
  0.0 33.7 %copy-start = (s32[2,64]{1,0:T(2,128)S(1)}, s32[2,64]{1,0:T(2,128)}, u32[]{:S(2)}) copy-start(s32[2,64]{1,0:T(2,128)} %offsets.5) | copy-start | bytes 1540
  0.0 33.7 %copy-start.1 = (f32[2,64]{1,0:T(2,128)S(1)}, f32[2,64]{1,0:T(2,128)}, u32[]{:S(2)}) copy-start(f32[2,64]{1,0:T(2,128)} %fractions.5) | copy-start | bytes 1540
  0.0 33.7 %copy-start.2 = (f32[64]{0:T(128)S(1)}, f32[64]{0:T(128)}, u32[]{:S(2)}) copy-start(f32[64]{0:T(128)} %coefs.5) | copy-start | bytes 772
  34.4 10.5 %collective-permute-start = (f32[264,128]{1,0:T(8,128)S(1)}, f32[264,128]{1,0:T(8,128)S(1)}, u32[]{:S(2)}, u32[]{:S(2)}) collective-permute-start(f32[264,128]{1,0:T(8,128)S(1)} %get-tuple-element.10), channel_id=1, source_target_pairs={{0,24},{1,25},{2,26},{3,27},{4,28},{5,29},{6,30},{7,31},{8,16},{9,... | collective-permute-start | bytes 405512 | tf_op jit(solution)/shard_map/ppermute | solution.py:276
  36.3 8.6 %collective-permute-start.1 = (f32[264,128]{1,0:T(8,128)S(1)}, f32[264,128]{1,0:T(8,128)S(1)}, u32[]{:S(2)}, u32[]{:S(2)}) collective-permute-start(f32[264,128]{1,0:T(8,128)S(1)} %get-tuple-element.11), channel_id=1, source_target_pairs={{24,0},{25,1},{26,2},{27,3},{28,4},{29,5},{30,6},{31,7},{16,8},{17... | collective-permute-start | bytes 405512 | tf_op jit(solution)/shard_map/ppermute | solution.py:276

commit v15 on v14

--- a/solution.py
+++ b/solution.py
@@ -98,9 +98,8 @@
 
 def edge_radii_kernel(offsets, fractions, coefs, main, first, last):
     members, rows, width = main.shape
-    steps, per, half = offsets.shape[0], width // LANES, members // 2
+    per, half = width // LANES, members // 2
     part, parts = lax.axis_index("rad"), lax.axis_size("rad")
-    lane = lax.broadcasted_iota(jnp.int32, (1, LANES), 1)
     for out, start, sent in ((first, 0, part > 0), (last, rows - HALO, part < parts - 1)):
         for r in range(HALO):
             radius = main[:, start + r, :]
@@ -108,17 +107,12 @@
             radius = jnp.where(sent, radius, jnp.zeros_like(radius))
             for c in range(per):
                 out[pl.ds((r * per + c) * members, members)] = radius[:, c * LANES : (c + 1) * LANES]
-        table = HALO * per * members
-        out[pl.ds(table, TILE)] = jnp.zeros((TILE, LANES), jnp.float32)
-        for r in range(HALO):
-            at = start + r
-            entries = [offsets[step, at].astype(jnp.float32) for step in range(steps)]
-            entries += [fractions[step, at] for step in range(steps)]
-            entries.append(coefs[at])
-            line = jnp.zeros((1, LANES), jnp.float32)
-            for column, entry in enumerate(entries):
-                line = jnp.where(lane == column, jnp.where(sent, entry, 0.0), line)
-            out[pl.ds(table + r, 1)] = line
+        at = HALO * per * members
+        out[pl.ds(at, TILE)] = jnp.zeros((TILE, LANES), jnp.float32)
+        for entries in (offsets[...].astype(jnp.float32), fractions[...], coefs[...]):
+            count = entries.shape[0]
+            out[pl.ds(at, count), pl.ds(0, rows)] = jnp.where(sent, entries, jnp.zeros_like(entries))
+            at += count
 
 
 def inner_kernel(offsets, fractions, coefs, main, out, near, stepped, grid, once, twice):
@@ -168,7 +162,7 @@
             if 0 <= row < 2 * HALO:
                 return mine(row + side * (rows - 2 * HALO))
             if (column, at) not in taken:
-                taken[column, at] = tables[side][at - 2 * HALO * side, column]
+                taken[column, at] = tables[side][column, at + (rows - HALO if side == 0 else -2 * HALO)]
             return taken[column, at]
 
         def line(at, c):
@@ -216,10 +210,10 @@
     return pl.pallas_call(
         edge_radii_kernel,
         out_shape=[side, side],
-        in_specs=[SMEM] * 3 + [VMEM],
+        in_specs=[VMEM] * 4,
         out_specs=[VMEM, VMEM],
         compiler_params=grant(2),
-    )(offsets, fractions, coefs, main)
+    )(offsets, fractions, coefs[None], main)
 
 
 def inner(offsets, fractions, coefs, main):

time: 78.3 us -> 77.7 us (level)
  no operation moved by 1% of the time
where the time goes in v15:
time: 77.7 us; the launch traced here: 77.5 us
  blocking collectives  64.4 us (83%)
  Pallas kernels  6.29 us (8%)
  starting transfers between devices  5.44 us (7%)
  local copies, waits for them, and re-layouts  1.33 us (2%)
    all_to_all x2, blocking collectives, exchanged(): lax.all_to_all(blocks, ('rad', 'azi'), 0, 0, axis_index_groups=devices, t...  64.4 us
    pallas_call x1, Pallas kernels, inner(): pl.pallas_call(inner_kernel, out_shape=[pltpu.VMEM(main.shape, jnp.float3...  5 us
    ppermute x1, starting transfers between devices, from_neighbours(): lax.ppermute(first, ('rad', 'azi'), back)  3.55 us
    ppermute x1, starting transfers between devices, from_neighbours(): lax.ppermute(last, ('rad', 'azi'), forth)  1.89 us
  transfers between devices with their start and end apart: 2, of which 0 were waited for; matrix products, arithmetic and copies ran while one was open for 0% of the time, Pallas kernels for 6%

profile of v15, /device:TPU:1, one launch (start us, length us, event | category | flops | bytes accessed | tf_op | source)
XLA Modules:
  0.0 77.5 jit_solution(785477767048564283)
XLA Ops:
  0.0 0.0 copy-start
  0.0 0.0 copy-start.1
  0.0 0.0 copy-start.2
  0.0 33.7 %all_to_all.10.main = f32[16,64,512]{2,1,0:T(8,128)S(1)} all-to-all(f32[16,64,512]{2,1,0:T(8,128)} %bitcast.5), channel_id=1, replica_groups={{0,1,2,3,4,5,6,7,8,9,10,11,12,13,14,15},{24,25,26,27,28,29,30,31,16,17,..., dimensions={0} | all-to-all | bytes 4194304 | tf_op jit(solution)/shard_map/all_to_all | solution.py:264
  33.7 0.0 copy-done
  33.7 0.0 copy-done.1
  33.7 0.0 copy-done.2
  33.7 0.1 shard_map.46
  33.8 1.9 %collective-permute-start = (f32[264,128]{1,0:T(8,128)S(1)}, f32[264,128]{1,0:T(8,128)S(1)}, u32[]{:S(2)}, u32[]{:S(2)}) collective-permute-start(f32[264,128]{1,0:T(8,128)S(1)} %get-tuple-element.10), channel_id=1, source_target_pairs={{0,24},{1,25},{2,26},{3,27},{4,28},{5,29},{6,30},{7,31},{8,16},{9,... | collective-permute-start | bytes 405512 | tf_op jit(solution)/shard_map/ppermute | solution.py:270
  35.7 3.6 %collective-permute-start.1 = (f32[264,128]{1,0:T(8,128)S(1)}, f32[264,128]{1,0:T(8,128)S(1)}, u32[]{:S(2)}, u32[]{:S(2)}) collective-permute-start(f32[264,128]{1,0:T(8,128)S(1)} %get-tuple-element.11), channel_id=1, source_target_pairs={{24,0},{25,1},{26,2},{27,3},{28,4},{29,5},{30,6},{31,7},{16,8},{17... | collective-permute-start | bytes 405512 | tf_op jit(solution)/shard_map/ppermute | solution.py:270
  39.2 5.0 %shard_map.47 = (f32[16,64,512]{2,1,0:T(8,128)S(1)}, f32[2,4,4,16,128]{4,3,2,1,0:T(8,128)S(1)}, f32[2,4,4,32,128]{4,3,2,1,0:T(8,128)S(1)}) custom-call(s32[2,64]{1,0:T(2,128)S(1)} %copy-done, f32[2,64]{1,0:T(2,128)S(1)} %copy-done.1, f32[64]{0:T(128)S(1)} %copy-done.2, f32[16,64,512]{2,1,0:T(8,128)S(1)} %all_to_all.10.main), custom_call_target="tpu_custom_call" | custom-call | tf_op jit(solution)/shard_map/pallas_call | solution.py:222
  44.2 0.0 collective-permute-done.before
  44.3 0.0 collective-permute-done.1.after
  44.3 1.2 %shard_map.48 = f32[16,64,512]{2,1,0:T(8,128)S(1)} custom-call(s32[2,64]{1,0:T(2,128)S(1)} %copy-done, f32[2,64]{1,0:T(2,128)S(1)} %copy-done.1, f32[64]{0:T(128)S(1)} %copy-done.2, f32[264,128]{1,0:T(8,128)S(1)} %collective-permute-done.before, f32[264,128]{1,0:T(8,128)S(1)} %collective-permute-done.1.after, ...), custom_call_target="tpu_custom_call", output_to_operand_aliasing={{}: (7, {})} | custom-call | tf_op jit(solution)/shard_map/pallas_call | solution.py:244
  45.5 30.7 %all_to_all.11 = f32[16,64,512]{2,1,0:T(8,128)S(1)} all-to-all(f32[16,64,512]{2,1,0:T(8,128)S(1)} %shard_map.48), channel_id=1, replica_groups={{0,1,2,3,4,5,6,7,8,9,10,11,12,13,14,15},{24,25,26,27,28,29,30,31,16,17,..., dimensions={0} | all-to-all | bytes 4194304 | tf_op jit(solution)/shard_map/all_to_all | solution.py:264
  76.2 1.3 %copy.8 = f32[8,2,64,512]{3,2,1,0:T(8,128)} copy(f32[8,2,64,512]{3,2,1,0:T(8,128)S(1)} %bitcast.4) | data formatting | bytes 4194304
Async XLA Ops:
  0.0 33.7 %copy-start = (s32[2,64]{1,0:T(2,128)S(1)}, s32[2,64]{1,0:T(2,128)}, u32[]{:S(2)}) copy-start(s32[2,64]{1,0:T(2,128)} %offsets.5) | copy-start | bytes 1540
  0.0 33.7 %copy-start.1 = (f32[2,64]{1,0:T(2,128)S(1)}, f32[2,64]{1,0:T(2,128)}, u32[]{:S(2)}) copy-start(f32[2,64]{1,0:T(2,128)} %fractions.5) | copy-start | bytes 1540
  0.0 33.7 %copy-start.2 = (f32[64]{0:T(128)S(1)}, f32[64]{0:T(128)}, u32[]{:S(2)}) copy-start(f32[64]{0:T(128)} %coefs.3) | copy-start | bytes 772
  33.8 10.5 %collective-permute-start = (f32[264,128]{1,0:T(8,128)S(1)}, f32[264,128]{1,0:T(8,128)S(1)}, u32[]{:S(2)}, u32[]{:S(2)}) collective-permute-start(f32[264,128]{1,0:T(8,128)S(1)} %get-tuple-element.10), channel_id=1, source_target_pairs={{0,24},{1,25},{2,26},{3,27},{4,28},{5,29},{6,30},{7,31},{8,16},{9,... | collective-permute-start | bytes 405512 | tf_op jit(solution)/shard_map/ppermute | solution.py:270
  35.7 8.6 %collective-permute-start.1 = (f32[264,128]{1,0:T(8,128)S(1)}, f32[264,128]{1,0:T(8,128)S(1)}, u32[]{:S(2)}, u32[]{:S(2)}) collective-permute-start(f32[264,128]{1,0:T(8,128)S(1)} %get-tuple-element.11), channel_id=1, source_target_pairs={{24,0},{25,1},{26,2},{27,3},{28,4},{29,5},{30,6},{31,7},{16,8},{17... | collective-permute-start | bytes 405512 | tf_op jit(solution)/shard_map/ppermute | solution.py:270

commit v16 on v15

--- a/solution.py
+++ b/solution.py
@@ -149,6 +149,7 @@
     members, rows, width = out.shape
     steps, per = offsets.shape[0], width // LANES
     halos = (before, after)
+    offsets, fractions, coefs = offsets[...], fractions[...], coefs[...]
     tables = [halo[pl.ds(HALO * per * members, TILE)] for halo in halos]
 
     def side_steps(side):
@@ -159,9 +160,11 @@
 
         def entry(mine, column, at):
             row = own(at)
+            if (column, at) in taken:
+                return taken[column, at]
             if 0 <= row < 2 * HALO:
-                return mine(row + side * (rows - 2 * HALO))
-            if (column, at) not in taken:
+                taken[column, at] = mine(row + side * (rows - 2 * HALO))
+            else:
                 taken[column, at] = tables[side][column, at + (rows - HALO if side == 0 else -2 * HALO)]
             return taken[column, at]
 
@@ -182,7 +185,7 @@
             return entry(lambda row: fractions[step, row], steps + step, at)
 
         def factor(at):
-            return entry(lambda row: coefs[row], 2 * steps, at) * PER_DIFFERENCE
+            return entry(lambda row: coefs[0, row], 2 * steps, at) * PER_DIFFERENCE
 
         return offset, *two_steps(offset, fraction, factor, line, once.at[side], twice.at[side], kept)
 
@@ -244,7 +247,7 @@
     return pl.pallas_call(
         edge_kernel,
         out_shape=pltpu.VMEM(done.shape, jnp.float32),
-        in_specs=[SMEM] * 3 + [VMEM] * 5,
+        in_specs=[VMEM] * 8,
         out_specs=VMEM,
         scratch_shapes=[
             pltpu.VMEM((2, HALO + 2 * REACH, per, 2 * members, LANES), jnp.float32),
@@ -252,7 +255,7 @@
         ],
         input_output_aliases={7: 0},
         compiler_params=grant(6),
-    )(offsets, fractions, coefs, before, after, near, stepped, done)
+    )(offsets, fractions, coefs[None], before, after, near, stepped, done)
 
 
 def owners(parts, members):

time: 77.7 us -> 77.4 us (level)
  no operation moved by 1% of the time
where the time goes in v16:
time: 77.4 us; the launch traced here: 77.2 us
  blocking collectives  64.4 us (83%)
  Pallas kernels  5.99 us (8%)
  starting transfers between devices  5.44 us (7%)
  local copies, waits for them, and re-layouts  1.33 us (2%)
    all_to_all x2, blocking collectives, exchanged(): lax.all_to_all(blocks, ('rad', 'azi'), 0, 0, axis_index_groups=devices, t...  64.4 us
    pallas_call x1, Pallas kernels, inner(): pl.pallas_call(inner_kernel, out_shape=[pltpu.VMEM(main.shape, jnp.float3...  5 us
    ppermute x1, starting transfers between devices, from_neighbours(): lax.ppermute(first, ('rad', 'azi'), back)  3.55 us
    ppermute x1, starting transfers between devices, from_neighbours(): lax.ppermute(last, ('rad', 'azi'), forth)  1.89 us
  transfers between devices with their start and end apart: 2, of which 0 were waited for; matrix products, arithmetic and copies ran while one was open for 0% of the time, Pallas kernels for 6%

profile of v16, /device:TPU:1, one launch (start us, length us, event | category | flops | bytes accessed | tf_op | source)
XLA Modules:
  0.0 77.2 jit_solution(9175811577126469045)
XLA Ops:
  0.0 0.0 copy-start
  0.0 0.0 copy-start.1
  0.0 0.0 copy-start.2
  0.0 33.7 %all_to_all.10.main = f32[16,64,512]{2,1,0:T(8,128)S(1)} all-to-all(f32[16,64,512]{2,1,0:T(8,128)} %bitcast.6), channel_id=1, replica_groups={{0,1,2,3,4,5,6,7,8,9,10,11,12,13,14,15},{24,25,26,27,28,29,30,31,16,17,..., dimensions={0} | all-to-all | bytes 4194304 | tf_op jit(solution)/shard_map/all_to_all | solution.py:267
  33.7 0.0 copy-done
  33.7 0.0 copy-done.1
  33.7 0.0 copy-done.2
  33.7 0.1 shard_map.46
  33.8 1.9 %collective-permute-start = (f32[264,128]{1,0:T(8,128)S(1)}, f32[264,128]{1,0:T(8,128)S(1)}, u32[]{:S(2)}, u32[]{:S(2)}) collective-permute-start(f32[264,128]{1,0:T(8,128)S(1)} %get-tuple-element.10), channel_id=1, source_target_pairs={{0,24},{1,25},{2,26},{3,27},{4,28},{5,29},{6,30},{7,31},{8,16},{9,... | collective-permute-start | bytes 405512 | tf_op jit(solution)/shard_map/ppermute | solution.py:273
  35.7 3.6 %collective-permute-start.1 = (f32[264,128]{1,0:T(8,128)S(1)}, f32[264,128]{1,0:T(8,128)S(1)}, u32[]{:S(2)}, u32[]{:S(2)}) collective-permute-start(f32[264,128]{1,0:T(8,128)S(1)} %get-tuple-element.11), channel_id=1, source_target_pairs={{24,0},{25,1},{26,2},{27,3},{28,4},{29,5},{30,6},{31,7},{16,8},{17... | collective-permute-start | bytes 405512 | tf_op jit(solution)/shard_map/ppermute | solution.py:273
  39.2 5.0 %shard_map.47 = (f32[16,64,512]{2,1,0:T(8,128)S(1)}, f32[2,4,4,16,128]{4,3,2,1,0:T(8,128)S(1)}, f32[2,4,4,32,128]{4,3,2,1,0:T(8,128)S(1)}) custom-call(s32[2,64]{1,0:T(2,128)S(1)} %copy-done, f32[2,64]{1,0:T(2,128)S(1)} %copy-done.1, f32[64]{0:T(128)S(1)} %copy-done.2, f32[16,64,512]{2,1,0:T(8,128)S(1)} %all_to_all.10.main), custom_call_target="tpu_custom_call" | custom-call | tf_op jit(solution)/shard_map/pallas_call | solution.py:225
  44.2 0.0 collective-permute-done.before
  44.3 0.0 collective-permute-done.1.after
  44.3 0.9 %shard_map.48 = f32[16,64,512]{2,1,0:T(8,128)S(1)} custom-call(s32[2,64]{1,0:T(2,128)S(1)} %copy-done, f32[2,64]{1,0:T(2,128)S(1)} %copy-done.1, f32[1,64]{1,0:T(1,128)S(1)} %bitcast.4, f32[264,128]{1,0:T(8,128)S(1)} %collective-permute-done.before, f32[264,128]{1,0:T(8,128)S(1)} %collective-permute-done.1.after, ...), custom_call_target="tpu_custom_call", output_to_operand_aliasing={{}: (7, {})} | custom-call | tf_op jit(solution)/shard_map/pallas_call | solution.py:247
  45.2 30.7 %all_to_all.11 = f32[16,64,512]{2,1,0:T(8,128)S(1)} all-to-all(f32[16,64,512]{2,1,0:T(8,128)S(1)} %shard_map.48), channel_id=1, replica_groups={{0,1,2,3,4,5,6,7,8,9,10,11,12,13,14,15},{24,25,26,27,28,29,30,31,16,17,..., dimensions={0} | all-to-all | bytes 4194304 | tf_op jit(solution)/shard_map/all_to_all | solution.py:267
  75.9 1.3 %copy.8 = f32[8,2,64,512]{3,2,1,0:T(8,128)} copy(f32[8,2,64,512]{3,2,1,0:T(8,128)S(1)} %bitcast.5) | data formatting | bytes 4194304
Async XLA Ops:
  0.0 33.7 %copy-start = (s32[2,64]{1,0:T(2,128)S(1)}, s32[2,64]{1,0:T(2,128)}, u32[]{:S(2)}) copy-start(s32[2,64]{1,0:T(2,128)} %offsets.5) | copy-start | bytes 1540
  0.0 33.7 %copy-start.1 = (f32[2,64]{1,0:T(2,128)S(1)}, f32[2,64]{1,0:T(2,128)}, u32[]{:S(2)}) copy-start(f32[2,64]{1,0:T(2,128)} %fractions.5) | copy-start | bytes 1540
  0.0 33.7 %copy-start.2 = (f32[64]{0:T(128)S(1)}, f32[64]{0:T(128)}, u32[]{:S(2)}) copy-start(f32[64]{0:T(128)} %coefs.1) | copy-start | bytes 772
  33.8 10.4 %collective-permute-start = (f32[264,128]{1,0:T(8,128)S(1)}, f32[264,128]{1,0:T(8,128)S(1)}, u32[]{:S(2)}, u32[]{:S(2)}) collective-permute-start(f32[264,128]{1,0:T(8,128)S(1)} %get-tuple-element.10), channel_id=1, source_target_pairs={{0,24},{1,25},{2,26},{3,27},{4,28},{5,29},{6,30},{7,31},{8,16},{9,... | collective-permute-start | bytes 405512 | tf_op jit(solution)/shard_map/ppermute | solution.py:273
  35.7 8.6 %collective-permute-start.1 = (f32[264,128]{1,0:T(8,128)S(1)}, f32[264,128]{1,0:T(8,128)S(1)}, u32[]{:S(2)}, u32[]{:S(2)}) collective-permute-start(f32[264,128]{1,0:T(8,128)S(1)} %get-tuple-element.11), channel_id=1, source_target_pairs={{24,0},{25,1},{26,2},{27,3},{28,4},{29,5},{30,6},{31,7},{16,8},{17... | collective-permute-start | bytes 405512 | tf_op jit(solution)/shard_map/ppermute | solution.py:273
